TPU v7x, 32 devices: a whole 2x2x4 slice. The times are simulated.
32 devices in a mesh: gx: 8 (over y, x, core), gy: 4 (over z).
Axes of the slice: x: 2, y: 2, z: 4, core: 2. Of those that a mesh axis runs over, the one named last changes fastest.
Arguments:
- block_input: bfloat16 [25088, 512], P(('gx', 'gy')), may hold values from -6 to 6
- cotangent: bfloat16 [25088, 512], P(('gx', 'gy')), may hold values from -6 to 6
- live_images: int32 [8], P('gx'), may hold values from 1 to 16, 96 in all
- ln1_gain: bfloat16 [512], replicated, may hold values from 0.25 to 1.75
- ln1_bias: bfloat16 [512], replicated, may hold values from -3 to 3
- qkv_weight: bfloat16 [512, 3, 512], P('gx', None, 'gy'), may hold values from -0.25 to 0.25
- qv_bias: bfloat16 [2, 512], P(None, 'gy'), may hold values from -3 to 3
- rel_table: bfloat16 [169, 16], P(None, 'gy'), may hold values from -4 to 254
- proj_weight: bfloat16 [512, 512], P('gy', 'gx'), may hold values from -0.75 to 0.75
- proj_bias: bfloat16 [512], replicated, may hold values from -3 to 3
- ln2_gain: bfloat16 [512], replicated, may hold values from 0.25 to 1.75
- ln2_bias: bfloat16 [512], replicated, may hold values from -3 to 3
- fc1_weight: bfloat16 [512, 2048], P('gx', 'gy'), may hold values from -0.25 to 0.25
- fc1_bias: bfloat16 [2048], P('gy'), may hold values from -3 to 3
- fc2_weight: bfloat16 [2048, 512], P('gy', 'gx'), may hold values from -0.1875 to 0.1875
- fc2_bias: bfloat16 [512], replicated, may hold values from -3 to 3
Outputs:
- output: bfloat16 [25088, 512], P(('gx', 'gy'))
- d_input: bfloat16 [25088, 512], P(('gx', 'gy'))
- d_ln1_gain: float32 [512], replicated
- d_ln1_bias: float32 [512], replicated
- d_qkv_weight: float32 [512, 3, 512], P('gx', None, 'gy')
- d_qv_bias: float32 [2, 512], P(None, 'gy')
- d_rel_table: float32 [169, 16], P(None, 'gy')
- d_proj_weight: float32 [512, 512], P('gy', 'gx')
- d_proj_bias: float32 [512], replicated
- d_ln2_gain: float32 [512], replicated
- d_ln2_bias: float32 [512], replicated
- d_fc1_weight: float32 [512, 2048], P('gx', 'gy')
- d_fc1_bias: float32 [2048], P('gy')
- d_fc2_weight: float32 [2048, 512], P('gy', 'gx')
- d_fc2_bias: float32 [512], replicated
Inputs may be any that keep to these rules, and one draw needn't show every extreme that they name: Image slot s of index i of gx (slots 0 to 15 in order) holds an image exactly when s < live_images[i]; the counts add up to 96.
All inputs are finite; a program needn't handle non-finite values. No bound on the sum of `live_images` on one device may be relied on, other than what follows from the above.
Results may differ from a plain program's by a relative error of at most 0.014.
Values may be sent and summed in bfloat16 or wider, within the bound.
A program may use at most 192 MiB of HBM per device.

v0:
```python
import functools
import jax
import jax.numpy as jnp
from jax import lax
import numpy as np
from jax.experimental import pallas as pl
from jax.experimental.pallas import tpu as pltpu
from jax.sharding import PartitionSpec as P

HD = 32
GRID = 14
WIN = 7
SHIFT = 3
RELS = 169


eps_norm = 1e-05
mask_value = -100.0
inv_root_two = 0.7071067811865476
inv_root_two_pi = 0.3989422804014327


def matmul(left, right):
    return jnp.dot(left, right, preferred_element_type=jnp.float32)


def matmul_tn(left, right):
    return lax.dot_general(
        left, right, (((0,), (0,)), ((), ())), preferred_element_type=jnp.float32
    )


def matmul_nt(left, right):
    return lax.dot_general(
        left, right, (((1,), (1,)), ((), ())), preferred_element_type=jnp.float32
    )


SLOT = 64
PACK = 8
WIN_COUNT = (GRID // WIN) ** 2
IMAGE = GRID * GRID
ALIGN = 16
STEP = IMAGE // ALIGN * ALIGN
SPAN = STEP + ALIGN
far_below = -1e30


def static_tables(image_count):
    rows = np.arange(WIN_COUNT * SLOT)
    win, place = rows // SLOT, rows % SLOT
    row = (win // (GRID // WIN) * WIN + place // WIN + SHIFT) % GRID
    col = (win % (GRID // WIN) * WIN + place % WIN + SHIFT) % GRID
    token = np.where(place < WIN * WIN, row * GRID + col, -1)
    offset = np.arange(image_count) * (IMAGE - STEP)
    column = np.where(token[None] >= 0, token[None] + offset[:, None], -1)
    places = np.arange(SLOT)
    live = places < WIN * WIN
    pr, pc = places // WIN, places % WIN
    rel = (pr[None, :] - pr[:, None] + WIN - 1) * (2 * WIN - 1) + pc[None, :] - pc[:, None] + WIN - 1
    rel = np.where(live[:, None] & live[None, :], rel, -1)
    cells = np.arange(GRID)
    region = np.where(cells < GRID - WIN, 0, np.where(cells < GRID - SHIFT, 1, 2))
    shifted_row = (win // (GRID // WIN) * WIN + np.minimum(place // WIN, WIN - 1)).reshape(WIN_COUNT, SLOT)
    shifted_col = (win % (GRID // WIN) * WIN + place % WIN).reshape(WIN_COUNT, SLOT)
    ids = region[shifted_row] * 3 + region[shifted_col]
    mask = np.where(ids[:, :, None] == ids[:, None, :], 0.0, mask_value)
    mask = np.where(live[None, None, :] & live[None, :, None], mask, 0.0)
    mask = np.where(live[None, :, None], mask, far_below)
    return column.astype(np.int32), rel.astype(np.int32), mask.astype(np.float32)


def attention_tables(rel_table, image_count):
    column, rel, mask = static_tables(image_count)
    spots = np.arange(SPAN, dtype=np.int32)
    perm = jnp.asarray((column[:, :, None] == spots).astype(np.float32)).astype(jnp.bfloat16)
    perm_t = jnp.asarray((column[:, None, :] == spots[:, None]).astype(np.float32)).astype(jnp.bfloat16)
    heads = rel_table.shape[0]
    onehot = (jnp.arange(RELS, dtype=jnp.int32)[:, None] == jnp.asarray(rel.reshape(1, -1))).astype(
        jnp.bfloat16
    )
    bias = lax.dot_general(
        rel_table, onehot, (((1,), (0,)), ((), ())), preferred_element_type=jnp.float32
    )
    bias = bias.reshape(heads // PACK, PACK, SLOT, SLOT).transpose(0, 2, 1, 3)
    bias = bias[None] + jnp.asarray(mask)[:, None, :, None, :]
    bias = bias.reshape(WIN_COUNT, heads // PACK, SLOT, PACK * SLOT)
    owner = np.arange(PACK * SLOT)[:, None] // SLOT == np.arange(PACK * HD)[None, :] // HD
    owner = jnp.asarray(owner.astype(np.float32)).astype(jnp.bfloat16)
    return perm, perm_t, bias, owner, onehot


def spread(rows, owner):
    return jnp.concatenate([rows] * PACK, axis=0) * owner


def gather_heads(full):
    lanes = lax.broadcasted_iota(jnp.int32, (SLOT, PACK * HD), 1) // HD
    total = full[:SLOT]
    for h in range(1, PACK):
        total = jnp.where(lanes == h, full[h * SLOT : (h + 1) * SLOT], total)
    return total


def forward_kernel(qkv_ref, perm_ref, perm_t_ref, bias_ref, owner_ref, context_ref, windows_ref, probs_ref, ctx_ref):
    image = pl.program_id(0)
    width = context_ref.shape[1]
    groups = width // (PACK * HD)
    start = pl.multiple_of(image * STEP, ALIGN)
    windows_ref[0] = matmul(perm_ref[0], qkv_ref[pl.ds(start, SPAN), :]).astype(jnp.bfloat16)
    for w in range(WIN_COUNT):
        rows = slice(w * SLOT, (w + 1) * SLOT)
        for g in range(groups):
            low = g * PACK * HD
            query = windows_ref[0, rows, low : low + PACK * HD]
            keys = windows_ref[0, rows, width + low : width + low + PACK * HD]
            values = windows_ref[0, rows, 2 * width + low : 2 * width + low + PACK * HD]
            scores = matmul_nt(keys, spread(query, owner_ref[...])) * HD ** (-0.5) + bias_ref[w, g]
            raised = jnp.exp(scores - jnp.max(scores, 0, keepdims=True))
            probs = raised * (1.0 / jnp.sum(raised, 0, keepdims=True))
            probs_ref[0, w * groups + g] = probs
            full = matmul_tn(probs.astype(jnp.bfloat16), values)
            ctx_ref[rows, low : low + PACK * HD] = gather_heads(full).astype(jnp.bfloat16)

    @pl.when(image == 0)
    def _():
        context_ref[...] = jnp.zeros_like(context_ref)

    context_ref[pl.ds(start, SPAN), :] += matmul(perm_t_ref[0], ctx_ref[...]).astype(jnp.bfloat16)


def backward_kernel(
    d_context_ref, windows_ref, probs_ref, perm_ref, perm_t_ref, owner_ref,
    d_mixed_ref, d_bias_ref, d_qv_ref, d_ctx_ref, d_win_ref,
):
    image = pl.program_id(0)
    width = d_context_ref.shape[1]
    groups = width // (PACK * HD)
    start = pl.multiple_of(image * STEP, ALIGN)

    @pl.when(image == 0)
    def _():
        d_mixed_ref[...] = jnp.zeros_like(d_mixed_ref)
        d_bias_ref[...] = jnp.zeros_like(d_bias_ref)
        d_qv_ref[...] = jnp.zeros_like(d_qv_ref)

    d_ctx_ref[...] = matmul(perm_ref[0], d_context_ref[pl.ds(start, SPAN), :]).astype(jnp.bfloat16)
    for g in range(groups):
        low = g * PACK * HD
        cols = slice(low, low + PACK * HD)
        d_bias = jnp.zeros((SLOT, PACK * SLOT), jnp.float32)
        d_query_sum = jnp.zeros((1, PACK * HD), jnp.float32)
        d_value_sum = jnp.zeros((1, PACK * HD), jnp.float32)
        for w in range(WIN_COUNT):
            rows = slice(w * SLOT, (w + 1) * SLOT)
            query = windows_ref[0, rows, low : low + PACK * HD]
            keys = windows_ref[0, rows, width + low : width + low + PACK * HD]
            values = windows_ref[0, rows, 2 * width + low : 2 * width + low + PACK * HD]
            probs = probs_ref[0, w * groups + g]
            d_wide = spread(d_ctx_ref[rows, cols], owner_ref[...])
            d_probs = matmul_nt(values, d_wide)
            d_values = matmul(probs.astype(jnp.bfloat16), d_wide)
            d_scores = probs * (d_probs - jnp.sum(probs * d_probs, 0, keepdims=True))
            d_bias = d_bias + d_scores
            d_low = d_scores.astype(jnp.bfloat16)
            d_keys = matmul(d_low, spread(query, owner_ref[...])) * HD ** (-0.5)
            d_query = gather_heads(matmul_tn(d_low, keys)) * HD ** (-0.5)
            d_win_ref[rows, low : low + PACK * HD] = d_query.astype(jnp.bfloat16)
            d_win_ref[rows, width + low : width + low + PACK * HD] = d_keys.astype(jnp.bfloat16)
            d_win_ref[rows, 2 * width + low : 2 * width + low + PACK * HD] = d_values.astype(jnp.bfloat16)
            d_query_sum = d_query_sum + jnp.sum(d_query, 0, keepdims=True)
            d_value_sum = d_value_sum + jnp.sum(d_values, 0, keepdims=True)
        d_bias_ref[g] += d_bias
        d_qv_ref[0:1, cols] += d_query_sum
        d_qv_ref[1:2, cols] += d_value_sum
    d_mixed_ref[pl.ds(start, SPAN), :] += matmul(perm_t_ref[0], d_win_ref[...]).astype(jnp.bfloat16)


def whole(shape):
    return pl.BlockSpec(shape, lambda n: (0,) * len(shape))


def per_image(shape):
    return pl.BlockSpec((1,) + shape, lambda n: (n,) + (0,) * len(shape))


def attend_forward(qkv, tables):
    perm, perm_t, bias, owner, _ = tables
    tok, wide = qkv.shape
    width = wide // 3
    count, spots = perm.shape[:2]
    tiles = WIN_COUNT * width // (PACK * HD)
    return pl.pallas_call(
        forward_kernel,
        grid=(count,),
        in_specs=[whole(qkv.shape), per_image((spots, SPAN)), per_image((SPAN, spots)), whole(bias.shape), whole(owner.shape)],
        out_specs=[whole((tok, width)), per_image((spots, wide)), per_image((tiles, SLOT, PACK * SLOT))],
        out_shape=[
            jax.ShapeDtypeStruct((tok, width), jnp.bfloat16),
            jax.ShapeDtypeStruct((count, spots, wide), jnp.bfloat16),
            jax.ShapeDtypeStruct((count, tiles, SLOT, PACK * SLOT), jnp.float32),
        ],
        scratch_shapes=[pltpu.VMEM((spots, width), jnp.bfloat16)],
        cost_estimate=pl.CostEstimate(flops=6_000_000_000, bytes_accessed=24_000_000, transcendentals=tok * width * 2),
        name="attend_forward",
    )(qkv, perm, perm_t, bias, owner)


def attend_backward(d_context, windows, probs, tables):
    perm, perm_t, _, owner, onehot = tables
    tok, width = d_context.shape
    count, spots, wide = windows.shape
    groups = width // (PACK * HD)
    tiles = probs.shape[1]
    d_mixed, d_bias, d_qv = pl.pallas_call(
        backward_kernel,
        grid=(count,),
        in_specs=[
            whole(d_context.shape), per_image((spots, wide)), per_image((tiles, SLOT, PACK * SLOT)),
            per_image((spots, SPAN)), per_image((SPAN, spots)), whole(owner.shape),
        ],
        out_specs=[whole((tok, wide)), whole((groups, SLOT, PACK * SLOT)), whole((2, width))],
        out_shape=[
            jax.ShapeDtypeStruct((tok, wide), jnp.bfloat16),
            jax.ShapeDtypeStruct((groups, SLOT, PACK * SLOT), jnp.float32),
            jax.ShapeDtypeStruct((2, width), jnp.float32),
        ],
        scratch_shapes=[pltpu.VMEM((spots, width), jnp.bfloat16), pltpu.VMEM((spots, wide), jnp.bfloat16)],
        cost_estimate=pl.CostEstimate(flops=9_000_000_000, bytes_accessed=32_000_000, transcendentals=0),
        name="attend_backward",
    )(d_context, windows, probs, perm, perm_t, owner)
    d_bias = d_bias.reshape(groups, SLOT, PACK, SLOT).transpose(0, 2, 1, 3).reshape(groups * PACK, SLOT * SLOT)
    d_table = lax.dot_general(
        onehot.astype(jnp.float32), d_bias, (((1,), (1,)), ((), ())), precision=lax.Precision.HIGHEST
    )
    return d_mixed, d_qv, d_table


def gelu_parts(pre_act):
    cdf_part = 0.5 * (1.0 + jax.scipy.special.erf(pre_act * inv_root_two))
    return (
        pre_act * cdf_part,
        cdf_part + pre_act * jnp.exp(-0.5 * pre_act * pre_act) * inv_root_two_pi,
    )


def layer_norm(rows, gain, shift):
    row_mean = jnp.mean(rows, -1, keepdims=True)
    row_var = jnp.mean(rows * rows, -1, keepdims=True) - row_mean * row_mean
    inv_std = lax.rsqrt(row_var + eps_norm)
    normed = (rows - row_mean) * inv_std
    return (normed, inv_std, normed * gain + shift)


def norm_back(d_out, normed, inv_std, gain):
    d_normed = d_out * gain
    return inv_std * (
        d_normed
        - jnp.mean(d_normed, -1, keepdims=True)
        - normed * jnp.mean(d_normed * normed, -1, keepdims=True)
    )


ROW_PAD = 16


def bit_of(index, bit):
    return (index // (1 << bit)) % 2


def bits_of(size):
    return size.bit_length() - 1


def greet(gx_size, gy_size):
    mine, row = lax.axis_index("gx"), lax.axis_index("gy")
    barrier = pltpu.get_barrier_semaphore()
    for name, index, size in (("gx", mine, gx_size), ("gy", row, gy_size)):
        for bit in range(bits_of(size)):
            there = index + (1 << bit) * (1 - 2 * bit_of(index, bit))
            pl.semaphore_signal(barrier, inc=1, device_id={name: there}, device_id_type=pl.DeviceIdType.MESH)
    pl.semaphore_wait(barrier, bits_of(gx_size) + bits_of(gy_size))


class Sender:
    def __init__(self, send, recv):
        self.send, self.recv, self.used = send, recv, 0

    def start(self, src, dst, name, there):
        copy = pltpu.make_async_remote_copy(
            src_ref=src,
            dst_ref=dst,
            send_sem=self.send.at[self.used],
            recv_sem=self.recv.at[self.used],
            device_id={name: there},
            device_id_type=pl.DeviceIdType.MESH,
        )
        self.used += 1
        copy.start()
        return copy


def split_steps(index, size):
    top = bits_of(size) - 1
    core = index % 2
    high, low = bit_of(index, top), bit_of(index, top - 1)
    big, small = 1 << top, 1 << (top - 1)
    first_step = (1 - core) * big * (1 - 2 * high) + core * small * (1 - 2 * low)
    second_step = (1 - core) * small * (1 - 2 * low) + core * big * (1 - 2 * high)
    return core, high, low, first_step, second_step


def gather_column(sender, local, slots, sizes, sem):
    gy_size = sizes[1]
    row = lax.axis_index("gy")
    own = [pltpu.make_async_copy(ref, slot.at[row], sem.at[n]) for n, (ref, slot) in enumerate(zip(local, slots))]
    for copy in own:
        copy.start()
    held = [row]
    for bit in range(bits_of(gy_size))[::-1]:
        step = (1 << bit) * (1 - 2 * bit_of(row, bit))
        copies = [
            sender.start(local[n] if place == 0 else slot.at[at], slot.at[at], "gy", row + step)
            for place, at in enumerate(held)
            for n, slot in enumerate(slots)
        ]
        yield
        for copy in copies:
            copy.wait()
        held = held + [at + step for at in held]
    for copy in own:
        copy.wait()


def join_rows(slots, full, groups):
    mine = lax.axis_index("gx")
    gy_size, rows, wide = slots.shape
    width = wide // groups
    at = pl.multiple_of(mine * rows, rows)
    for i in range(gy_size):
        for k in range(groups):
            low = (k * gy_size + i) * width
            full[pl.ds(at, rows), low : low + width] = slots[i, :, k * width : (k + 1) * width]


def gather_plane(sender, fulls, sizes):
    gx_size = sizes[0]
    mine = lax.axis_index("gx")
    core, _, _, first_step, second_step = split_steps(mine, gx_size)
    steps = [first_step, second_step]
    for bit in range(1, bits_of(gx_size) - 2)[::-1]:
        steps.append((1 << bit) * (1 - 2 * bit_of(mine, bit)))
    over = 1 - 2 * core

    def push(at, there):
        out = []
        for full in fulls:
            rows = full.shape[0] // gx_size
            view = full.at[pl.ds(pl.multiple_of(at * rows, rows), rows), :]
            out.append(sender.start(view, view, "gx", there))
        return out

    held = [mine]
    shared = []
    fresh = [mine]
    for step in steps:
        copies = [copy for at in held for copy in push(at, mine + step)]
        shared += [copy for at in fresh for copy in push(at, mine + over)]
        yield
        for copy in copies:
            copy.wait()
        fresh = [at + step for at in held]
        held = held + fresh
    shared += [copy for at in fresh for copy in push(at, mine + over)]
    yield
    for copy in shared:
        copy.wait()


def run_all(*streams):
    for stream in streams:
        for _ in stream:
            pass


def advance(stream, count=1):
    for _ in range(count):
        next(stream, None)


def gather_kernel(sizes, qkv_ref, proj_ref, small_ref, fc1_ref, fc2_ref, qkv_full, proj_full, fc1_full, fc2_full, small_all,
                  qkv_slots, proj_slots, fc1_slots, fc2_slots, send, recv, own_sem):
    gx_size, gy_size = sizes
    greet(gx_size, gy_size)
    sender = Sender(send, recv)

    def early():
        yield from gather_column(sender, [qkv_ref, proj_ref, small_ref], [qkv_slots, proj_slots, small_all], sizes, own_sem.at[0])
        join_rows(qkv_slots, qkv_full, 3)
        join_rows(proj_slots, proj_full, 1)
        yield from gather_plane(sender, [qkv_full, proj_full], sizes)

    def later():
        yield from gather_column(sender, [fc1_ref, fc2_ref], [fc1_slots, fc2_slots], sizes, own_sem.at[1])
        join_rows(fc1_slots, fc1_full, 1)
        join_rows(fc2_slots, fc2_full, 1)
        yield from gather_plane(sender, [fc1_full, fc2_full], sizes)

    first, second = early(), later()
    advance(first, 2)
    advance(second)
    while True:
        done = next(first, "done")
        advance(second)
        if done == "done":
            break
    run_all(second)


def vmem_spec():
    return pl.BlockSpec(memory_space=pltpu.VMEM)


def gather_weights(qkv, proj_t, small, fc1, fc2_t):
    sizes = (lax.axis_size("gx"), lax.axis_size("gy"))
    gx_size, gy_size = sizes
    rows = qkv.shape[0]
    full = [jax.ShapeDtypeStruct((rows * gx_size, v.shape[1] * gy_size), v.dtype) for v in (qkv, proj_t, fc1, fc2_t)]
    slots = [pltpu.VMEM((gy_size,) + v.shape, v.dtype) for v in (qkv, proj_t, fc1, fc2_t)]
    count = 5 * (gy_size - 1) + 4 * (gx_size - 1)
    return pl.pallas_call(
        functools.partial(gather_kernel, sizes),
        in_specs=[vmem_spec()] * 5,
        out_specs=[vmem_spec()] * 5,
        out_shape=full + [jax.ShapeDtypeStruct((gy_size,) + small.shape, small.dtype)],
        scratch_shapes=slots + [
            pltpu.SemaphoreType.DMA((count,)), pltpu.SemaphoreType.DMA((count,)), pltpu.SemaphoreType.DMA((2, 3)),
        ],
        compiler_params=pltpu.CompilerParams(collective_id=0, has_side_effects=True, vmem_limit_bytes=24 << 20),
        name="gather_weights",
    )(qkv, proj_t, small, fc1, fc2_t)


def add_into(target, left, right):
    target[...] = (left[...].astype(jnp.float32) + right[...].astype(jnp.float32)).astype(target.dtype)


def share_plane(sender, full, halves, sizes):
    gx_size = sizes[0]
    mine = lax.axis_index("gx")
    rows = full.shape[0] // gx_size
    core, high, low, first_step, second_step = split_steps(mine, gx_size)

    def block(at):
        return full.at[pl.ds(pl.multiple_of(at * rows, rows), rows), :]

    held = block
    count = gx_size
    for bit in range(bits_of(gx_size)):
        came = halves[bit]
        count //= 2
        own = bit_of(mine, bit)
        if count >= 4:
            step = (1 << bit) * (1 - 2 * own)
            away = [2 * k + 1 - own for k in range(count)]
            kept = [2 * k + own for k in range(count)]
        elif count == 2:
            step = second_step
            away = [(1 - core) * (2 * k + 1 - low) + core * (2 * (1 - high) + k) for k in range(count)]
            kept = [(1 - core) * (2 * k + low) + core * (2 * high + k) for k in range(count)]
        else:
            step = first_step
            last = (1 - core) * high + core * low
            away, kept = [1 - last], [last]
        copies = [sender.start(held(at), came.at[k], "gx", mine + step) for k, at in enumerate(away)]
        yield
        for k, at in enumerate(kept):
            copies[k].wait()
            add_into(came.at[k], came.at[k], held(at))
        held = (lambda ref: lambda at: ref.at[at])(came)


def share_column(sender, total, slots, halves, out, groups, sizes):
    gy_size = sizes[1]
    row = lax.axis_index("gy")
    width = slots.shape[2] // groups
    for i in range(gy_size):
        for k in range(groups):
            low = (k * gy_size + i) * width
            slots[i, :, k * width : (k + 1) * width] = total[0, :, low : low + width]
    held = slots
    count = gy_size
    for bit in range(bits_of(gy_size)):
        came = halves[bit]
        count //= 2
        own = bit_of(row, bit)
        step = (1 << bit) * (1 - 2 * own)
        copies = [sender.start(held.at[2 * k + 1 - own], came.at[k], "gy", row + step) for k in range(count)]
        yield
        for k in range(count):
            copies[k].wait()
            if count == 1:
                add_into(out, came.at[0], held.at[own])
            else:
                add_into(came.at[k], came.at[k], held.at[2 * k + own])
        held = came


def sum_small(sender, value, came, totals, out, sizes):
    held = value
    stage = 0
    stages = bits_of(sizes[0]) + bits_of(sizes[1])
    for name, size in (("gx", sizes[0]), ("gy", sizes[1])):
        index = lax.axis_index(name)
        for bit in range(bits_of(size)):
            there = index + (1 << bit) * (1 - 2 * bit_of(index, bit))
            copy = sender.start(held, came.at[stage], name, there)
            yield
            copy.wait()
            target = out if stage == stages - 1 else totals.at[stage]
            target[...] = held[...] + came[stage]
            held = target
            stage += 1


def share_kernel(sizes, groups, *refs):
    gx_size, gy_size = sizes
    arrays = len(groups)
    gx_bits, gy_bits = bits_of(gx_size), bits_of(gy_size)
    refs = list(refs)

    def take(count):
        out = refs[:count]
        del refs[:count]
        return out

    fulls, (small,) = take(arrays), take(1)
    outs, (small_out,) = take(arrays), take(1)
    planes = [take(gx_bits) for _ in range(arrays)]
    slots = take(arrays)
    columns = [take(gy_bits) for _ in range(arrays)]
    small_came, small_totals, send, recv = take(4)
    greet(gx_size, gy_size)
    sender = Sender(send, recv)

    def one(n):
        yield from share_plane(sender, fulls[n], planes[n], sizes)
        yield from share_column(sender, planes[n][-1], slots[n], columns[n], outs[n], groups[n], sizes)

    streams = [one(n) for n in range(arrays)] + [sum_small(sender, small, small_came, small_totals, small_out, sizes)]
    for _ in range(gx_bits + gy_bits + 1):
        for stream in streams:
            next(stream, None)


def share_sums(fulls, groups, small):
    sizes = (lax.axis_size("gx"), lax.axis_size("gy"))
    gx_size, gy_size = sizes
    gx_bits, gy_bits = bits_of(gx_size), bits_of(gy_size)
    rows = fulls[0].shape[0] // gx_size
    planes, slots, columns = [], [], []
    for full in fulls:
        wide = full.shape[1]
        planes += [pltpu.VMEM((gx_size >> (bit + 1), rows, wide), full.dtype) for bit in range(gx_bits)]
        slots.append(pltpu.VMEM((gy_size, rows, wide // gy_size), full.dtype))
        columns += [pltpu.VMEM((gy_size >> (bit + 1), rows, wide // gy_size), full.dtype) for bit in range(gy_bits)]
    stages = gx_bits + gy_bits
    count = len(fulls) * (gx_size - 1 + gy_size - 1) + stages
    return pl.pallas_call(
        functools.partial(share_kernel, sizes, groups),
        in_specs=[vmem_spec()] * (len(fulls) + 1),
        out_specs=[vmem_spec()] * (len(fulls) + 1),
        out_shape=[jax.ShapeDtypeStruct((rows, full.shape[1] // gy_size), jnp.float32) for full in fulls]
        + [jax.ShapeDtypeStruct(small.shape, small.dtype)],
        scratch_shapes=planes + slots + columns + [
            pltpu.VMEM((stages,) + small.shape, small.dtype),
            pltpu.VMEM((stages,) + small.shape, small.dtype),
            pltpu.SemaphoreType.DMA((count,)),
            pltpu.SemaphoreType.DMA((count,)),
        ],
        compiler_params=pltpu.CompilerParams(collective_id=1, has_side_effects=True, vmem_limit_bytes=40 << 20),
        name="share_sums",
    )(*fulls, small)


def pack_rows(values):
    rows = []
    for value in values:
        flat = value.reshape(-1)
        rows.append(jnp.pad(flat, (0, -flat.shape[0] % 1024)).reshape(-1, 128))
    return jnp.concatenate(rows, 0)


def unpack_rows(packed, shapes):
    at, out = 0, []
    for shape in shapes:
        size = int(np.prod(shape))
        count = (size + 1023) // 1024 * 8
        out.append(packed[at : at + count].reshape(-1)[:size].reshape(shape))
        at += count
    return out


def own_columns(summed, axis):
    size = summed.shape[axis] // lax.axis_size("gy")
    return lax.dynamic_slice_in_dim(summed, lax.axis_index("gy") * size, size, axis)


def local_live(tok_local, live_images):
    position = lax.axis_index("gy")
    per_device = tok_local // (GRID * GRID)
    slot_index = position * per_device + jnp.arange(tok_local, dtype=jnp.int32) // (GRID * GRID)
    return slot_index < live_images[0]


def blocked_layer(block_input, cotangent, live_images, params):
    (
        ln1_gain,
        ln1_bias,
        qkv_weight,
        qv_bias,
        rel_table,
        proj_weight,
        proj_bias,
        ln2_gain,
        ln2_bias,
        fc1_weight,
        fc1_bias,
        fc2_weight,
        fc2_bias,
    ) = params
    tok_local, width = block_input.shape
    block_rows = qkv_weight.shape[0]
    part, hidden_local = qkv_weight.shape[2], fc1_weight.shape[1]
    heads_local = rel_table.shape[1]

    def lane_row(value):
        value = value.reshape(value.shape[0], -1)
        return jnp.pad(value, ((0, 0), (0, hidden_local - value.shape[1])))

    small = jnp.concatenate([fc1_bias[None], lane_row(qv_bias.reshape(1, -1)), lane_row(rel_table.T)], 0)
    small = jnp.pad(small, ((0, ROW_PAD - small.shape[0]), (0, 0)))
    qkv_flat, proj_cols, fc1_rows, fc2_cols, small = gather_weights(
        qkv_weight.reshape(block_rows, -1), proj_weight.T, small, fc1_weight, fc2_weight.T
    )
    fc1_bias = small[:, 0].reshape(-1)
    qv_bias = small[:, 1, : 2 * part].reshape(-1, 2, part).transpose(1, 0, 2).reshape(2, -1)
    rel_table = small[:, 2 : 2 + heads_local, :RELS].reshape(-1, RELS)
    gain_one = ln1_gain.astype(jnp.float32)
    gain_two = ln2_gain.astype(jnp.float32)
    resid = block_input.astype(jnp.float32)
    normed_one, scale_one, pre_one = layer_norm(resid, gain_one, ln1_bias.astype(jnp.float32))
    hidden_one = (pre_one.astype(jnp.bfloat16))
    bias_row = jnp.stack([qv_bias[0], jnp.zeros_like(qv_bias[0]), qv_bias[1]]).reshape(1, 3 * width)
    mixed = (matmul(hidden_one, qkv_flat) + bias_row.astype(jnp.float32)).astype(jnp.bfloat16)
    tables = attention_tables(rel_table, tok_local // IMAGE)
    context, windows, probs = attend_forward(mixed, tables)
    resid_one = resid + (matmul_nt(context, proj_cols)) + proj_bias.astype(jnp.float32)
    normed_two, scale_two, pre_two = layer_norm(resid_one, gain_two, ln2_bias.astype(jnp.float32))
    hidden_two = (pre_two.astype(jnp.bfloat16))
    pre_act = matmul(hidden_two, fc1_rows) + fc1_bias.astype(jnp.float32)
    act_full, slope = gelu_parts(pre_act)
    act_low = act_full.astype(jnp.bfloat16)
    output = (
        resid_one + (matmul_nt(act_low, fc2_cols)) + fc2_bias.astype(jnp.float32)
    ).astype(jnp.bfloat16)
    live_rows = local_live(tok_local, live_images)
    grad_out = jnp.where(live_rows[:, None], cotangent, jnp.zeros_like(cotangent))
    grad_float = grad_out.astype(jnp.float32)
    grad_full = (grad_out)
    d_fc2_bias = jnp.sum(grad_float, 0)
    d_fc2_weight = matmul_tn(grad_full, act_low).astype(jnp.bfloat16)
    d_pre = matmul(grad_full, fc2_cols) * slope
    d_fc1_bias = jnp.sum(d_pre, 0)
    d_pre_low = d_pre.astype(jnp.bfloat16)
    d_fc1_weight = matmul_tn(hidden_two, d_pre_low).astype(jnp.bfloat16)
    d_hidden_two = (matmul_nt(d_pre_low, fc1_rows))
    d_ln2_gain = jnp.sum(d_hidden_two * normed_two, 0)
    d_ln2_bias = jnp.sum(d_hidden_two, 0)
    d_resid_one = grad_float + norm_back(d_hidden_two, normed_two, scale_two, gain_two)
    d_proj_bias = jnp.sum(d_resid_one, 0)
    d_resid_full = (d_resid_one.astype(jnp.bfloat16))
    d_proj_weight = matmul_tn(d_resid_full, context).astype(jnp.bfloat16)
    d_context = matmul(d_resid_full, proj_cols).astype(jnp.bfloat16)
    d_mixed, d_qv_bias, d_table = attend_backward(d_context, windows, probs, tables)
    d_qkv_weight = matmul_tn(hidden_one, d_mixed).astype(jnp.bfloat16)
    d_hidden_one = (matmul_nt(d_mixed, qkv_flat))
    d_ln1_gain = jnp.sum(d_hidden_one * normed_one, 0)
    d_ln1_bias = jnp.sum(d_hidden_one, 0)
    d_input = (d_resid_one + norm_back(d_hidden_one, normed_one, scale_one, gain_one)).astype(
        jnp.bfloat16
    )
    own = (d_ln1_gain, d_ln1_bias, d_proj_bias, d_ln2_gain, d_ln2_bias, d_fc2_bias, d_qv_bias, d_table, d_fc1_bias)
    d_fc1_weight, d_fc2_weight, d_qkv_weight, d_proj_weight, sums = share_sums(
        (d_fc1_weight, d_fc2_weight, d_qkv_weight, d_proj_weight), (1, 1, 3, 1), pack_rows(own)
    )
    d_fc2_weight = d_fc2_weight.T
    d_proj_weight = d_proj_weight.T
    d_qkv_weight = d_qkv_weight.reshape(block_rows, 3, part)
    sums = unpack_rows(sums, [value.shape for value in own])
    norm_sums = sums[:6]
    head_sums = (own_columns(sums[6], 1), own_columns(sums[7], 1), own_columns(sums[8], 0))
    return (
        output,
        d_input,
        norm_sums[0],
        norm_sums[1],
        d_qkv_weight,
        head_sums[0],
        head_sums[1],
        d_proj_weight,
        norm_sums[2],
        norm_sums[3],
        norm_sums[4],
        d_fc1_weight,
        head_sums[2],
        d_fc2_weight,
        norm_sums[5],
    )


def shards(
    block_input,
    cotangent,
    live_images,
    ln1_gain,
    ln1_bias,
    qkv_weight,
    qv_bias,
    rel_table,
    proj_weight,
    proj_bias,
    ln2_gain,
    ln2_bias,
    fc1_weight,
    fc1_bias,
    fc2_weight,
    fc2_bias,
):
    params = (
        ln1_gain,
        ln1_bias,
        qkv_weight,
        qv_bias,
        rel_table,
        proj_weight,
        proj_bias,
        ln2_gain,
        ln2_bias,
        fc1_weight,
        fc1_bias,
        fc2_weight,
        fc2_bias,
    )
    return blocked_layer(block_input, cotangent, live_images, params)


def solution(mesh):
    return jax.shard_map(
        shards,
        mesh=mesh,
        in_specs=(
            P(("gx", "gy"), None),
            P(("gx", "gy"), None),
            P("gx"),
            P(),
            P(),
            P("gx", None, "gy"),
            P(None, "gy"),
            P(None, "gy"),
            P("gy", "gx"),
            P(),
            P(),
            P(),
            P("gx", "gy"),
            P("gy"),
            P("gy", "gx"),
            P(),
        ),
        out_specs=(
            P(("gx", "gy"), None),
            P(("gx", "gy"), None),
            P(),
            P(),
            P("gx", None, "gy"),
            P(None, "gy"),
            P(None, "gy"),
            P("gy", "gx"),
            P(),
            P(),
            P(),
            P("gx", "gy"),
            P("gy"),
            P("gy", "gx"),
            P(),
        ),
        check_vma=False,
    )
```

profile of v0, /device:TPU:0, one launch (start us, length us, event | category | flops | bytes accessed | tf_op | source)
XLA Modules:
  0.0 208.6 jit_solution(3776690239549946744)
XLA Ops:
  0.7 0.8 copy-done
  1.5 0.7 broadcast_in_dim.9
  2.1 0.7 copy.61
  2.8 0.7 fusion.31
  3.5 0.8 copy-done.1
  4.4 0.8 copy-done.2
  5.2 0.7 copy-done.3
  5.9 51.5 %gather_weights.1 = (bf16[512,1536]{1,0:T(8,128)(2,1)S(1)}, bf16[512,512]{1,0:T(8,128)(2,1)S(1)}, bf16[512,2048]{1,0:T(8,128)(2,1)S(1)}, bf16[512,2048]{1,0:T(8,128)(2,1)S(1)}, bf16[4,16,512]{2,1,0:T(8,128)(2,1)S(1)}) custom-call(bf16[64,384]{1,0:T(8,128)(2,1)S(1)} %copy_bitcast_fusion.2.qkv_ref, bf16[64,128]{1,0:T(8,128)(2,1)S(1)} %bitcast.105, ...), custom_call_target="tpu_custom_call" | custom-call | tf_op jit(solution)/shard_map/gather_weights/pallas_call | solution.py:431
  57.4 1.3 copy-done.4
  58.8 1.2 copy-done.7
  60.1 1.5 convert_reduce_fusion
  61.6 0.7 convert_element_type.111
  62.3 0.7 convert_element_type.112
  63.6 4.6 %add_convert_fusion.qkv_ref = bf16[784,1536]{1,0:T(8,128)(2,1)} fusion(bf16[512,1536]{1,0:T(8,128)(2,1)} %copy-done.7, f32[1536]{0:T(1024)S(1)} %reshape.243, bf16[784,512]{1,0:T(8,128)(2,1)} %param.21, f32[512]{0:T(512)S(1)} %convert_element_type.112, f32[512]{0:T(512)S(1)} %convert_element_type.111, f32[784]{0:T(1024)S(1)} %get-tuple-element.101, ...), kind=kOutput, calls=%fused_computation.8 | convolution fusion | flops 1237942272 | bytes 4800640 | tf_op jit(solution)/shard_map/dot_general | solution.py:24
  68.2 0.7 iota_compare_fusion
  69.0 0.9 convolution_bitcast_fusion
  70.0 1.9 add.156
  72.0 1.5 add.157
  73.5 1.1 broadcast_add_fusion.bias_ref
  74.6 11.5 %attend_forward.1 = (bf16[784,512]{1,0:T(8,128)(2,1)}, bf16[4,256,1536]{2,1,0:T(8,128)(2,1)}, f32[4,8,64,512]{3,2,1,0:T(8,128)}) custom-call(bf16[784,1536]{1,0:T(8,128)(2,1)} %add_convert_fusion.qkv_ref, bf16[4,256,208]{2,1,0:T(8,128)(2,1)} %constant.93.perm_ref, bf16[4,208,256]{2,1,0:T(8,128)(2,1)} %constant.94.perm_t_ref, ...), custom_call_target="tpu_custom_call" | custom-call | flops 6000000000 | bytes 24000000 | tf_op jit(solution)/shard_map/attend_forward/pallas_call | solution.py:193
  86.2 2.1 %fusion.41 = (f32[784]{0:T(1024)S(1)}, f32[784]{0:T(1024)S(1)}, f32[784,512]{1,0:T(8,128)S(1)}) fusion(f32[512]{0:T(512)S(1)} %convert_element_type.120, bf16[784,512]{1,0:T(8,128)(2,1)} %get-tuple-element.33, bf16[512,512]{1,0:T(8,128)(2,1)S(1)} %get-tuple-element.34, bf16[784,512]{1,0:T(8,128)(2,1)S(1)} %copy-done.14), kind=kOutput, calls=%fused_computation.111 | convolution fusion | flops 413448704 | bytes 3743872 | tf_op jit(solution)/shard_map/dot_general | solution.py:34
  88.5 5.5 %multiply_convert_fusion = (bf16[784,2048]{1,0:T(8,128)(2,1)}, f32[784,2048]{1,0:T(8,128)}) fusion(f32[2048]{0:T(1024)S(1)} %bitcast.109, bf16[512,2048]{1,0:T(8,128)(2,1)S(1)} %copy-done.5, f32[784,512]{1,0:T(8,128)S(1)} %get-tuple-element.104, f32[512]{0:T(512)S(1)} %convert_element_type.122, f32[512]{0:T(512)S(1)} %convert_element_type.121, ...), kind=kOutput, calls=%fused_computation.6 | convolution fusion | flops 1655808000 | bytes 13355136 | tf_op jit(solution)/shard_map/dot_general | solution.py:24
  94.7 6.2 %fusion.43 = (f32[2048]{0:T(1024)S(1)}, bf16[784,2048]{1,0:T(8,128)(2,1)S(1)}) fusion(f32[784,2048]{1,0:T(8,128)} %get-tuple-element.106, f32[2048]{0:T(1024)} %bitcast.110, bf16[512,2048]{1,0:T(8,128)(2,1)S(1)} %get-tuple-element.36, bf16[784,512]{1,0:T(8,128)(2,1)} %param.22, pred[784]{0:T(1024)(128)(4,1)S(1)} %fusion.34), kind=kOutput, calls=%fused_computation.113 | convolution fusion | flops 1663834112 | bytes 12550928 | tf_op jit(solution)/shard_map/dot_general | solution.py:24
  100.9 2.3 %multiply_reduce_fusion = (f32[512]{0:T(512)S(1)}, f32[784]{0:T(1024)S(1)}, f32[784]{0:T(1024)S(1)}, f32[512]{0:T(512)S(1)}, f32[784,512]{1,0:T(8,128)S(1)}) fusion(f32[784,512]{1,0:T(8,128)S(1)} %copy-done.10, f32[784]{0:T(1024)S(1)} %get-tuple-element.99, f32[784]{0:T(1024)S(1)} %get-tuple-element.98, f32[512]{0:T(512)S(1)} %convert_element_type.121, ...), kind=kOutput, calls=%fused_computation.36 | convolution fusion | flops 1647777280 | bytes 8538368 | tf_op jit(solution)/shard_map/dot_general | solution.py:34
  103.3 1.1 fusion.42
  104.4 1.5 convolution_convert_fusion.3.d_context_ref
  105.9 15.8 %attend_backward.1 = (bf16[784,1536]{1,0:T(8,128)(2,1)}, f32[2,64,512]{2,1,0:T(8,128)}, f32[2,512]{1,0:T(2,128)}) custom-call(bf16[784,512]{1,0:T(8,128)(2,1)} %convolution_convert_fusion.3.d_context_ref, bf16[4,256,1536]{2,1,0:T(8,128)(2,1)} %get-tuple-element.37.windows_ref, f32[4,8,64,512]{3,2,1,0:T(8,128)} %get-tuple-element.38.probs_ref, ...), custom_call_target="tpu_custom_call" | custom-call | flops 8999999488 | bytes 32000000 | tf_op jit(solution)/shard_map/attend_backward/pallas_call | solution.py:215
  121.7 5.5 %fusion.18 = (f32[512]{0:T(512)S(1)}, f32[784]{0:T(1024)}, f32[784]{0:T(1024)}, f32[512]{0:T(512)S(1)}, f32[784,512]{1,0:T(8,128)}) fusion(bf16[784,512]{1,0:T(8,128)(2,1)S(1)} %copy-done.14, f32[784]{0:T(1024)S(1)} %get-tuple-element.101, f32[784]{0:T(1024)S(1)} %get-tuple-element.100, f32[512]{0:T(512)S(1)} %copy-done.21, ...), kind=kOutput, calls=%fused_computation.33 | convolution fusion | flops 1237136896 | bytes 6408448 | tf_op jit(solution)/shard_map/dot_general | solution.py:34
  127.3 0.9 reshape.236
  128.3 2.0 copy.59
  130.2 1.2 reshape.237
  131.5 1.4 fusion.5
  133.0 2.5 %convolution_convert_fusion.4.refs_3_ = bf16[512,512]{1,0:T(8,128)(2,1)S(1)} fusion(bf16[784,512]{1,0:T(8,128)(2,1)} %get-tuple-element.33, f32[784,512]{1,0:T(8,128)} %copy-done.8), kind=kOutput, calls=%fused_computation.49 | convolution fusion | flops 411705344 | bytes 2932736 | tf_op jit(solution)/shard_map/dot_general | solution.py:28
  135.5 4.7 %convolution_convert_fusion.1.refs_0_ = bf16[512,2048]{1,0:T(8,128)(2,1)S(1)} fusion(bf16[784,2048]{1,0:T(8,128)(2,1)} %copy-done.13, f32[784,512]{1,0:T(8,128)S(1)} %copy-done.11, f32[512]{0:T(512)S(1)} %convert_element_type.122, f32[512]{0:T(512)S(1)} %convert_element_type.121, f32[784]{0:T(1024)S(1)} %get-tuple-element.99, f32[784]{0:T(1024)S(1)} %get-tuple-element.98), kind=kOutput, calls=%fused_computation.11 | convolution fusion | flops 1647222784 | bytes 6924416 | tf_op jit(solution)/shard_map/dot_general | solution.py:28
  140.2 2.0 convolution_convert_fusion.2.refs_2_
  142.4 2.5 %convolution_convert_fusion.refs_1_ = bf16[512,2048]{1,0:T(8,128)(2,1)S(1)} fusion(bf16[784,2048]{1,0:T(8,128)(2,1)S(1)} %copy-done.30, bf16[784,512]{1,0:T(8,128)(2,1)S(1)} %copy-done.16, pred[784]{0:T(1024)(128)(4,1)S(1)} %fusion.34), kind=kOutput, calls=%fused_computation.10 | convolution fusion | flops 1645617152 | bytes 6112016 | tf_op jit(solution)/shard_map/dot_general | solution.py:28
  144.9 49.3 %share_sums.1 = (f32[64,512]{1,0:T(8,128)S(1)}, f32[64,512]{1,0:T(8,128)S(1)}, f32[64,384]{1,0:T(8,128)S(1)}, f32[64,128]{1,0:T(8,128)S(1)}, f32[96,128]{1,0:T(8,128)S(1)}) custom-call(bf16[512,2048]{1,0:T(8,128)(2,1)S(1)} %convolution_convert_fusion.1.refs_0_, bf16[512,2048]{1,0:T(8,128)(2,1)S(1)} %convolution_convert_fusion.refs_1_, ...), custom_call_target="tpu_custom_call" | custom-call | tf_op jit(solution)/shard_map/share_sums/pallas_call | solution.py:569
  194.3 0.6 slice.110
  194.9 1.0 constant_dynamic-slice_fusion
  195.9 0.7 copy.44
  196.6 0.6 copy_bitcast_fusion.1
  197.2 0.7 dynamic_slice.11
  199.0 0.7 broadcast_multiply_fusion
  199.7 0.7 broadcast_multiply_fusion.1
  200.4 3.5 %fusion.17 = bf16[784,512]{1,0:T(8,128)(2,1)} fusion(f32[784,512]{1,0:T(8,128)} %copy-done.8, bf16[784,512]{1,0:T(8,128)(2,1)S(1)} %copy-done.14, f32[784,512]{1,0:T(8,128)} %get-tuple-element.108, f32[784]{0:T(1024)S(1)} %broadcast_multiply_fusion, f32[784]{0:T(1024)S(1)} %broadcast_multiply_fusion.1, f32[512]{0:T(512)} %copy-done.20, ...), kind=kLoop, calls=%fused_computation.32 | loop fusion | flops 4014080 | bytes 4831488 | tf_op jit(solution)/shard_map/convert_element_type | solution.py:690
  204.0 2.8 %add_convert_fusion.1 = bf16[784,512]{1,0:T(8,128)(2,1)} fusion(f32[784,512]{1,0:T(8,128)S(1)} %copy-done.12, bf16[784,2048]{1,0:T(8,128)(2,1)S(1)} %copy-done.31, bf16[512,2048]{1,0:T(8,128)(2,1)S(1)} %get-tuple-element.36, f32[512]{0:T(512)S(1)} %convert_element_type.127), kind=kOutput, calls=%fused_computation.41 | convolution fusion | flops 1645371392 | bytes 7718912 | tf_op jit(solution)/shard_map/dot_general | solution.py:34
  207.3 0.7 copy.77
  208.0 0.7 copy.78
  (101 shorter events, 3.3 us)
Async XLA Ops:
  0.6 0.8 copy-start
  3.5 0.8 copy-start.1
  4.4 0.8 copy-start.2
  5.2 0.7 copy-start.3
  57.4 1.3 copy-start.4
  58.8 1.2 copy-start.7
  62.3 0.7 copy-start.20
  63.0 0.6 copy-start.24
  63.6 4.7 %copy-start.18 = (s32[4096]{0:T(1024)S(1)}, s32[4096]{0:T(1024)}, u32[]{:S(2)}) copy-start(s32[4096]{0:T(1024)} %constant.95) | copy-start | bytes 49156
  74.6 11.5 %copy-start.26 = (bf16[512]{0:T(512)(128)(2,1)S(1)}, bf16[512]{0:T(512)(128)(2,1)}, u32[]{:S(2)}) copy-start(bf16[512]{0:T(512)(128)(2,1)} %param.30) | copy-start | bytes 3076
  74.6 11.6 %copy-start.14 = (bf16[784,512]{1,0:T(8,128)(2,1)S(1)}, bf16[784,512]{1,0:T(8,128)(2,1)}, u32[]{:S(2)}) copy-start(bf16[784,512]{1,0:T(8,128)(2,1)} %param.21) | copy-start | bytes 2408452
  86.2 2.2 %copy-start.27 = (bf16[512]{0:T(512)(128)(2,1)S(1)}, bf16[512]{0:T(512)(128)(2,1)}, u32[]{:S(2)}) copy-start(bf16[512]{0:T(512)(128)(2,1)} %param.31) | copy-start | bytes 3076
  86.2 2.2 %copy-start.28 = (bf16[512]{0:T(512)(128)(2,1)S(1)}, bf16[512]{0:T(512)(128)(2,1)}, u32[]{:S(2)}) copy-start(bf16[512]{0:T(512)(128)(2,1)} %param.32) | copy-start | bytes 3076
  86.2 2.2 %copy-start.5 = (bf16[512,2048]{1,0:T(8,128)(2,1)S(1)}, bf16[512,2048]{1,0:T(8,128)(2,1)}, u32[]{:S(2)}) copy-start(bf16[512,2048]{1,0:T(8,128)(2,1)} %copy-done.4) | copy-start | bytes 6291460
  88.4 5.6 %copy-start.9 = (f32[784,512]{1,0:T(8,128)}, f32[784,512]{1,0:T(8,128)S(1)}, u32[]{:S(2)}) copy-start(f32[784,512]{1,0:T(8,128)S(1)} %get-tuple-element.104) | copy-start | bytes 4816900
  88.4 5.6 %copy-start.22 = (f32[4,1,512]{2,1,0:T(1,128)}, f32[4,1,512]{2,1,0:T(1,128)S(1)}, u32[]{:S(2)}) copy-start(f32[4,1,512]{2,1,0:T(1,128)S(1)} %slice_convert_fusion) | copy-start | bytes 24580
  94.6 6.3 %copy-start.6 = (bf16[512,2048]{1,0:T(8,128)(2,1)S(1)}, bf16[512,2048]{1,0:T(8,128)(2,1)}, u32[]{:S(2)}) copy-start(bf16[512,2048]{1,0:T(8,128)(2,1)} %copy-done.4) | copy-start | bytes 6291460
  94.7 6.3 %copy-start.10 = (f32[784,512]{1,0:T(8,128)S(1)}, f32[784,512]{1,0:T(8,128)}, u32[]{:S(2)}) copy-start(f32[784,512]{1,0:T(8,128)} %copy-done.9) | copy-start | bytes 4816900
  100.9 2.3 %copy-start.13 = (bf16[784,2048]{1,0:T(8,128)(2,1)}, bf16[784,2048]{1,0:T(8,128)(2,1)S(1)}, u32[]{:S(2)}) copy-start(bf16[784,2048]{1,0:T(8,128)(2,1)S(1)} %get-tuple-element.110) | copy-start | bytes 9633796
  100.9 2.3 %copy-start.15 = (bf16[784,512]{1,0:T(8,128)(2,1)S(1)}, bf16[784,512]{1,0:T(8,128)(2,1)}, u32[]{:S(2)}) copy-start(bf16[784,512]{1,0:T(8,128)(2,1)} %param.22) | copy-start | bytes 2408452
  104.4 1.5 copy-start.8
  105.9 15.8 %copy-start.21 = (f32[512]{0:T(512)S(1)}, f32[512]{0:T(512)}, u32[]{:S(2)}) copy-start(f32[512]{0:T(512)} %copy-done.20) | copy-start | bytes 6148
  121.7 5.6 %copy-start.23 = (f32[2,512]{1,0:T(2,128)S(1)}, f32[2,512]{1,0:T(2,128)}, u32[]{:S(2)}) copy-start(f32[2,512]{1,0:T(2,128)} %get-tuple-element.40) | copy-start | bytes 12292
  121.7 5.6 %copy-start.17 = (f32[2,64,512]{2,1,0:T(8,128)S(1)}, f32[2,64,512]{2,1,0:T(8,128)}, u32[]{:S(2)}) copy-start(f32[2,64,512]{2,1,0:T(8,128)} %get-tuple-element.41) | copy-start | bytes 786436
  127.2 4.2 %copy-start.19 = (s32[4096]{0:T(1024)S(1)}, s32[4096]{0:T(1024)}, u32[]{:S(2)}) copy-start(s32[4096]{0:T(1024)} %constant.95) | copy-start | bytes 49156
  133.0 2.5 %copy-start.11 = (f32[784,512]{1,0:T(8,128)S(1)}, f32[784,512]{1,0:T(8,128)}, u32[]{:S(2)}) copy-start(f32[784,512]{1,0:T(8,128)} %copy-done.9) | copy-start | bytes 4816900
  135.5 4.7 %copy-start.25 = (f32[512]{0:T(512)S(1)}, f32[512]{0:T(512)}, u32[]{:S(2)}) copy-start(f32[512]{0:T(512)} %copy-done.24) | copy-start | bytes 6148
  135.5 4.7 %copy-start.32 = (bf16[784,1536]{1,0:T(8,128)(2,1)S(1)}, bf16[784,1536]{1,0:T(8,128)(2,1)}, u32[]{:S(2)}) copy-start(bf16[784,1536]{1,0:T(8,128)(2,1)} %get-tuple-element.39) | copy-start | bytes 7225348
  140.2 2.0 copy-start.16
  140.2 2.2 %copy-start.30 = (bf16[784,2048]{1,0:T(8,128)(2,1)S(1)}, bf16[784,2048]{1,0:T(8,128)(2,1)}, u32[]{:S(2)}) copy-start(bf16[784,2048]{1,0:T(8,128)(2,1)} %get-tuple-element.105) | copy-start | bytes 9633796
  200.4 3.5 %copy-start.29 = (bf16[512]{0:T(512)(128)(2,1)S(1)}, bf16[512]{0:T(512)(128)(2,1)}, u32[]{:S(2)}) copy-start(bf16[512]{0:T(512)(128)(2,1)} %param.36) | copy-start | bytes 3076
  200.4 3.5 %copy-start.12 = (f32[784,512]{1,0:T(8,128)S(1)}, f32[784,512]{1,0:T(8,128)}, u32[]{:S(2)}) copy-start(f32[784,512]{1,0:T(8,128)} %copy-done.9) | copy-start | bytes 4816900
  200.4 3.5 %copy-start.31 = (bf16[784,2048]{1,0:T(8,128)(2,1)S(1)}, bf16[784,2048]{1,0:T(8,128)(2,1)}, u32[]{:S(2)}) copy-start(bf16[784,2048]{1,0:T(8,128)(2,1)} %get-tuple-element.105) | copy-start | bytes 9633796
where the time goes:
time: 209 us
  Pallas kernels  128 us (61%)
  matrix products  44.5 us (21%)
  local copies, waits for them, and re-layouts  22.6 us (11%)
  other arithmetic  11.5 us (6%)
    pallas_call x1, Pallas kernels, gather_weights(): pl.pallas_call(functools.partial(gather_kernel, sizes), in_specs=[vmem_sp...  51.5 us
    pallas_call x1, Pallas kernels, share_sums(): pl.pallas_call(functools.partial(share_kernel, sizes, groups), in_specs=[...  49.3 us
    dot_general x4, matrix products, matmul(): return jnp.dot(left, right, preferred_element_type=jnp.float32)  17.8 us
    pallas_call x1, Pallas kernels, attend_backward(): pl.pallas_call(backward_kernel, grid=(count,), in_specs=[whole(d_context....  15.8 us
    dot_general x4, matrix products, matmul_nt(): lax.dot_general(left, right, (((1,), (1,)), ((), ())), preferred_element_...  12.7 us
    dot_general x4, matrix products, matmul_tn(): lax.dot_general(left, right, (((0,), (0,)), ((), ())), preferred_element_...  11.6 us
    pallas_call x1, Pallas kernels, attend_forward(): pl.pallas_call(forward_kernel, grid=(count,), in_specs=[whole(qkv.shape),...  11.5 us
    unnamed x81, local copies, waits for them, and re-layouts  10.5 us

commit v1 on v0

--- a/solution.py
+++ b/solution.py
@@ -184,56 +184,77 @@
     return pl.BlockSpec((1,) + shape, lambda n: (n,) + (0,) * len(shape))
 
 
-def attend_forward(qkv, tables):
+def attend_forward(qkv, tables, later):
     perm, perm_t, bias, owner, _ = tables
     tok, wide = qkv.shape
     width = wide // 3
     count, spots = perm.shape[:2]
     tiles = WIN_COUNT * width // (PACK * HD)
+    sizes = mesh_sizes()
+    copies = len(later) * (sizes[0] - 1)
     return pl.pallas_call(
-        forward_kernel,
+        functools.partial(forward_stage, sizes),
         grid=(count,),
-        in_specs=[whole(qkv.shape), per_image((spots, SPAN)), per_image((SPAN, spots)), whole(bias.shape), whole(owner.shape)],
-        out_specs=[whole((tok, width)), per_image((spots, wide)), per_image((tiles, SLOT, PACK * SLOT))],
+        in_specs=[whole(qkv.shape), per_image((spots, SPAN)), per_image((SPAN, spots)), whole(bias.shape), whole(owner.shape)]
+        + [whole(rows.shape) for rows in later],
+        out_specs=[whole((tok, width)), per_image((spots, wide)), per_image((tiles, SLOT, PACK * SLOT))] + [hbm_spec()] * len(later),
         out_shape=[
             jax.ShapeDtypeStruct((tok, width), jnp.bfloat16),
             jax.ShapeDtypeStruct((count, spots, wide), jnp.bfloat16),
             jax.ShapeDtypeStruct((count, tiles, SLOT, PACK * SLOT), jnp.float32),
+        ]
+        + [jax.ShapeDtypeStruct((rows.shape[0] * sizes[0], rows.shape[1]), rows.dtype) for rows in later],
+        scratch_shapes=[
+            pltpu.VMEM((spots, width), jnp.bfloat16),
+            pltpu.SemaphoreType.DMA((copies,)),
+            pltpu.SemaphoreType.DMA((copies,)),
+            pltpu.SemaphoreType.DMA((len(later),)),
         ],
-        scratch_shapes=[pltpu.VMEM((spots, width), jnp.bfloat16)],
+        compiler_params=pltpu.CompilerParams(collective_id=2, has_side_effects=True, vmem_limit_bytes=32 << 20),
         cost_estimate=pl.CostEstimate(flops=6_000_000_000, bytes_accessed=24_000_000, transcendentals=tok * width * 2),
         name="attend_forward",
-    )(qkv, perm, perm_t, bias, owner)
-
-
-def attend_backward(d_context, windows, probs, tables):
+    )(qkv, perm, perm_t, bias, owner, *later)
+
+
+def attend_backward(d_context, windows, probs, tables, sums):
     perm, perm_t, _, owner, onehot = tables
     tok, width = d_context.shape
     count, spots, wide = windows.shape
     groups = width // (PACK * HD)
     tiles = probs.shape[1]
-    d_mixed, d_bias, d_qv = pl.pallas_call(
-        backward_kernel,
+    sizes = mesh_sizes()
+    blocks = [(full.shape[0] // sizes[0], full.shape[1]) for full in sums]
+    halves = [
+        pltpu.VMEM((sizes[0] >> (bit + 1),) + block, jnp.bfloat16) for block in blocks for bit in range(bits_of(sizes[0]))
+    ]
+    copies = len(sums) * (sizes[0] - 1)
+    d_mixed, d_bias, d_qv, *sums = pl.pallas_call(
+        functools.partial(backward_stage, sizes),
         grid=(count,),
         in_specs=[
             whole(d_context.shape), per_image((spots, wide)), per_image((tiles, SLOT, PACK * SLOT)),
             per_image((spots, SPAN)), per_image((SPAN, spots)), whole(owner.shape),
-        ],
-        out_specs=[whole((tok, wide)), whole((groups, SLOT, PACK * SLOT)), whole((2, width))],
+        ]
+        + [whole(full.shape) for full in sums],
+        out_specs=[whole((tok, wide)), whole((groups, SLOT, PACK * SLOT)), whole((2, width))] + [whole(block) for block in blocks],
         out_shape=[
             jax.ShapeDtypeStruct((tok, wide), jnp.bfloat16),
             jax.ShapeDtypeStruct((groups, SLOT, PACK * SLOT), jnp.float32),
             jax.ShapeDtypeStruct((2, width), jnp.float32),
-        ],
-        scratch_shapes=[pltpu.VMEM((spots, width), jnp.bfloat16), pltpu.VMEM((spots, wide), jnp.bfloat16)],
+        ]
+        + [jax.ShapeDtypeStruct(block, jnp.bfloat16) for block in blocks],
+        scratch_shapes=[pltpu.VMEM((spots, width), jnp.bfloat16), pltpu.VMEM((spots, wide), jnp.bfloat16)]
+        + halves
+        + [pltpu.SemaphoreType.DMA((copies,)), pltpu.SemaphoreType.DMA((copies,))],
+        compiler_params=pltpu.CompilerParams(collective_id=3, has_side_effects=True, vmem_limit_bytes=44 << 20),
         cost_estimate=pl.CostEstimate(flops=9_000_000_000, bytes_accessed=32_000_000, transcendentals=0),
         name="attend_backward",
-    )(d_context, windows, probs, perm, perm_t, owner)
+    )(d_context, windows, probs, perm, perm_t, owner, *sums)
     d_bias = d_bias.reshape(groups, SLOT, PACK, SLOT).transpose(0, 2, 1, 3).reshape(groups * PACK, SLOT * SLOT)
     d_table = lax.dot_general(
         onehot.astype(jnp.float32), d_bias, (((1,), (1,)), ((), ())), precision=lax.Precision.HIGHEST
     )
-    return d_mixed, d_qv, d_table
+    return d_mixed, d_qv, d_table, sums
 
 
 def gelu_parts(pre_act):
@@ -286,7 +307,7 @@
     def __init__(self, send, recv):
         self.send, self.recv, self.used = send, recv, 0
 
-    def start(self, src, dst, name, there):
+    def plan(self, src, dst, name, there):
         copy = pltpu.make_async_remote_copy(
             src_ref=src,
             dst_ref=dst,
@@ -296,8 +317,19 @@
             device_id_type=pl.DeviceIdType.MESH,
         )
         self.used += 1
-        copy.start()
         return copy
+
+
+def phase(waits=(), act=None, starts=()):
+    def run():
+        for copy in waits:
+            copy.wait()
+        if act is not None:
+            act()
+        for copy in starts:
+            copy.start()
+
+    return run
 
 
 def split_steps(index, size):
@@ -310,142 +342,81 @@
     return core, high, low, first_step, second_step
 
 
-def gather_column(sender, local, slots, sizes, sem):
-    gy_size = sizes[1]
+def gather_column(sender, local, slots, sem, sizes, act=None):
     row = lax.axis_index("gy")
     own = [pltpu.make_async_copy(ref, slot.at[row], sem.at[n]) for n, (ref, slot) in enumerate(zip(local, slots))]
-    for copy in own:
-        copy.start()
+    waits, starts, phases = [], list(own), []
     held = [row]
-    for bit in range(bits_of(gy_size))[::-1]:
+    for bit in range(bits_of(sizes[1]))[::-1]:
         step = (1 << bit) * (1 - 2 * bit_of(row, bit))
         copies = [
-            sender.start(local[n] if place == 0 else slot.at[at], slot.at[at], "gy", row + step)
+            sender.plan(local[n] if place == 0 else slot.at[at], slot.at[at], "gy", row + step)
             for place, at in enumerate(held)
             for n, slot in enumerate(slots)
         ]
-        yield
-        for copy in copies:
-            copy.wait()
+        phases.append(phase(waits, None, starts + copies))
+        waits, starts = copies, []
         held = held + [at + step for at in held]
-    for copy in own:
-        copy.wait()
-
-
-def join_rows(slots, full, groups):
-    mine = lax.axis_index("gx")
-    gy_size, rows, wide = slots.shape
+    phases.append(phase(waits + own, act))
+    return phases
+
+
+def join_rows(slots, rows_ref, groups):
+    gy_size, _, wide = slots.shape
     width = wide // groups
-    at = pl.multiple_of(mine * rows, rows)
     for i in range(gy_size):
         for k in range(groups):
             low = (k * gy_size + i) * width
-            full[pl.ds(at, rows), low : low + width] = slots[i, :, k * width : (k + 1) * width]
-
-
-def gather_plane(sender, fulls, sizes):
+            rows_ref[:, low : low + width] = slots[i, :, k * width : (k + 1) * width]
+
+
+def gather_plane(sender, own, full, sem, sizes):
     gx_size = sizes[0]
     mine = lax.axis_index("gx")
+    rows = own.shape[0]
     core, _, _, first_step, second_step = split_steps(mine, gx_size)
     steps = [first_step, second_step]
     for bit in range(1, bits_of(gx_size) - 2)[::-1]:
         steps.append((1 << bit) * (1 - 2 * bit_of(mine, bit)))
     over = 1 - 2 * core
 
-    def push(at, there):
-        out = []
-        for full in fulls:
-            rows = full.shape[0] // gx_size
-            view = full.at[pl.ds(pl.multiple_of(at * rows, rows), rows), :]
-            out.append(sender.start(view, view, "gx", there))
-        return out
-
-    held = [mine]
-    shared = []
-    fresh = [mine]
-    for step in steps:
-        copies = [copy for at in held for copy in push(at, mine + step)]
-        shared += [copy for at in fresh for copy in push(at, mine + over)]
-        yield
-        for copy in copies:
-            copy.wait()
+    def view(at):
+        return full.at[pl.ds(pl.multiple_of(at * rows, rows), rows), :]
+
+    def push(at, first, there):
+        return sender.plan(own if first else view(at), view(at), "gx", there)
+
+    keep = pltpu.make_async_copy(own, view(mine), sem)
+    held, fresh = [mine], [mine]
+    waits, shared, phases = [], [keep], []
+    for place, step in enumerate(steps):
+        copies = [push(at, n == 0, mine + step) for n, at in enumerate(held)]
+        across = [push(at, place == 0, mine + over) for at in fresh]
+        phases.append(phase(waits, None, copies + across + ([keep] if place == 0 else [])))
+        waits = copies
+        shared += across
         fresh = [at + step for at in held]
         held = held + fresh
-    shared += [copy for at in fresh for copy in push(at, mine + over)]
-    yield
-    for copy in shared:
-        copy.wait()
-
-
-def run_all(*streams):
-    for stream in streams:
-        for _ in stream:
-            pass
-
-
-def advance(stream, count=1):
-    for _ in range(count):
-        next(stream, None)
-
-
-def gather_kernel(sizes, qkv_ref, proj_ref, small_ref, fc1_ref, fc2_ref, qkv_full, proj_full, fc1_full, fc2_full, small_all,
-                  qkv_slots, proj_slots, fc1_slots, fc2_slots, send, recv, own_sem):
-    gx_size, gy_size = sizes
-    greet(gx_size, gy_size)
-    sender = Sender(send, recv)
-
-    def early():
-        yield from gather_column(sender, [qkv_ref, proj_ref, small_ref], [qkv_slots, proj_slots, small_all], sizes, own_sem.at[0])
-        join_rows(qkv_slots, qkv_full, 3)
-        join_rows(proj_slots, proj_full, 1)
-        yield from gather_plane(sender, [qkv_full, proj_full], sizes)
-
-    def later():
-        yield from gather_column(sender, [fc1_ref, fc2_ref], [fc1_slots, fc2_slots], sizes, own_sem.at[1])
-        join_rows(fc1_slots, fc1_full, 1)
-        join_rows(fc2_slots, fc2_full, 1)
-        yield from gather_plane(sender, [fc1_full, fc2_full], sizes)
-
-    first, second = early(), later()
-    advance(first, 2)
-    advance(second)
-    while True:
-        done = next(first, "done")
-        advance(second)
-        if done == "done":
-            break
-    run_all(second)
-
-
-def vmem_spec():
-    return pl.BlockSpec(memory_space=pltpu.VMEM)
-
-
-def gather_weights(qkv, proj_t, small, fc1, fc2_t):
-    sizes = (lax.axis_size("gx"), lax.axis_size("gy"))
-    gx_size, gy_size = sizes
-    rows = qkv.shape[0]
-    full = [jax.ShapeDtypeStruct((rows * gx_size, v.shape[1] * gy_size), v.dtype) for v in (qkv, proj_t, fc1, fc2_t)]
-    slots = [pltpu.VMEM((gy_size,) + v.shape, v.dtype) for v in (qkv, proj_t, fc1, fc2_t)]
-    count = 5 * (gy_size - 1) + 4 * (gx_size - 1)
-    return pl.pallas_call(
-        functools.partial(gather_kernel, sizes),
-        in_specs=[vmem_spec()] * 5,
-        out_specs=[vmem_spec()] * 5,
-        out_shape=full + [jax.ShapeDtypeStruct((gy_size,) + small.shape, small.dtype)],
-        scratch_shapes=slots + [
-            pltpu.SemaphoreType.DMA((count,)), pltpu.SemaphoreType.DMA((count,)), pltpu.SemaphoreType.DMA((2, 3)),
-        ],
-        compiler_params=pltpu.CompilerParams(collective_id=0, has_side_effects=True, vmem_limit_bytes=24 << 20),
-        name="gather_weights",
-    )(qkv, proj_t, small, fc1, fc2_t)
+    across = [push(at, False, mine + over) for at in fresh]
+    phases.append(phase(waits, None, across))
+    phases.append(phase(shared + across))
+    return phases
 
 
 def add_into(target, left, right):
     target[...] = (left[...].astype(jnp.float32) + right[...].astype(jnp.float32)).astype(target.dtype)
 
 
-def share_plane(sender, full, halves, sizes):
+def add_arrived(copies, came, kept, out=None):
+    def run():
+        for k, (copy, view) in enumerate(zip(copies, kept)):
+            copy.wait()
+            add_into(came.at[k] if out is None else out, came.at[k], view)
+
+    return run
+
+
+def share_plane(sender, full, halves, out, sizes):
     gx_size = sizes[0]
     mine = lax.axis_index("gx")
     rows = full.shape[0] // gx_size
@@ -454,7 +425,7 @@
     def block(at):
         return full.at[pl.ds(pl.multiple_of(at * rows, rows), rows), :]
 
-    held = block
+    held, act, phases = block, None, []
     count = gx_size
     for bit in range(bits_of(gx_size)):
         came = halves[bit]
@@ -472,61 +443,130 @@
             step = first_step
             last = (1 - core) * high + core * low
             away, kept = [1 - last], [last]
-        copies = [sender.start(held(at), came.at[k], "gx", mine + step) for k, at in enumerate(away)]
-        yield
-        for k, at in enumerate(kept):
-            copies[k].wait()
-            add_into(came.at[k], came.at[k], held(at))
+        copies = [sender.plan(held(at), came.at[k], "gx", mine + step) for k, at in enumerate(away)]
+        phases.append(phase((), act, copies))
+        act = add_arrived(copies, came, [held(at) for at in kept], out if count == 1 else None)
         held = (lambda ref: lambda at: ref.at[at])(came)
+    phases.append(phase((), act))
+    return phases
 
 
 def share_column(sender, total, slots, halves, out, groups, sizes):
     gy_size = sizes[1]
     row = lax.axis_index("gy")
     width = slots.shape[2] // groups
-    for i in range(gy_size):
-        for k in range(groups):
-            low = (k * gy_size + i) * width
-            slots[i, :, k * width : (k + 1) * width] = total[0, :, low : low + width]
-    held = slots
+
+    def act():
+        for i in range(gy_size):
+            for k in range(groups):
+                low = (k * gy_size + i) * width
+                slots[i, :, k * width : (k + 1) * width] = total[:, low : low + width]
+
+    held, phases = slots, []
     count = gy_size
     for bit in range(bits_of(gy_size)):
         came = halves[bit]
         count //= 2
         own = bit_of(row, bit)
         step = (1 << bit) * (1 - 2 * own)
-        copies = [sender.start(held.at[2 * k + 1 - own], came.at[k], "gy", row + step) for k in range(count)]
-        yield
-        for k in range(count):
-            copies[k].wait()
-            if count == 1:
-                add_into(out, came.at[0], held.at[own])
-            else:
-                add_into(came.at[k], came.at[k], held.at[2 * k + own])
+        copies = [sender.plan(held.at[2 * k + 1 - own], came.at[k], "gy", row + step) for k in range(count)]
+        phases.append(phase((), act, copies))
+        act = add_arrived(copies, came, [held.at[2 * k + own] for k in range(count)], out if count == 1 else None)
         held = came
+    phases.append(phase((), act))
+    return phases
 
 
 def sum_small(sender, value, came, totals, out, sizes):
-    held = value
+    held, act, phases = value, None, []
     stage = 0
     stages = bits_of(sizes[0]) + bits_of(sizes[1])
     for name, size in (("gx", sizes[0]), ("gy", sizes[1])):
         index = lax.axis_index(name)
         for bit in range(bits_of(size)):
             there = index + (1 << bit) * (1 - 2 * bit_of(index, bit))
-            copy = sender.start(held, came.at[stage], name, there)
-            yield
-            copy.wait()
+            copy = sender.plan(held, came.at[stage], name, there)
+            phases.append(phase((), act, [copy]))
             target = out if stage == stages - 1 else totals.at[stage]
-            target[...] = held[...] + came[stage]
+            act = add_small(copy, held, came, stage, target)
             held = target
             stage += 1
-
-
-def share_kernel(sizes, groups, *refs):
+    phases.append(phase((), act))
+    return phases
+
+
+def add_small(copy, held, came, stage, target):
+    def run():
+        copy.wait()
+        target[...] = held[...] + came[stage]
+
+    return run
+
+
+def gather_kernel(sizes, qkv_ref, small_ref, proj_ref, fc1_ref, fc2_ref, qkv_full, small_all, proj_rows, fc1_rows, fc2_rows,
+                  qkv_slots, proj_slots, fc1_slots, fc2_slots, qkv_rows, send, recv, own_sem, keep_sem):
+    greet(*sizes)
+    sender = Sender(send, recv)
+
+    def join_later():
+        join_rows(proj_slots, proj_rows, 1)
+        join_rows(fc1_slots, fc1_rows, 1)
+        join_rows(fc2_slots, fc2_rows, 1)
+
+    first = gather_column(
+        sender, [qkv_ref, small_ref], [qkv_slots, small_all], own_sem.at[0], sizes, lambda: join_rows(qkv_slots, qkv_rows, 3)
+    )
+    second = gather_column(
+        sender, [proj_ref, fc1_ref, fc2_ref], [proj_slots, fc1_slots, fc2_slots], own_sem.at[1], sizes, join_later
+    )
+    plane = gather_plane(sender, qkv_rows, qkv_full, keep_sem.at[0], sizes)
+    for run in first:
+        run()
+    while plane or second:
+        for queue in (plane, second):
+            if queue:
+                queue.pop(0)()
+
+
+def vmem_spec():
+    return pl.BlockSpec(memory_space=pltpu.VMEM)
+
+
+def hbm_spec():
+    return pl.BlockSpec(memory_space=pl.ANY)
+
+
+def mesh_sizes():
+    return lax.axis_size("gx"), lax.axis_size("gy")
+
+
+def gather_weights(qkv, small, proj_t, fc1, fc2_t):
+    sizes = mesh_sizes()
     gx_size, gy_size = sizes
+    rows = qkv.shape[0]
+    later = [jax.ShapeDtypeStruct((rows, v.shape[1] * gy_size), v.dtype) for v in (proj_t, fc1, fc2_t)]
+    wide = qkv.shape[1] * gy_size
+    count = 5 * (gy_size - 1) + gx_size - 1
+    return pl.pallas_call(
+        functools.partial(gather_kernel, sizes),
+        in_specs=[vmem_spec()] * 5,
+        out_specs=[hbm_spec()] + [vmem_spec()] * 4,
+        out_shape=[jax.ShapeDtypeStruct((rows * gx_size, wide), qkv.dtype), jax.ShapeDtypeStruct((gy_size,) + small.shape, small.dtype)]
+        + later,
+        scratch_shapes=[pltpu.VMEM((gy_size,) + v.shape, v.dtype) for v in (qkv, proj_t, fc1, fc2_t)]
+        + [
+            pltpu.VMEM((rows, wide), qkv.dtype),
+            pltpu.SemaphoreType.DMA((count,)), pltpu.SemaphoreType.DMA((count,)), pltpu.SemaphoreType.DMA((2, 3)),
+            pltpu.SemaphoreType.DMA((1,)),
+        ],
+        compiler_params=pltpu.CompilerParams(collective_id=0, has_side_effects=True, vmem_limit_bytes=16 << 20),
+        name="gather_weights",
+    )(qkv, small, proj_t, fc1, fc2_t)
+
+
+def share_kernel(sizes, groups, whole_count, *refs):
+    gx_bits, gy_bits = bits_of(sizes[0]), bits_of(sizes[1])
     arrays = len(groups)
-    gx_bits, gy_bits = bits_of(gx_size), bits_of(gy_size)
     refs = list(refs)
 
     def take(count):
@@ -534,53 +574,139 @@
         del refs[:count]
         return out
 
-    fulls, (small,) = take(arrays), take(1)
+    inputs, (small,) = take(arrays), take(1)
     outs, (small_out,) = take(arrays), take(1)
-    planes = [take(gx_bits) for _ in range(arrays)]
+    planes = [take(gx_bits) for _ in range(whole_count)]
+    totals = take(whole_count)
     slots = take(arrays)
     columns = [take(gy_bits) for _ in range(arrays)]
     small_came, small_totals, send, recv = take(4)
-    greet(gx_size, gy_size)
+    greet(*sizes)
     sender = Sender(send, recv)
-
-    def one(n):
-        yield from share_plane(sender, fulls[n], planes[n], sizes)
-        yield from share_column(sender, planes[n][-1], slots[n], columns[n], outs[n], groups[n], sizes)
-
-    streams = [one(n) for n in range(arrays)] + [sum_small(sender, small, small_came, small_totals, small_out, sizes)]
-    for _ in range(gx_bits + gy_bits + 1):
-        for stream in streams:
-            next(stream, None)
-
-
-def share_sums(fulls, groups, small):
-    sizes = (lax.axis_size("gx"), lax.axis_size("gy"))
+    streams = []
+    for n in range(arrays):
+        phases = share_plane(sender, inputs[n], planes[n], totals[n], sizes) if n < whole_count else []
+        total = totals[n] if n < whole_count else inputs[n]
+        phases += share_column(sender, total, slots[n], columns[n], outs[n], groups[n], sizes)
+        streams.append(phases)
+    streams.append(sum_small(sender, small, small_came, small_totals, small_out, sizes))
+    while any(streams):
+        for queue in streams:
+            if queue:
+                queue.pop(0)()
+
+
+def share_sums(fulls, rows_sums, groups, small):
+    sizes = mesh_sizes()
     gx_size, gy_size = sizes
     gx_bits, gy_bits = bits_of(gx_size), bits_of(gy_size)
     rows = fulls[0].shape[0] // gx_size
+    arrays = tuple(fulls) + tuple(rows_sums)
     planes, slots, columns = [], [], []
     for full in fulls:
-        wide = full.shape[1]
-        planes += [pltpu.VMEM((gx_size >> (bit + 1), rows, wide), full.dtype) for bit in range(gx_bits)]
-        slots.append(pltpu.VMEM((gy_size, rows, wide // gy_size), full.dtype))
-        columns += [pltpu.VMEM((gy_size >> (bit + 1), rows, wide // gy_size), full.dtype) for bit in range(gy_bits)]
+        planes += [pltpu.VMEM((gx_size >> (bit + 1), rows, full.shape[1]), full.dtype) for bit in range(gx_bits)]
+    for value in arrays:
+        wide = value.shape[1] // gy_size
+        slots.append(pltpu.VMEM((gy_size, rows, wide), value.dtype))
+        columns += [pltpu.VMEM((gy_size >> (bit + 1), rows, wide), value.dtype) for bit in range(gy_bits)]
     stages = gx_bits + gy_bits
-    count = len(fulls) * (gx_size - 1 + gy_size - 1) + stages
+    count = len(fulls) * (gx_size - 1) + len(arrays) * (gy_size - 1) + stages
     return pl.pallas_call(
-        functools.partial(share_kernel, sizes, groups),
-        in_specs=[vmem_spec()] * (len(fulls) + 1),
-        out_specs=[vmem_spec()] * (len(fulls) + 1),
-        out_shape=[jax.ShapeDtypeStruct((rows, full.shape[1] // gy_size), jnp.float32) for full in fulls]
+        functools.partial(share_kernel, sizes, groups, len(fulls)),
+        in_specs=[vmem_spec()] * (len(arrays) + 1),
+        out_specs=[vmem_spec()] * (len(arrays) + 1),
+        out_shape=[jax.ShapeDtypeStruct((rows, value.shape[1] // gy_size), jnp.float32) for value in arrays]
         + [jax.ShapeDtypeStruct(small.shape, small.dtype)],
-        scratch_shapes=planes + slots + columns + [
+        scratch_shapes=planes + [pltpu.VMEM((rows, full.shape[1]), full.dtype) for full in fulls] + slots + columns + [
             pltpu.VMEM((stages,) + small.shape, small.dtype),
             pltpu.VMEM((stages,) + small.shape, small.dtype),
             pltpu.SemaphoreType.DMA((count,)),
             pltpu.SemaphoreType.DMA((count,)),
         ],
-        compiler_params=pltpu.CompilerParams(collective_id=1, has_side_effects=True, vmem_limit_bytes=40 << 20),
+        compiler_params=pltpu.CompilerParams(collective_id=1, has_side_effects=True, vmem_limit_bytes=24 << 20),
         name="share_sums",
-    )(*fulls, small)
+    )(*arrays, small)
+
+
+def forward_stage(
+    sizes, qkv_ref, perm_ref, perm_t_ref, bias_ref, owner_ref, proj_rows, fc1_rows, fc2_rows,
+    context_ref, windows_ref, probs_ref, proj_full, fc1_full, fc2_full, ctx_ref, send, recv, keep_sem,
+):
+    image, last = pl.program_id(0), pl.num_programs(0) - 1
+
+    @pl.when(image == 0)
+    def _():
+        greet(*sizes)
+
+    sender = Sender(send, recv)
+    own = (proj_rows, fc1_rows, fc2_rows)
+    fulls = (proj_full, fc1_full, fc2_full)
+    streams = [gather_plane(sender, own[n], fulls[n], keep_sem.at[n], sizes) for n in range(3)]
+
+    @pl.when(image == 0)
+    def _():
+        for phases in streams:
+            phases[0]()
+
+    for n, phases in enumerate(streams):
+        @pl.when(image == jnp.minimum(n + 1, last))
+        def _():
+            phases[1]()
+
+    forward_kernel(
+        qkv_ref, perm_ref, perm_t_ref, bias_ref, owner_ref, context_ref, windows_ref, probs_ref, ctx_ref
+    )
+
+    @pl.when(image == last)
+    def _():
+        for place in range(2, len(streams[0])):
+            for phases in streams:
+                phases[place]()
+
+
+def backward_stage(
+    sizes, d_context_ref, windows_ref, probs_ref, perm_ref, perm_t_ref, owner_ref, d_fc1_ref, d_fc2_ref,
+    d_mixed_ref, d_bias_ref, d_qv_ref, fc1_sum, fc2_sum, d_ctx_ref, d_win_ref, *rest,
+):
+    image, last = pl.program_id(0), pl.num_programs(0) - 1
+    gx_bits = bits_of(sizes[0])
+    fc1_halves, fc2_halves, (send, recv) = rest[:gx_bits], rest[gx_bits : 2 * gx_bits], rest[2 * gx_bits :]
+
+    @pl.when(image == 0)
+    def _():
+        greet(*sizes)
+
+    sender = Sender(send, recv)
+    streams = [
+        share_plane(sender, d_fc1_ref, fc1_halves, fc1_sum, sizes),
+        share_plane(sender, d_fc2_ref, fc2_halves, fc2_sum, sizes),
+    ]
+
+    @pl.when(image == 0)
+    def _():
+        for phases in streams:
+            phases[0]()
+
+    @pl.when(image == jnp.minimum(1, last))
+    def _():
+        for phases in streams:
+            phases[1]()
+
+    @pl.when(image == last)
+    def _():
+        streams[0][2]()
+
+    backward_kernel(
+        d_context_ref, windows_ref, probs_ref, perm_ref, perm_t_ref, owner_ref,
+        d_mixed_ref, d_bias_ref, d_qv_ref, d_ctx_ref, d_win_ref,
+    )
+
+    @pl.when(image == last)
+    def _():
+        streams[1][2]()
+        for place in range(3, len(streams[0])):
+            for phases in streams:
+                phases[place]()
 
 
 def pack_rows(values):
@@ -640,8 +766,8 @@
 
     small = jnp.concatenate([fc1_bias[None], lane_row(qv_bias.reshape(1, -1)), lane_row(rel_table.T)], 0)
     small = jnp.pad(small, ((0, ROW_PAD - small.shape[0]), (0, 0)))
-    qkv_flat, proj_cols, fc1_rows, fc2_cols, small = gather_weights(
-        qkv_weight.reshape(block_rows, -1), proj_weight.T, small, fc1_weight, fc2_weight.T
+    qkv_flat, small, *later = gather_weights(
+        qkv_weight.reshape(block_rows, -1), small, proj_weight.T, fc1_weight, fc2_weight.T
     )
     fc1_bias = small[:, 0].reshape(-1)
     qv_bias = small[:, 1, : 2 * part].reshape(-1, 2, part).transpose(1, 0, 2).reshape(2, -1)
@@ -654,7 +780,7 @@
     bias_row = jnp.stack([qv_bias[0], jnp.zeros_like(qv_bias[0]), qv_bias[1]]).reshape(1, 3 * width)
     mixed = (matmul(hidden_one, qkv_flat) + bias_row.astype(jnp.float32)).astype(jnp.bfloat16)
     tables = attention_tables(rel_table, tok_local // IMAGE)
-    context, windows, probs = attend_forward(mixed, tables)
+    context, windows, probs, proj_cols, fc1_rows, fc2_cols = attend_forward(mixed, tables, later)
     resid_one = resid + (matmul_nt(context, proj_cols)) + proj_bias.astype(jnp.float32)
     normed_two, scale_two, pre_two = layer_norm(resid_one, gain_two, ln2_bias.astype(jnp.float32))
     hidden_two = (pre_two.astype(jnp.bfloat16))
@@ -682,7 +808,7 @@
     d_resid_full = (d_resid_one.astype(jnp.bfloat16))
     d_proj_weight = matmul_tn(d_resid_full, context).astype(jnp.bfloat16)
     d_context = matmul(d_resid_full, proj_cols).astype(jnp.bfloat16)
-    d_mixed, d_qv_bias, d_table = attend_backward(d_context, windows, probs, tables)
+    d_mixed, d_qv_bias, d_table, sums = attend_backward(d_context, windows, probs, tables, (d_fc1_weight, d_fc2_weight))
     d_qkv_weight = matmul_tn(hidden_one, d_mixed).astype(jnp.bfloat16)
     d_hidden_one = (matmul_nt(d_mixed, qkv_flat))
     d_ln1_gain = jnp.sum(d_hidden_one * normed_one, 0)
@@ -691,8 +817,8 @@
         jnp.bfloat16
     )
     own = (d_ln1_gain, d_ln1_bias, d_proj_bias, d_ln2_gain, d_ln2_bias, d_fc2_bias, d_qv_bias, d_table, d_fc1_bias)
-    d_fc1_weight, d_fc2_weight, d_qkv_weight, d_proj_weight, sums = share_sums(
-        (d_fc1_weight, d_fc2_weight, d_qkv_weight, d_proj_weight), (1, 1, 3, 1), pack_rows(own)
+    d_qkv_weight, d_proj_weight, d_fc1_weight, d_fc2_weight, sums = share_sums(
+        (d_qkv_weight, d_proj_weight), sums, (3, 1, 1, 1), pack_rows(own)
     )
     d_fc2_weight = d_fc2_weight.T
     d_proj_weight = d_proj_weight.T

time: 209 us -> 189 us (0.904)
  Pallas kernels: 128 us -> 112 us
  matrix products: 44.5 us -> 41.3 us
    pallas_call x1, Pallas kernels: 51.5 us -> 28.1 us  [gather_weights(): pl.pallas_call(functools.partial(gather_kernel, sizes), in_specs=[vmem_sp...]
    pallas_call x3, Pallas kernels: 76.6 us -> 83.8 us  [the longest x1 28.2 us: attend_backward(): pl.pallas_call(functools.partial(backward_stage, sizes), grid=(count,), i...]
    unnamed x81 -> x99, local copies, waits for them, and re-layouts: 10.5 us -> 15.1 us
    reshape x3, local copies, waits for them, and re-layouts: 4.13 us -> 0.43 us  [attend_backward(): d_bias.reshape(groups, SLOT, PACK, SLOT).transpose(0, 2, 1, 3)]
    dot_general x4, matrix products: 11.6 us -> 9.3 us  [matmul_tn(): lax.dot_general(left, right, (((0,), (0,)), ((), ())), preferred_element_...]
    dot_general x4, matrix products: 12.7 us -> 10.5 us  [matmul_nt(): lax.dot_general(left, right, (((1,), (1,)), ((), ())), preferred_element_...]
where the time goes in v1:
time: 189 us; the launch traced here: 188 us
  Pallas kernels  112 us (59%)
  matrix products  41.3 us (22%)
  local copies, waits for them, and re-layouts  22.9 us (12%)
  other arithmetic  10 us (5%)
  between operations  2.02 us (1%)
    pallas_call x1, Pallas kernels, attend_backward(): pl.pallas_call(functools.partial(backward_stage, sizes), grid=(count,), i...  28.2 us
    pallas_call x1, Pallas kernels, gather_weights(): pl.pallas_call(functools.partial(gather_kernel, sizes), in_specs=[vmem_sp...  28.1 us
    pallas_call x1, Pallas kernels, attend_forward(): pl.pallas_call(functools.partial(forward_stage, sizes), grid=(count,), in...  28 us
    pallas_call x1, Pallas kernels, share_sums(): pl.pallas_call(functools.partial(share_kernel, sizes, groups, len(fulls))...  27.6 us
    dot_general x4, matrix products, matmul(): return jnp.dot(left, right, preferred_element_type=jnp.float32)  18.3 us
    unnamed x99, local copies, waits for them, and re-layouts  15.1 us
    dot_general x4, matrix products, matmul_nt(): lax.dot_general(left, right, (((1,), (1,)), ((), ())), preferred_element_...  10.5 us
    dot_general x4, matrix products, matmul_tn(): lax.dot_general(left, right, (((0,), (0,)), ((), ())), preferred_element_...  9.3 us

profile of v1, /device:TPU:0, one launch (start us, length us, event | category | flops | bytes accessed | tf_op | source)
XLA Modules:
  0.0 188.1 jit_solution(6699934981159265324)
XLA Ops:
  0.7 0.8 copy-done
  1.5 0.7 broadcast_in_dim.9
  2.1 0.7 copy.61
  2.8 0.7 fusion.31
  3.5 0.8 copy-done.1
  4.4 0.8 copy-done.2
  5.2 0.7 copy-done.3
  5.9 28.1 %gather_weights.1 = (bf16[512,1536]{1,0:T(8,128)(2,1)S(1)}, bf16[4,16,512]{2,1,0:T(8,128)(2,1)S(1)}, bf16[64,512]{1,0:T(8,128)(2,1)S(1)}, bf16[64,2048]{1,0:T(8,128)(2,1)S(1)}, bf16[64,2048]{1,0:T(8,128)(2,1)S(1)}) custom-call(bf16[64,384]{1,0:T(8,128)(2,1)S(1)} %copy_bitcast_fusion.2.qkv_ref, bf16[16,512]{1,0:T(8,128)(2,1)S(1)} %pad.37.small_ref, ...), custom_call_target="tpu_custom_call" | custom-call | tf_op jit(solution)/shard_map/gather_weights/pallas_call | solution.py:550
  34.2 1.5 convert_reduce_fusion
  35.7 0.7 convert_element_type.111
  36.4 0.7 convert_element_type.112
  37.1 4.1 %add_convert_fusion.qkv_ref = bf16[784,1536]{1,0:T(8,128)(2,1)} fusion(bf16[512,1536]{1,0:T(8,128)(2,1)S(1)} %get-tuple-element.36, f32[1536]{0:T(1024)S(1)} %reshape.243, bf16[784,512]{1,0:T(8,128)(2,1)} %param.21, f32[512]{0:T(512)S(1)} %convert_element_type.112, f32[512]{0:T(512)S(1)} %convert_element_type.111, f32[784]{0:T(1024)S(1)} %get-tuple-element.111, ...), kind=kOutput, calls=%fused_computation.8 | convolution fusion | flops 1237942272 | bytes 4800640 | tf_op jit(solution)/shard_map/dot_general | solution.py:24
  41.3 0.7 iota_compare_fusion
  42.0 1.7 convolution_bitcast_fusion
  43.7 1.9 %add.154 = f32[2,64,512]{2,1,0:T(8,128)} reshape(f32[2,64,8,64]{3,2,1,0:T(8,128)} %convolution_bitcast_fusion) | data formatting | bytes 524288 | tf_op jit(solution)/shard_map/add | solution.py:86
  45.7 1.1 add.156
  46.7 1.5 add.157
  48.3 1.2 broadcast_add_fusion.bias_ref
  49.5 1.7 copy-done.17
  51.2 28.0 %attend_forward.1 = (bf16[784,512]{1,0:T(8,128)(2,1)S(1)}, bf16[4,256,1536]{2,1,0:T(8,128)(2,1)S(1)}, f32[4,8,64,512]{3,2,1,0:T(8,128)S(1)}, bf16[512,512]{1,0:T...) custom-call(bf16[784,1536]{1,0:T(8,128)(2,1)S(1)} %copy-done.17, ...), custom_call_target="tpu_custom_call" | custom-call | flops 6000000000 | bytes 24000000 | tf_op jit(solution)/shard_map/attend_forward/pallas_call | solution.py:195
  79.1 1.3 copy-done.15
  80.5 2.1 %copy-done.18 = f32[4,8,64,512]{3,2,1,0:T(8,128)} copy-done((f32[4,8,64,512]{3,2,1,0:T(8,128)}, f32[4,8,64,512]{3,2,1,0:T(8,128)S(1)}, u32[]{:S(2)}) %copy-start.18) | copy-done | bytes 4194328
  82.5 1.6 copy-done.19
  84.2 0.9 fusion.41
  85.2 0.6 copy-done.11
  85.7 5.6 %multiply_convert_fusion = (bf16[784,2048]{1,0:T(8,128)(2,1)}, f32[784,2048]{1,0:T(8,128)}) fusion(f32[2048]{0:T(1024)S(1)} %bitcast.109, bf16[512,2048]{1,0:T(8,128)(2,1)S(1)} %get-tuple-element.43, f32[784,512]{1,0:T(8,128)S(1)} %get-tuple-element.114, f32[512]{0:T(512)S(1)} %convert_element_type.122, f32[512]{0:T(512)S(1)} %convert_element_type.121, ...), kind=kOutput, calls=%fused_computation.6 | convolution fusion | flops 1655808000 | bytes 13355136 | tf_op jit(solution)/shard_map/dot_general | solution.py:24
  92.0 8.0 %fusion.43 = (f32[2048]{0:T(1024)}, bf16[784,2048]{1,0:T(8,128)(2,1)S(1)}) fusion(f32[784,2048]{1,0:T(8,128)} %get-tuple-element.116, f32[2048]{0:T(1024)} %bitcast.110, bf16[512,2048]{1,0:T(8,128)(2,1)} %copy-done.15, bf16[784,512]{1,0:T(8,128)(2,1)S(1)} %copy-done.27, pred[784]{0:T(1024)(128)(4,1)S(1)} %fusion.34), kind=kOutput, calls=%fused_computation.113 | convolution fusion | flops 1663834112 | bytes 12550928 | tf_op jit(solution)/shard_map/dot_general | solution.py:24
  100.0 2.6 %convolution_convert_fusion.1.d_fc1_ref = bf16[512,2048]{1,0:T(8,128)(2,1)S(1)} fusion(bf16[784,2048]{1,0:T(8,128)(2,1)S(1)} %get-tuple-element.120, f32[784,512]{1,0:T(8,128)S(1)} %copy-done.22, f32[512]{0:T(512)S(1)} %convert_element_type.122, f32[512]{0:T(512)S(1)} %convert_element_type.121, f32[784]{0:T(1024)S(1)} %get-tuple-element.109, ...), kind=kOutput, calls=%fused_computation.11 | convolution fusion | flops 1647222784 | bytes 6924416 | tf_op jit(solution)/shard_map/dot_general | solution.py:28
  102.6 2.3 %multiply_reduce_fusion = (f32[512]{0:T(512)S(1)}, f32[784]{0:T(1024)S(1)}, f32[784]{0:T(1024)S(1)}, f32[512]{0:T(512)S(1)}, f32[784,512]{1,0:T(8,128)S(1)}) fusion(f32[784,512]{1,0:T(8,128)S(1)} %copy-done.22, f32[784]{0:T(1024)S(1)} %get-tuple-element.109, f32[784]{0:T(1024)S(1)} %get-tuple-element.108, f32[512]{0:T(512)S(1)} %convert_element_type.121, ...), kind=kOutput, calls=%fused_computation.36 | convolution fusion | flops 1647777280 | bytes 8538368 | tf_op jit(solution)/shard_map/dot_general | solution.py:34
  104.9 0.9 fusion.42
  105.9 0.6 convolution_convert_fusion.3.d_context_ref
  106.8 2.5 %convolution_convert_fusion.d_fc2_ref = bf16[512,2048]{1,0:T(8,128)(2,1)S(1)} fusion(bf16[784,2048]{1,0:T(8,128)(2,1)S(1)} %copy-done.41, bf16[784,512]{1,0:T(8,128)(2,1)S(1)} %copy-done.27, pred[784]{0:T(1024)(128)(4,1)S(1)} %fusion.34), kind=kOutput, calls=%fused_computation.10 | convolution fusion | flops 1645617152 | bytes 6112016 | tf_op jit(solution)/shard_map/dot_general | solution.py:28
  109.4 28.2 %attend_backward.1 = (bf16[784,1536]{1,0:T(8,128)(2,1)S(1)}, f32[2,64,512]{2,1,0:T(8,128)S(1)}, f32[2,512]{1,0:T(2,128)S(1)}, bf16[64,2048]{1,0:T(8,128)(2,1)S(1)}, bf16[64,2048]{1,0:T(8,128)(2,1)S(1)}) custom-call(bf16[784,512]{1,0:T(8,128)(2,1)S(1)} %convolution_convert_fusion.3.d_context_ref, bf16[4,256,1536]{2,1,0:T(8,128)(2,1)} %copy-done.19, ...), custom_call_target="tpu_custom_call" | custom-call | flops 8999999488 | bytes 32000000 | tf_op jit(solution)/shard_map/attend_backward/pallas_call | solution.py:231
  137.6 2.7 %fusion.18 = (f32[512]{0:T(512)S(1)}, f32[784]{0:T(1024)S(1)}, f32[784]{0:T(1024)S(1)}, f32[512]{0:T(512)S(1)}, f32[784,512]{1,0:T(8,128)}) fusion(bf16[784,512]{1,0:T(8,128)(2,1)S(1)} %copy-done.25, f32[784]{0:T(1024)S(1)} %get-tuple-element.111, f32[784]{0:T(1024)S(1)} %get-tuple-element.110, f32[512]{0:T(512)S(1)} %copy-done.32, ...), kind=kOutput, calls=%fused_computation.33 | convolution fusion | flops 1237136896 | bytes 6408448 | tf_op jit(solution)/shard_map/dot_general | solution.py:34
  141.1 1.4 fusion.5
  142.6 2.3 %convolution_convert_fusion.4.refs_1_ = bf16[512,512]{1,0:T(8,128)(2,1)S(1)} fusion(bf16[784,512]{1,0:T(8,128)(2,1)S(1)} %copy-done.10, f32[784,512]{1,0:T(8,128)} %copy-done.20), kind=kOutput, calls=%fused_computation.49 | convolution fusion | flops 411705344 | bytes 2932736 | tf_op jit(solution)/shard_map/dot_general | solution.py:28
  145.0 2.0 %convolution_convert_fusion.2.refs_0_ = bf16[512,1536]{1,0:T(8,128)(2,1)S(1)} fusion(bf16[784,1536]{1,0:T(8,128)(2,1)S(1)} %copy-done.14, bf16[784,512]{1,0:T(8,128)(2,1)S(1)} %copy-done.26, f32[512]{0:T(512)S(1)} %copy-done.36, f32[512]{0:T(512)S(1)} %copy-done.32, f32[784]{0:T(1024)S(1)} %get-tuple-element.111, f32[784]{0:T(1024)S(1)} %get-tuple-element.110), kind=kOutput, calls=%fused_computation.12 | convolution fusion | flops 1236320256 | bytes 4794496 | tf_op jit(solution)/shard_map/dot_general | solution.py:28
  146.9 27.6 %share_sums.1 = (f32[64,384]{1,0:T(8,128)S(1)}, f32[64,128]{1,0:T(8,128)S(1)}, f32[64,512]{1,0:T(8,128)S(1)}, f32[64,512]{1,0:T(8,128)S(1)}, f32[96,128]{1,0:T(8,128)S(1)}) custom-call(bf16[512,1536]{1,0:T(8,128)(2,1)S(1)} %convolution_convert_fusion.2.refs_0_, bf16[512,512]{1,0:T(8,128)(2,1)S(1)} %convolution_convert_fusion.4.refs_1_, ...), custom_call_target="tpu_custom_call" | custom-call | tf_op jit(solution)/shard_map/share_sums/pallas_call | solution.py:614
  174.7 0.7 copy.44
  175.4 0.6 copy_bitcast_fusion.1
  176.1 0.7 dynamic_slice.11
  176.7 0.6 constant_dynamic-slice_fusion.1
  177.3 0.6 slice_bitcast_fusion.1
  177.9 3.5 %fusion.17 = bf16[784,512]{1,0:T(8,128)(2,1)} fusion(f32[784,512]{1,0:T(8,128)} %copy-done.20, bf16[784,512]{1,0:T(8,128)(2,1)S(1)} %copy-done.26, f32[784,512]{1,0:T(8,128)} %get-tuple-element.118, f32[784]{0:T(1024)S(1)} %broadcast_multiply_fusion, f32[784]{0:T(1024)S(1)} %broadcast_multiply_fusion.1, f32[512]{0:T(512)S(1)} %copy-done.32, ...), kind=kLoop, calls=%fused_computation.32 | loop fusion | flops 4014080 | bytes 4831488 | tf_op jit(solution)/shard_map/convert_element_type | solution.py:816
  181.5 4.7 %add_convert_fusion.1 = bf16[784,512]{1,0:T(8,128)(2,1)} fusion(f32[784,512]{1,0:T(8,128)S(1)} %copy-done.23, bf16[784,2048]{1,0:T(8,128)(2,1)} %get-tuple-element.115, bf16[512,2048]{1,0:T(8,128)(2,1)S(1)} %copy-done.16, f32[512]{0:T(512)S(1)} %convert_element_type.127), kind=kOutput, calls=%fused_computation.41 | convolution fusion | flops 1645371392 | bytes 7718912 | tf_op jit(solution)/shard_map/dot_general | solution.py:34
  186.1 0.6 copy.76
  186.7 0.7 copy.77
  187.4 0.7 copy.78
  (119 shorter events, 1.7 us)
Async XLA Ops:
  0.6 0.8 copy-start
  3.5 0.8 copy-start.1
  4.4 0.8 copy-start.2
  5.2 0.7 copy-start.3
  36.4 4.8 %copy-start.31 = (f32[512]{0:T(512)}, f32[512]{0:T(512)S(1)}, u32[]{:S(2)}) copy-start(f32[512]{0:T(512)S(1)} %convert_element_type.111) | copy-start | bytes 6148
  37.1 4.1 %copy-start.35 = (f32[512]{0:T(512)}, f32[512]{0:T(512)S(1)}, u32[]{:S(2)}) copy-start(f32[512]{0:T(512)S(1)} %convert_element_type.112) | copy-start | bytes 6148
  37.1 4.2 %copy-start.29 = (s32[4096]{0:T(1024)S(1)}, s32[4096]{0:T(1024)}, u32[]{:S(2)}) copy-start(s32[4096]{0:T(1024)} %constant.95) | copy-start | bytes 49156
  41.3 4.4 %copy-start.28 = (f32[4,64,64]{2,1,0:T(8,128)S(1)}, f32[4,64,64]{2,1,0:T(8,128)}, u32[]{:S(2)}) copy-start(f32[4,64,64]{2,1,0:T(8,128)} %constant.68.clone) | copy-start | bytes 196612
  46.7 2.7 %copy-start.4 = (bf16[4,256,208]{2,1,0:T(8,128)(2,1)S(1)}, bf16[4,256,208]{2,1,0:T(8,128)(2,1)}, u32[]{:S(2)}) copy-start(bf16[4,256,208]{2,1,0:T(8,128)(2,1)} %constant.93.perm_ref) | copy-start | bytes 1277956
  48.3 1.2 copy-start.5
  48.3 1.2 copy-start.7
  49.5 1.7 copy-start.17
  51.2 33.0 %copy-start.37 = (bf16[512]{0:T(512)(128)(2,1)S(1)}, bf16[512]{0:T(512)(128)(2,1)}, u32[]{:S(2)}) copy-start(bf16[512]{0:T(512)(128)(2,1)} %param.30) | copy-start | bytes 3076
  51.2 33.0 %copy-start.24 = (bf16[784,512]{1,0:T(8,128)(2,1)S(1)}, bf16[784,512]{1,0:T(8,128)(2,1)}, u32[]{:S(2)}) copy-start(bf16[784,512]{1,0:T(8,128)(2,1)} %param.21) | copy-start | bytes 2408452
  79.1 1.3 copy-start.15
  80.5 2.1 %copy-start.18 = (f32[4,8,64,512]{3,2,1,0:T(8,128)}, f32[4,8,64,512]{3,2,1,0:T(8,128)S(1)}, u32[]{:S(2)}) copy-start(f32[4,8,64,512]{3,2,1,0:T(8,128)S(1)} %get-tuple-element.46.probs_ref) | copy-start | bytes 12582916
  82.5 1.6 copy-start.19
  84.2 0.9 copy-start.9
  84.2 1.6 copy-start.11
  84.2 0.9 copy-start.38
  84.2 0.9 copy-start.39
  85.1 6.2 %copy-start.21 = (f32[784,512]{1,0:T(8,128)}, f32[784,512]{1,0:T(8,128)S(1)}, u32[]{:S(2)}) copy-start(f32[784,512]{1,0:T(8,128)S(1)} %get-tuple-element.114) | copy-start | bytes 4816900
  85.1 6.2 %copy-start.34 = (f32[4,1,512]{2,1,0:T(1,128)}, f32[4,1,512]{2,1,0:T(1,128)S(1)}, u32[]{:S(2)}) copy-start(f32[4,1,512]{2,1,0:T(1,128)S(1)} %slice_convert_fusion) | copy-start | bytes 24580
  85.7 6.2 %copy-start.27 = (bf16[784,512]{1,0:T(8,128)(2,1)S(1)}, bf16[784,512]{1,0:T(8,128)(2,1)}, u32[]{:S(2)}) copy-start(bf16[784,512]{1,0:T(8,128)(2,1)} %param.22) | copy-start | bytes 2408452
  92.0 8.1 %copy-start.22 = (f32[784,512]{1,0:T(8,128)S(1)}, f32[784,512]{1,0:T(8,128)}, u32[]{:S(2)}) copy-start(f32[784,512]{1,0:T(8,128)} %copy-done.21) | copy-start | bytes 4816900
  100.0 2.6 %copy-start.12 = (bf16[512,2048]{1,0:T(8,128)(2,1)S(1)}, bf16[512,2048]{1,0:T(8,128)(2,1)}, u32[]{:S(2)}) copy-start(bf16[512,2048]{1,0:T(8,128)(2,1)} %copy-done.11) | copy-start | bytes 6291460
  104.9 1.9 %copy-start.41 = (bf16[784,2048]{1,0:T(8,128)(2,1)S(1)}, bf16[784,2048]{1,0:T(8,128)(2,1)}, u32[]{:S(2)}) copy-start(bf16[784,2048]{1,0:T(8,128)(2,1)} %get-tuple-element.115) | copy-start | bytes 9633796
  105.9 3.4 %copy-start.20 = (f32[784,512]{1,0:T(8,128)}, f32[784,512]{1,0:T(8,128)S(1)}, u32[]{:S(2)}) copy-start(f32[784,512]{1,0:T(8,128)S(1)} %get-tuple-element.100) | copy-start | bytes 4816900
  106.8 2.5 %copy-start.6 = (bf16[4,208,256]{2,1,0:T(8,128)(2,1)S(1)}, bf16[4,208,256]{2,1,0:T(8,128)(2,1)}, u32[]{:S(2)}) copy-start(bf16[4,208,256]{2,1,0:T(8,128)(2,1)} %constant.94.perm_t_ref) | copy-start | bytes 1277956
  106.8 2.5 %copy-start.8 = (bf16[512,256]{1,0:T(8,128)(2,1)S(1)}, bf16[512,256]{1,0:T(8,128)(2,1)}, u32[]{:S(2)}) copy-start(bf16[512,256]{1,0:T(8,128)(2,1)} %constant.96.owner_ref) | copy-start | bytes 786436
  109.3 28.3 %copy-start.25 = (bf16[784,512]{1,0:T(8,128)(2,1)S(1)}, bf16[784,512]{1,0:T(8,128)(2,1)}, u32[]{:S(2)}) copy-start(bf16[784,512]{1,0:T(8,128)(2,1)} %param.21) | copy-start | bytes 2408452
  109.3 28.3 %copy-start.32 = (f32[512]{0:T(512)S(1)}, f32[512]{0:T(512)}, u32[]{:S(2)}) copy-start(f32[512]{0:T(512)} %copy-done.31) | copy-start | bytes 6148
  137.6 2.8 %copy-start.13 = (bf16[784,1536]{1,0:T(8,128)(2,1)}, bf16[784,1536]{1,0:T(8,128)(2,1)S(1)}, u32[]{:S(2)}) copy-start(bf16[784,1536]{1,0:T(8,128)(2,1)S(1)} %get-tuple-element.47) | copy-start | bytes 7225348
  140.3 0.7 copy-start.30
  140.6 2.0 %copy-start.33 = (f32[2048]{0:T(1024)S(1)}, f32[2048]{0:T(1024)}, u32[]{:S(2)}) copy-start(f32[2048]{0:T(1024)} %get-tuple-element.119) | copy-start | bytes 24580
  140.6 2.0 %copy-start.10 = (bf16[784,512]{1,0:T(8,128)(2,1)S(1)}, bf16[784,512]{1,0:T(8,128)(2,1)}, u32[]{:S(2)}) copy-start(bf16[784,512]{1,0:T(8,128)(2,1)} %copy-done.9) | copy-start | bytes 2408452
  141.1 3.9 %copy-start.26 = (bf16[784,512]{1,0:T(8,128)(2,1)S(1)}, bf16[784,512]{1,0:T(8,128)(2,1)}, u32[]{:S(2)}) copy-start(bf16[784,512]{1,0:T(8,128)(2,1)} %param.21) | copy-start | bytes 2408452
  142.5 2.5 %copy-start.36 = (f32[512]{0:T(512)S(1)}, f32[512]{0:T(512)}, u32[]{:S(2)}) copy-start(f32[512]{0:T(512)} %copy-done.35) | copy-start | bytes 6148
  142.6 2.4 %copy-start.14 = (bf16[784,1536]{1,0:T(8,128)(2,1)S(1)}, bf16[784,1536]{1,0:T(8,128)(2,1)}, u32[]{:S(2)}) copy-start(bf16[784,1536]{1,0:T(8,128)(2,1)} %copy-done.13) | copy-start | bytes 7225348
  177.9 3.5 %copy-start.40 = (bf16[512]{0:T(512)(128)(2,1)S(1)}, bf16[512]{0:T(512)(128)(2,1)}, u32[]{:S(2)}) copy-start(bf16[512]{0:T(512)(128)(2,1)} %param.36) | copy-start | bytes 3076
  177.9 3.5 %copy-start.16 = (bf16[512,2048]{1,0:T(8,128)(2,1)S(1)}, bf16[512,2048]{1,0:T(8,128)(2,1)}, u32[]{:S(2)}) copy-start(bf16[512,2048]{1,0:T(8,128)(2,1)} %copy-done.15) | copy-start | bytes 6291460
  177.9 3.5 %copy-start.23 = (f32[784,512]{1,0:T(8,128)S(1)}, f32[784,512]{1,0:T(8,128)}, u32[]{:S(2)}) copy-start(f32[784,512]{1,0:T(8,128)} %copy-done.21) | copy-start | bytes 4816900

commit v2 on v1

--- a/solution.py
+++ b/solution.py
@@ -70,24 +70,15 @@
     return column.astype(np.int32), rel.astype(np.int32), mask.astype(np.float32)
 
 
-def attention_tables(rel_table, image_count):
-    column, rel, mask = static_tables(image_count)
+def attention_tables(image_count):
+    column, rel, _ = static_tables(image_count)
     spots = np.arange(SPAN, dtype=np.int32)
     perm = jnp.asarray((column[:, :, None] == spots).astype(np.float32)).astype(jnp.bfloat16)
     perm_t = jnp.asarray((column[:, None, :] == spots[:, None]).astype(np.float32)).astype(jnp.bfloat16)
-    heads = rel_table.shape[0]
-    onehot = (jnp.arange(RELS, dtype=jnp.int32)[:, None] == jnp.asarray(rel.reshape(1, -1))).astype(
-        jnp.bfloat16
-    )
-    bias = lax.dot_general(
-        rel_table, onehot, (((1,), (0,)), ((), ())), preferred_element_type=jnp.float32
-    )
-    bias = bias.reshape(heads // PACK, PACK, SLOT, SLOT).transpose(0, 2, 1, 3)
-    bias = bias[None] + jnp.asarray(mask)[:, None, :, None, :]
-    bias = bias.reshape(WIN_COUNT, heads // PACK, SLOT, PACK * SLOT)
+    onehot = (jnp.arange(RELS, dtype=jnp.int32)[:, None] == jnp.asarray(rel.reshape(1, -1))).astype(jnp.bfloat16)
     owner = np.arange(PACK * SLOT)[:, None] // SLOT == np.arange(PACK * HD)[None, :] // HD
     owner = jnp.asarray(owner.astype(np.float32)).astype(jnp.bfloat16)
-    return perm, perm_t, bias, owner, onehot
+    return perm, perm_t, owner, onehot
 
 
 def spread(rows, owner):
@@ -184,14 +175,16 @@
     return pl.BlockSpec((1,) + shape, lambda n: (n,) + (0,) * len(shape))
 
 
-def attend_forward(qkv, tables, later):
-    perm, perm_t, bias, owner, _ = tables
+def attend_forward(qkv, tables, bias, later):
+    perm, perm_t, owner, _ = tables
     tok, wide = qkv.shape
     width = wide // 3
     count, spots = perm.shape[:2]
     tiles = WIN_COUNT * width // (PACK * HD)
     sizes = mesh_sizes()
-    copies = len(later) * (sizes[0] - 1)
+    copies = len(later) * (sizes[0] - 1) + sizes[1] - 1
+    proj_rows, fc1_rows, fc2_local = later
+    shapes = [(rows.shape[0] * sizes[0], columns) for rows, columns in zip(later, (proj_rows.shape[1], fc1_rows.shape[1], fc2_local.shape[1] * sizes[1]))]
     return pl.pallas_call(
         functools.partial(forward_stage, sizes),
         grid=(count,),
@@ -200,24 +193,27 @@
         out_specs=[whole((tok, width)), per_image((spots, wide)), per_image((tiles, SLOT, PACK * SLOT))] + [hbm_spec()] * len(later),
         out_shape=[
             jax.ShapeDtypeStruct((tok, width), jnp.bfloat16),
-            jax.ShapeDtypeStruct((count, spots, wide), jnp.bfloat16),
-            jax.ShapeDtypeStruct((count, tiles, SLOT, PACK * SLOT), jnp.float32),
+            pltpu.HBM((count, spots, wide), jnp.bfloat16),
+            pltpu.HBM((count, tiles, SLOT, PACK * SLOT), jnp.float32),
         ]
-        + [jax.ShapeDtypeStruct((rows.shape[0] * sizes[0], rows.shape[1]), rows.dtype) for rows in later],
+        + [jax.ShapeDtypeStruct(shape, jnp.bfloat16) for shape in shapes],
         scratch_shapes=[
             pltpu.VMEM((spots, width), jnp.bfloat16),
+            pltpu.VMEM((sizes[1],) + later[2].shape, jnp.bfloat16),
+            pltpu.VMEM((later[2].shape[0], later[2].shape[1] * sizes[1]), jnp.bfloat16),
             pltpu.SemaphoreType.DMA((copies,)),
             pltpu.SemaphoreType.DMA((copies,)),
             pltpu.SemaphoreType.DMA((len(later),)),
+            pltpu.SemaphoreType.DMA((1,)),
         ],
-        compiler_params=pltpu.CompilerParams(collective_id=2, has_side_effects=True, vmem_limit_bytes=32 << 20),
+        compiler_params=pltpu.CompilerParams(collective_id=2, has_side_effects=True, vmem_limit_bytes=FWD_GRANT),
         cost_estimate=pl.CostEstimate(flops=6_000_000_000, bytes_accessed=24_000_000, transcendentals=tok * width * 2),
         name="attend_forward",
     )(qkv, perm, perm_t, bias, owner, *later)
 
 
 def attend_backward(d_context, windows, probs, tables, sums):
-    perm, perm_t, _, owner, onehot = tables
+    perm, perm_t, owner, onehot = tables
     tok, width = d_context.shape
     count, spots, wide = windows.shape
     groups = width // (PACK * HD)
@@ -246,7 +242,7 @@
         scratch_shapes=[pltpu.VMEM((spots, width), jnp.bfloat16), pltpu.VMEM((spots, wide), jnp.bfloat16)]
         + halves
         + [pltpu.SemaphoreType.DMA((copies,)), pltpu.SemaphoreType.DMA((copies,))],
-        compiler_params=pltpu.CompilerParams(collective_id=3, has_side_effects=True, vmem_limit_bytes=44 << 20),
+        compiler_params=pltpu.CompilerParams(collective_id=3, has_side_effects=True, vmem_limit_bytes=BWD_GRANT),
         cost_estimate=pl.CostEstimate(flops=9_000_000_000, bytes_accessed=32_000_000, transcendentals=0),
         name="attend_backward",
     )(d_context, windows, probs, perm, perm_t, owner, *sums)
@@ -283,6 +279,8 @@
 
 
 ROW_PAD = 16
+FWD_GRANT = 16 << 20
+BWD_GRANT = 24 << 20
 
 
 def bit_of(index, bit):
@@ -296,11 +294,13 @@
 def greet(gx_size, gy_size):
     mine, row = lax.axis_index("gx"), lax.axis_index("gy")
     barrier = pltpu.get_barrier_semaphore()
-    for name, index, size in (("gx", mine, gx_size), ("gy", row, gy_size)):
-        for bit in range(bits_of(size)):
-            there = index + (1 << bit) * (1 - 2 * bit_of(index, bit))
-            pl.semaphore_signal(barrier, inc=1, device_id={name: there}, device_id_type=pl.DeviceIdType.MESH)
-    pl.semaphore_wait(barrier, bits_of(gx_size) + bits_of(gy_size))
+    for bit in range(bits_of(gx_size)):
+        there = mine + (1 << bit) * (1 - 2 * bit_of(mine, bit))
+        pl.semaphore_signal(barrier, inc=1, device_id={"gx": there}, device_id_type=pl.DeviceIdType.MESH)
+    for away in range(1, gy_size):
+        there = (row + away) % gy_size
+        pl.semaphore_signal(barrier, inc=1, device_id={"gy": there}, device_id_type=pl.DeviceIdType.MESH)
+    pl.semaphore_wait(barrier, bits_of(gx_size) + gy_size - 1)
 
 
 class Sender:
@@ -345,20 +345,12 @@
 def gather_column(sender, local, slots, sem, sizes, act=None):
     row = lax.axis_index("gy")
     own = [pltpu.make_async_copy(ref, slot.at[row], sem.at[n]) for n, (ref, slot) in enumerate(zip(local, slots))]
-    waits, starts, phases = [], list(own), []
-    held = [row]
-    for bit in range(bits_of(sizes[1]))[::-1]:
-        step = (1 << bit) * (1 - 2 * bit_of(row, bit))
-        copies = [
-            sender.plan(local[n] if place == 0 else slot.at[at], slot.at[at], "gy", row + step)
-            for place, at in enumerate(held)
-            for n, slot in enumerate(slots)
-        ]
-        phases.append(phase(waits, None, starts + copies))
-        waits, starts = copies, []
-        held = held + [at + step for at in held]
-    phases.append(phase(waits + own, act))
-    return phases
+    copies = [
+        sender.plan(ref, slot.at[row], "gy", (row + away) % sizes[1])
+        for ref, slot in zip(local, slots)
+        for away in range(1, sizes[1])
+    ]
+    return [phase((), None, own + copies), phase(own + copies, act)]
 
 
 def join_rows(slots, rows_ref, groups):
@@ -451,47 +443,52 @@
     return phases
 
 
-def share_column(sender, total, slots, halves, out, groups, sizes):
+def share_column(sender, total, slots, came, out, groups, sizes):
     gy_size = sizes[1]
     row = lax.axis_index("gy")
     width = slots.shape[2] // groups
 
-    def act():
+    def split():
         for i in range(gy_size):
             for k in range(groups):
                 low = (k * gy_size + i) * width
                 slots[i, :, k * width : (k + 1) * width] = total[:, low : low + width]
 
-    held, phases = slots, []
-    count = gy_size
-    for bit in range(bits_of(gy_size)):
-        came = halves[bit]
-        count //= 2
-        own = bit_of(row, bit)
-        step = (1 << bit) * (1 - 2 * own)
-        copies = [sender.plan(held.at[2 * k + 1 - own], came.at[k], "gy", row + step) for k in range(count)]
-        phases.append(phase((), act, copies))
-        act = add_arrived(copies, came, [held.at[2 * k + own] for k in range(count)], out if count == 1 else None)
-        held = came
-    phases.append(phase((), act))
-    return phases
-
-
-def sum_small(sender, value, came, totals, out, sizes):
+    targets = [(row + away) % gy_size for away in range(1, gy_size)]
+    copies = [sender.plan(slots.at[there], came.at[n], "gy", there) for n, there in enumerate(targets)]
+
+    def finish():
+        total = slots[row].astype(jnp.float32)
+        for n, copy in enumerate(copies):
+            copy.wait()
+            total = total + came[n].astype(jnp.float32)
+        out[...] = total
+
+    return [phase((), split, copies), phase((), finish)]
+
+
+def sum_small(sender, value, came, totals, column, out, sizes):
     held, act, phases = value, None, []
-    stage = 0
-    stages = bits_of(sizes[0]) + bits_of(sizes[1])
-    for name, size in (("gx", sizes[0]), ("gy", sizes[1])):
-        index = lax.axis_index(name)
-        for bit in range(bits_of(size)):
-            there = index + (1 << bit) * (1 - 2 * bit_of(index, bit))
-            copy = sender.plan(held, came.at[stage], name, there)
-            phases.append(phase((), act, [copy]))
-            target = out if stage == stages - 1 else totals.at[stage]
-            act = add_small(copy, held, came, stage, target)
-            held = target
-            stage += 1
-    phases.append(phase((), act))
+    mine, row = lax.axis_index("gx"), lax.axis_index("gy")
+    for bit in range(bits_of(sizes[0])):
+        there = mine + (1 << bit) * (1 - 2 * bit_of(mine, bit))
+        copy = sender.plan(held, came.at[bit], "gx", there)
+        phases.append(phase((), act, [copy]))
+        act = add_small(copy, held, came, bit, totals.at[bit])
+        held = totals.at[bit]
+    copies = [sender.plan(held, column.at[row], "gy", (row + away) % sizes[1]) for away in range(1, sizes[1])]
+    phases.append(phase((), act, copies))
+
+    def finish():
+        column[row] = held[...]
+        for copy in copies:
+            copy.wait()
+        total = column[0]
+        for i in range(1, sizes[1]):
+            total = total + column[i]
+        out[...] = total
+
+    phases.append(phase((), finish))
     return phases
 
 
@@ -503,29 +500,44 @@
     return run
 
 
-def gather_kernel(sizes, qkv_ref, small_ref, proj_ref, fc1_ref, fc2_ref, qkv_full, small_all, proj_rows, fc1_rows, fc2_rows,
-                  qkv_slots, proj_slots, fc1_slots, fc2_slots, qkv_rows, send, recv, own_sem, keep_sem):
+def fill_bias(small_all, rel_ref, mask_ref, bias_ref, spread_ref, heads_local):
+    gy_size, pad_rows, lanes = small_all.shape
+    depth = -(-RELS // 16) * 16
+    onehot = (lax.broadcasted_iota(jnp.int32, (depth, SLOT * SLOT), 0) == rel_ref[...]).astype(jnp.bfloat16)
+    table = small_all[...].reshape(gy_size * pad_rows, lanes)[:, :depth]
+    wide = matmul(table, onehot)
+    total = gy_size * pad_rows
+    for j in range(SLOT):
+        spread_ref[j * total : (j + 1) * total, :] = wide[:, j * SLOT : (j + 1) * SLOT]
+    for h in range(gy_size * heads_local):
+        line = h // heads_local * pad_rows + 2 + h % heads_local
+        one = spread_ref[pl.ds(line, SLOT, stride=total), :]
+        low = h % PACK * SLOT
+        for w in range(WIN_COUNT):
+            bias_ref[w, h // PACK, :, low : low + SLOT] = one + mask_ref[w]
+
+
+def gather_kernel(sizes, heads_local, qkv_ref, small_ref, proj_ref, fc1_ref, rel_ref, mask_ref,
+                  qkv_full, small_all, bias_ref, proj_rows, fc1_rows,
+                  qkv_slots, proj_slots, fc1_slots, qkv_rows, spread_ref, send, recv, own_sem, keep_sem):
     greet(*sizes)
     sender = Sender(send, recv)
 
     def join_later():
         join_rows(proj_slots, proj_rows, 1)
         join_rows(fc1_slots, fc1_rows, 1)
-        join_rows(fc2_slots, fc2_rows, 1)
-
-    first = gather_column(
-        sender, [qkv_ref, small_ref], [qkv_slots, small_all], own_sem.at[0], sizes, lambda: join_rows(qkv_slots, qkv_rows, 3)
-    )
-    second = gather_column(
-        sender, [proj_ref, fc1_ref, fc2_ref], [proj_slots, fc1_slots, fc2_slots], own_sem.at[1], sizes, join_later
-    )
+
+    first = gather_column(sender, [small_ref, qkv_ref], [small_all, qkv_slots], own_sem.at[0], sizes, lambda: join_rows(qkv_slots, qkv_rows, 3))
+    second = gather_column(sender, [proj_ref, fc1_ref], [proj_slots, fc1_slots], own_sem.at[1], sizes, join_later)
     plane = gather_plane(sender, qkv_rows, qkv_full, keep_sem.at[0], sizes)
-    for run in first:
+    first[0]()
+    second[0]()
+    first[1]()
+    plane[0]()
+    fill_bias(small_all, rel_ref, mask_ref, bias_ref, spread_ref, heads_local)
+    for run in plane[1:]:
         run()
-    while plane or second:
-        for queue in (plane, second):
-            if queue:
-                queue.pop(0)()
+    second[1]()
 
 
 def vmem_spec():
@@ -540,32 +552,39 @@
     return lax.axis_size("gx"), lax.axis_size("gy")
 
 
-def gather_weights(qkv, small, proj_t, fc1, fc2_t):
+def gather_weights(qkv, small, proj_t, fc1, heads_local):
     sizes = mesh_sizes()
     gx_size, gy_size = sizes
     rows = qkv.shape[0]
-    later = [jax.ShapeDtypeStruct((rows, v.shape[1] * gy_size), v.dtype) for v in (proj_t, fc1, fc2_t)]
+    _, rel, mask = static_tables(1)
+    later = [jax.ShapeDtypeStruct((rows, v.shape[1] * gy_size), v.dtype) for v in (proj_t, fc1)]
     wide = qkv.shape[1] * gy_size
-    count = 5 * (gy_size - 1) + gx_size - 1
+    count = 4 * (gy_size - 1) + gx_size - 1
+    bias = (WIN_COUNT, gy_size * heads_local // PACK, SLOT, PACK * SLOT)
     return pl.pallas_call(
-        functools.partial(gather_kernel, sizes),
-        in_specs=[vmem_spec()] * 5,
+        functools.partial(gather_kernel, sizes, heads_local),
+        in_specs=[hbm_spec()] * 4 + [vmem_spec()] * 2,
         out_specs=[hbm_spec()] + [vmem_spec()] * 4,
-        out_shape=[jax.ShapeDtypeStruct((rows * gx_size, wide), qkv.dtype), jax.ShapeDtypeStruct((gy_size,) + small.shape, small.dtype)]
+        out_shape=[
+            jax.ShapeDtypeStruct((rows * gx_size, wide), qkv.dtype),
+            jax.ShapeDtypeStruct((gy_size,) + small.shape, small.dtype),
+            jax.ShapeDtypeStruct(bias, jnp.float32),
+        ]
         + later,
-        scratch_shapes=[pltpu.VMEM((gy_size,) + v.shape, v.dtype) for v in (qkv, proj_t, fc1, fc2_t)]
+        scratch_shapes=[pltpu.VMEM((gy_size,) + v.shape, v.dtype) for v in (qkv, proj_t, fc1)]
         + [
             pltpu.VMEM((rows, wide), qkv.dtype),
-            pltpu.SemaphoreType.DMA((count,)), pltpu.SemaphoreType.DMA((count,)), pltpu.SemaphoreType.DMA((2, 3)),
+            pltpu.VMEM((SLOT * gy_size * small.shape[0], SLOT), jnp.float32),
+            pltpu.SemaphoreType.DMA((count,)), pltpu.SemaphoreType.DMA((count,)), pltpu.SemaphoreType.DMA((2, 2)),
             pltpu.SemaphoreType.DMA((1,)),
         ],
-        compiler_params=pltpu.CompilerParams(collective_id=0, has_side_effects=True, vmem_limit_bytes=16 << 20),
+        compiler_params=pltpu.CompilerParams(collective_id=0, has_side_effects=True, vmem_limit_bytes=14 << 20),
         name="gather_weights",
-    )(qkv, small, proj_t, fc1, fc2_t)
+    )(qkv, small, proj_t, fc1, jnp.asarray(rel.reshape(1, -1)), jnp.asarray(mask))
 
 
 def share_kernel(sizes, groups, whole_count, *refs):
-    gx_bits, gy_bits = bits_of(sizes[0]), bits_of(sizes[1])
+    gx_bits = bits_of(sizes[0])
     arrays = len(groups)
     refs = list(refs)
 
@@ -575,31 +594,53 @@
         return out
 
     inputs, (small,) = take(arrays), take(1)
-    outs, (small_out,) = take(arrays), take(1)
+    act, fc2_full, resid, shift = take(4)
+    outs, (small_out, output) = take(arrays), take(2)
     planes = [take(gx_bits) for _ in range(whole_count)]
-    totals = take(whole_count)
-    slots = take(arrays)
-    columns = [take(gy_bits) for _ in range(arrays)]
-    small_came, small_totals, send, recv = take(4)
+    totals, slots, columns = take(whole_count), take(arrays), take(arrays)
+    small_came, small_totals, small_column, send, recv = take(5)
     greet(*sizes)
     sender = Sender(send, recv)
     streams = []
     for n in range(arrays):
         phases = share_plane(sender, inputs[n], planes[n], totals[n], sizes) if n < whole_count else []
         total = totals[n] if n < whole_count else inputs[n]
-        phases += share_column(sender, total, slots[n], columns[n], outs[n], groups[n], sizes)
-        streams.append(phases)
-    streams.append(sum_small(sender, small, small_came, small_totals, small_out, sizes))
+        column = share_column(sender, total, slots[n], columns[n], outs[n], groups[n], sizes)
+        if phases:
+            last, after = phases.pop(), column.pop(0)
+            phases.append(both(last, after))
+        streams.append(phases + column)
+    streams.append(sum_small(sender, small, small_came, small_totals, small_column, small_out, sizes))
+    width = output.shape[1]
+    chunk = min(2 * 128, width)
+    rest = list(range(0, width, chunk))
+    place = 0
     while any(streams):
         for queue in streams:
             if queue:
                 queue.pop(0)()
-
-
-def share_sums(fulls, rows_sums, groups, small):
+        place += 1
+        if place >= 2 and rest:
+            low = rest.pop(0)
+            cols = slice(low, low + chunk)
+            output[:, cols] = (resid[:, cols] + matmul_nt(act[...], fc2_full[cols, :]) + shift[:, cols]).astype(output.dtype)
+    for low in rest:
+        cols = slice(low, low + chunk)
+        output[:, cols] = (resid[:, cols] + matmul_nt(act[...], fc2_full[cols, :]) + shift[:, cols]).astype(output.dtype)
+
+
+def both(one, other):
+    def run():
+        one()
+        other()
+
+    return run
+
+
+def share_sums(fulls, rows_sums, groups, small, product):
     sizes = mesh_sizes()
     gx_size, gy_size = sizes
-    gx_bits, gy_bits = bits_of(gx_size), bits_of(gy_size)
+    gx_bits = bits_of(gx_size)
     rows = fulls[0].shape[0] // gx_size
     arrays = tuple(fulls) + tuple(rows_sums)
     planes, slots, columns = [], [], []
@@ -608,29 +649,30 @@
     for value in arrays:
         wide = value.shape[1] // gy_size
         slots.append(pltpu.VMEM((gy_size, rows, wide), value.dtype))
-        columns += [pltpu.VMEM((gy_size >> (bit + 1), rows, wide), value.dtype) for bit in range(gy_bits)]
-    stages = gx_bits + gy_bits
-    count = len(fulls) * (gx_size - 1) + len(arrays) * (gy_size - 1) + stages
+        columns.append(pltpu.VMEM((gy_size - 1, rows, wide), value.dtype))
+    count = len(fulls) * (gx_size - 1) + len(arrays) * (gy_size - 1) + gx_bits + gy_size - 1
     return pl.pallas_call(
         functools.partial(share_kernel, sizes, groups, len(fulls)),
-        in_specs=[vmem_spec()] * (len(arrays) + 1),
-        out_specs=[vmem_spec()] * (len(arrays) + 1),
+        in_specs=[vmem_spec()] * (len(arrays) + 5),
+        out_specs=[vmem_spec()] * (len(arrays) + 2),
         out_shape=[jax.ShapeDtypeStruct((rows, value.shape[1] // gy_size), jnp.float32) for value in arrays]
-        + [jax.ShapeDtypeStruct(small.shape, small.dtype)],
+        + [jax.ShapeDtypeStruct(small.shape, small.dtype), jax.ShapeDtypeStruct(product[2].shape, jnp.bfloat16)],
         scratch_shapes=planes + [pltpu.VMEM((rows, full.shape[1]), full.dtype) for full in fulls] + slots + columns + [
-            pltpu.VMEM((stages,) + small.shape, small.dtype),
-            pltpu.VMEM((stages,) + small.shape, small.dtype),
+            pltpu.VMEM((gx_bits,) + small.shape, small.dtype),
+            pltpu.VMEM((gx_bits,) + small.shape, small.dtype),
+            pltpu.VMEM((gy_size,) + small.shape, small.dtype),
             pltpu.SemaphoreType.DMA((count,)),
             pltpu.SemaphoreType.DMA((count,)),
         ],
-        compiler_params=pltpu.CompilerParams(collective_id=1, has_side_effects=True, vmem_limit_bytes=24 << 20),
+        compiler_params=pltpu.CompilerParams(collective_id=1, has_side_effects=True, vmem_limit_bytes=18 << 20),
         name="share_sums",
-    )(*arrays, small)
+    )(*arrays, small, *product)
 
 
 def forward_stage(
-    sizes, qkv_ref, perm_ref, perm_t_ref, bias_ref, owner_ref, proj_rows, fc1_rows, fc2_rows,
-    context_ref, windows_ref, probs_ref, proj_full, fc1_full, fc2_full, ctx_ref, send, recv, keep_sem,
+    sizes, qkv_ref, perm_ref, perm_t_ref, bias_ref, owner_ref, proj_rows, fc1_rows, fc2_local,
+    context_ref, windows_ref, probs_ref, proj_full, fc1_full, fc2_full,
+    ctx_ref, fc2_slots, fc2_rows, send, recv, keep_sem, own_sem,
 ):
     image, last = pl.program_id(0), pl.num_programs(0) - 1
 
@@ -642,16 +684,23 @@
     own = (proj_rows, fc1_rows, fc2_rows)
     fulls = (proj_full, fc1_full, fc2_full)
     streams = [gather_plane(sender, own[n], fulls[n], keep_sem.at[n], sizes) for n in range(3)]
+    column = gather_column(sender, [fc2_local], [fc2_slots], own_sem, sizes, lambda: join_rows(fc2_slots, fc2_rows, 1))
 
     @pl.when(image == 0)
     def _():
-        for phases in streams:
-            phases[0]()
-
-    for n, phases in enumerate(streams):
-        @pl.when(image == jnp.minimum(n + 1, last))
-        def _():
-            phases[1]()
+        column[0]()
+        streams[0][0]()
+        streams[1][0]()
+
+    @pl.when(image == jnp.minimum(1, last))
+    def _():
+        streams[0][1]()
+
+    @pl.when(image == jnp.minimum(2, last))
+    def _():
+        streams[1][1]()
+        column[1]()
+        streams[2][0]()
 
     forward_kernel(
         qkv_ref, perm_ref, perm_t_ref, bias_ref, owner_ref, context_ref, windows_ref, probs_ref, ctx_ref
@@ -659,6 +708,7 @@
 
     @pl.when(image == last)
     def _():
+        streams[2][1]()
         for place in range(2, len(streams[0])):
             for phases in streams:
                 phases[place]()
@@ -766,12 +816,12 @@
 
     small = jnp.concatenate([fc1_bias[None], lane_row(qv_bias.reshape(1, -1)), lane_row(rel_table.T)], 0)
     small = jnp.pad(small, ((0, ROW_PAD - small.shape[0]), (0, 0)))
-    qkv_flat, small, *later = gather_weights(
-        qkv_weight.reshape(block_rows, -1), small, proj_weight.T, fc1_weight, fc2_weight.T
-    )
+    qkv_flat, small, bias, *later = gather_weights(
+        qkv_weight.reshape(block_rows, -1), small, proj_weight.T, fc1_weight, heads_local
+    )
+    later.append(fc2_weight.T)
     fc1_bias = small[:, 0].reshape(-1)
     qv_bias = small[:, 1, : 2 * part].reshape(-1, 2, part).transpose(1, 0, 2).reshape(2, -1)
-    rel_table = small[:, 2 : 2 + heads_local, :RELS].reshape(-1, RELS)
     gain_one = ln1_gain.astype(jnp.float32)
     gain_two = ln2_gain.astype(jnp.float32)
     resid = block_input.astype(jnp.float32)
@@ -779,17 +829,14 @@
     hidden_one = (pre_one.astype(jnp.bfloat16))
     bias_row = jnp.stack([qv_bias[0], jnp.zeros_like(qv_bias[0]), qv_bias[1]]).reshape(1, 3 * width)
     mixed = (matmul(hidden_one, qkv_flat) + bias_row.astype(jnp.float32)).astype(jnp.bfloat16)
-    tables = attention_tables(rel_table, tok_local // IMAGE)
-    context, windows, probs, proj_cols, fc1_rows, fc2_cols = attend_forward(mixed, tables, later)
+    tables = attention_tables(tok_local // IMAGE)
+    context, windows, probs, proj_cols, fc1_rows, fc2_cols = attend_forward(mixed, tables, bias, later)
     resid_one = resid + (matmul_nt(context, proj_cols)) + proj_bias.astype(jnp.float32)
     normed_two, scale_two, pre_two = layer_norm(resid_one, gain_two, ln2_bias.astype(jnp.float32))
     hidden_two = (pre_two.astype(jnp.bfloat16))
     pre_act = matmul(hidden_two, fc1_rows) + fc1_bias.astype(jnp.float32)
     act_full, slope = gelu_parts(pre_act)
     act_low = act_full.astype(jnp.bfloat16)
-    output = (
-        resid_one + (matmul_nt(act_low, fc2_cols)) + fc2_bias.astype(jnp.float32)
-    ).astype(jnp.bfloat16)
     live_rows = local_live(tok_local, live_images)
     grad_out = jnp.where(live_rows[:, None], cotangent, jnp.zeros_like(cotangent))
     grad_float = grad_out.astype(jnp.float32)
@@ -817,8 +864,9 @@
         jnp.bfloat16
     )
     own = (d_ln1_gain, d_ln1_bias, d_proj_bias, d_ln2_gain, d_ln2_bias, d_fc2_bias, d_qv_bias, d_table, d_fc1_bias)
-    d_qkv_weight, d_proj_weight, d_fc1_weight, d_fc2_weight, sums = share_sums(
-        (d_qkv_weight, d_proj_weight), sums, (3, 1, 1, 1), pack_rows(own)
+    product = (act_low, fc2_cols, resid_one, fc2_bias.astype(jnp.float32)[None])
+    d_qkv_weight, d_proj_weight, d_fc1_weight, d_fc2_weight, sums, output = share_sums(
+        (d_qkv_weight, d_proj_weight), sums, (3, 1, 1, 1), pack_rows(own), product
     )
     d_fc2_weight = d_fc2_weight.T
     d_proj_weight = d_proj_weight.T

time: 189 us -> 179 us (0.947)
  matrix products: 41.3 us -> 33.8 us
  Pallas kernels: 112 us -> 117 us
  local copies, waits for them, and re-layouts: 22.9 us -> 18.9 us
  other arithmetic: 10 us -> 6.41 us
    dot_general x4 -> x3, matrix products: 10.5 us -> 4.96 us  [matmul_nt(): lax.dot_general(left, right, (((1,), (1,)), ((), ())), preferred_element_...]
    add x3 -> x0, local copies, waits for them, and re-layouts: 4.51 us -> none  [attention_tables(): bias = bias[None] + jnp.asarray(mask)[:, None, :, None, :]]
    reshape x3, local copies, waits for them, and re-layouts: 0.43 us -> 4.89 us  [attend_backward(): d_bias.reshape(groups, SLOT, PACK, SLOT).transpose(0, 2, 1, 3)]
    unnamed x99 -> x88, local copies, waits for them, and re-layouts: 15.1 us -> 11.1 us
    dot_general x4, matrix products: 18.3 us -> 15.9 us  [matmul(): return jnp.dot(left, right, preferred_element_type=jnp.float32)]
    pallas_call x1, Pallas kernels: 28.1 us -> 30.3 us  [gather_weights(): pl.pallas_call(functools.partial(gather_kernel, sizes, heads_local), in_s...]
    convert_element_type x1, other arithmetic: 3.51 us -> 1.46 us  [blocked_layer(): (d_resid_one + norm_back(d_hidden_one, normed_one, scale_one, gain_one))....]
where the time goes in v2:
time: 179 us; the launch traced here: 178 us
  Pallas kernels  117 us (65%)
  matrix products  33.8 us (19%)
  local copies, waits for them, and re-layouts  18.9 us (11%)
  other arithmetic  6.41 us (4%)
  between operations  2.01 us (1%)
    pallas_call x1, Pallas kernels, gather_weights(): pl.pallas_call(functools.partial(gather_kernel, sizes, heads_local), in_s...  30.3 us
    pallas_call x1, Pallas kernels, attend_forward(): pl.pallas_call(functools.partial(forward_stage, sizes), grid=(count,), in...  29.3 us
    pallas_call x1, Pallas kernels, attend_backward(): pl.pallas_call(functools.partial(backward_stage, sizes), grid=(count,), i...  28.9 us
    pallas_call x1, Pallas kernels, share_sums(): pl.pallas_call(functools.partial(share_kernel, sizes, groups, len(fulls))...  28.8 us
    dot_general x4, matrix products, matmul(): return jnp.dot(left, right, preferred_element_type=jnp.float32)  15.9 us
    unnamed x88, local copies, waits for them, and re-layouts  11.1 us
    dot_general x4, matrix products, matmul_tn(): lax.dot_general(left, right, (((0,), (0,)), ((), ())), preferred_element_...  10.6 us
    dot_general x3, matrix products, matmul_nt(): lax.dot_general(left, right, (((1,), (1,)), ((), ())), preferred_element_...  4.96 us

profile of v2, /device:TPU:0, one launch (start us, length us, event | category | flops | bytes accessed | tf_op | source)
XLA Modules:
  0.0 178.5 jit_solution(13843511951762027620)
XLA Ops:
  0.7 0.8 copy-done
  1.5 0.7 broadcast_in_dim.15
  2.1 0.7 copy.61
  2.8 0.7 fusion.31
  3.5 0.9 copy-done.5
  4.4 0.8 copy-done.6
  5.3 0.7 copy-done.7
  6.0 0.7 copy-done.8
  6.7 30.3 %gather_weights.1 = (bf16[512,1536]{1,0:T(8,128)(2,1)S(1)}, bf16[4,16,512]{2,1,0:T(8,128)(2,1)S(1)}, f32[4,2,64,512]{3,2,1,0:T(8,128)S(1)}, bf16[64,512]{1,0:T(8,128)(2,1)S(1)}, bf16[64,2048]{1,0:T(8,128)(2,1)S(1)}) custom-call(bf16[64,384]{1,0:T(8,128)(2,1)S(1)} %copy_bitcast_fusion.2.qkv_ref, bf16[16,512]{1,0:T(8,128)(2,1)S(1)} %pad.37.small_ref, ...), custom_call_target="tpu_custom_call" | custom-call | tf_op jit(solution)/shard_map/gather_weights/pallas_call | solution.py:564
  37.0 0.6 copy-done.12
  37.8 1.8 %convert_reduce_fusion = (f32[784]{0:T(1024)S(1)}, f32[784]{0:T(1024)S(1)}) fusion(bf16[784,512]{1,0:T(8,128)(2,1)} %param.22), kind=kLoop, calls=%fused_computation.17 | loop fusion | flops 1604064 | bytes 809088 | tf_op jit(solution)/shard_map/reduce_sum | solution.py:265
  39.7 0.7 convert_element_type.106
  40.4 0.7 convert_element_type.107
  41.1 2.8 %add_convert_fusion.qkv_ref = bf16[784,1536]{1,0:T(8,128)(2,1)S(1)} fusion(bf16[512,1536]{1,0:T(8,128)(2,1)S(1)} %get-tuple-element.37, f32[1536]{0:T(1024)S(1)} %reshape.204, bf16[784,512]{1,0:T(8,128)(2,1)} %param.22, f32[512]{0:T(512)S(1)} %convert_element_type.107, f32[512]{0:T(512)S(1)} %convert_element_type.106, f32[784]{0:T(1024)S(1)} %get-tuple-element.113, ...), kind=kOutput, calls=%fused_computation.8 | convolution fusion | flops 1237942272 | bytes 4800640 | tf_op jit(solution)/shard_map/dot_general | solution.py:24
  43.9 29.3 %attend_forward.1 = (bf16[784,512]{1,0:T(8,128)(2,1)S(1)}, bf16[4,256,1536]{2,1,0:T(8,128)(2,1)}, f32[4,8,64,512]{3,2,1,0:T(8,128)}, bf16[512,512]{1,0:T(8,128)(...) custom-call(bf16[784,1536]{1,0:T(8,128)(2,1)S(1)} %add_convert_fusion.qkv_ref, ...), custom_call_target="tpu_custom_call" | custom-call | flops 6000000000 | bytes 24000000 | tf_op jit(solution)/shard_map/attend_forward/pallas_call | solution.py:188
  73.3 0.9 multiply_reduce_fusion.2
  74.2 0.4 copy-done.3
  74.6 0.2 copy-done.20
  74.8 5.6 %multiply_convert_fusion = (bf16[784,2048]{1,0:T(8,128)(2,1)}, f32[784,2048]{1,0:T(8,128)}) fusion(f32[2048]{0:T(1024)S(1)} %bitcast.95, bf16[512,2048]{1,0:T(8,128)(2,1)S(1)} %get-tuple-element.45, f32[784,512]{1,0:T(8,128)S(1)} %get-tuple-element.116.refs_7_, f32[512]{0:T(512)S(1)} %convert_element_type.118, f32[512]{0:T(512)S(1)} %convert_element_type.117, ...), kind=kOutput, calls=%fused_computation.6 | convolution fusion | flops 1655808000 | bytes 13355136 | tf_op jit(solution)/shard_map/dot_general | solution.py:24
  81.1 7.0 %fusion.41 = (f32[2048]{0:T(1024)S(1)}, bf16[784,2048]{1,0:T(8,128)(2,1)S(1)}) fusion(f32[784,2048]{1,0:T(8,128)} %get-tuple-element.119, f32[2048]{0:T(1024)S(1)} %bitcast.96, bf16[512,2048]{1,0:T(8,128)(2,1)} %copy-done.3, bf16[784,512]{1,0:T(8,128)(2,1)} %param.23, pred[784]{0:T(1024)(128)(4,1)S(1)} %fusion.33), kind=kOutput, calls=%fused_computation.107 | convolution fusion | flops 1663834112 | bytes 12550928 | tf_op jit(solution)/shard_map/dot_general | solution.py:24
  88.1 2.6 %convolution_convert_fusion.1.d_fc1_ref = bf16[512,2048]{1,0:T(8,128)(2,1)S(1)} fusion(bf16[784,2048]{1,0:T(8,128)(2,1)S(1)} %get-tuple-element.122, f32[784,512]{1,0:T(8,128)S(1)} %get-tuple-element.116.refs_7_, f32[512]{0:T(512)S(1)} %convert_element_type.118, f32[512]{0:T(512)S(1)} %convert_element_type.117, f32[784]{0:T(1024)S(1)} %get-tuple-element.111, ...), kind=kOutput, calls=%fused_computation.10 | convolution fusion | flops 1647222784 | bytes 6924416 | tf_op jit(solution)/shard_map/dot_general | solution.py:28
  90.7 2.3 %multiply_reduce_fusion = (f32[512]{0:T(512)S(1)}, f32[784]{0:T(1024)S(1)}, f32[784]{0:T(1024)S(1)}, f32[512]{0:T(512)S(1)}, f32[784,512]{1,0:T(8,128)S(1)}) fusion(f32[784,512]{1,0:T(8,128)S(1)} %get-tuple-element.116.refs_7_, f32[784]{0:T(1024)S(1)} %get-tuple-element.111, f32[784]{0:T(1024)S(1)} %get-tuple-element.110, ...), kind=kOutput, calls=%fused_computation.35 | convolution fusion | flops 1647777280 | bytes 8538368 | tf_op jit(solution)/shard_map/dot_general | solution.py:34
  93.0 0.9 fusion.40
  94.0 0.6 convolution_convert_fusion.3.d_context_ref
  94.6 0.3 copy-done.1
  94.9 2.5 %convolution_convert_fusion.d_fc2_ref = bf16[512,2048]{1,0:T(8,128)(2,1)S(1)} fusion(bf16[784,2048]{1,0:T(8,128)(2,1)S(1)} %copy-done.1, bf16[784,512]{1,0:T(8,128)(2,1)S(1)} %copy-done.30, pred[784]{0:T(1024)(128)(4,1)S(1)} %fusion.33), kind=kOutput, calls=%fused_computation.9 | convolution fusion | flops 1645617152 | bytes 6112016 | tf_op jit(solution)/shard_map/dot_general | solution.py:28
  97.5 0.6 copy-done.26
  98.1 28.9 %attend_backward.1 = (bf16[784,1536]{1,0:T(8,128)(2,1)S(1)}, f32[2,64,512]{2,1,0:T(8,128)S(1)}, f32[2,512]{1,0:T(2,128)S(1)}, bf16[64,2048]{1,0:T(8,128)(2,1)S(1)}, bf16[64,2048]{1,0:T(8,128)(2,1)S(1)}) custom-call(bf16[784,512]{1,0:T(8,128)(2,1)S(1)} %convolution_convert_fusion.3.d_context_ref, bf16[4,256,1536]{2,1,0:T(8,128)(2,1)S(1)} %copy-done.27, ...), custom_call_target="tpu_custom_call" | custom-call | flops 8999999488 | bytes 32000000 | tf_op jit(solution)/shard_map/attend_backward/pallas_call | solution.py:227
  127.0 1.8 %fusion.14 = (f32[784]{0:T(1024)S(1)}, f32[512]{0:T(512)S(1)}, f32[784]{0:T(1024)S(1)}, f32[512]{0:T(512)S(1)}, f32[784,512]{1,0:T(8,128)S(1)}) fusion(bf16[784,512]{1,0:T(8,128)(2,1)S(1)} %copy-done.29, f32[512]{0:T(512)S(1)} %convert_element_type.106, f32[784]{0:T(1024)S(1)} %get-tuple-element.113, f32[784]{0:T(1024)S(1)} %get-tuple-element.112, ...), kind=kOutput, calls=%fused_computation.28 | convolution fusion | flops 1237136896 | bytes 6408448 | tf_op jit(solution)/shard_map/dot_general | solution.py:34
  128.9 1.5 fusion.18
  130.4 0.9 reshape.197
  131.4 2.0 %copy.59 = f32[2,64,8,64]{3,1,2,0:T(8,128)} copy(f32[2,64,8,64]{3,2,1,0:T(8,128)} %reshape.197) | data formatting | bytes 524288 | tf_op jit(solution)/shard_map/reshape | solution.py:249
  133.4 1.9 %reshape.198 = f32[16,4096]{1,0:T(8,128)} reshape(f32[2,8,64,64]{3,2,1,0:T(8,128)} %bitcast.93) | data formatting | bytes 524288 | tf_op jit(solution)/shard_map/reshape | solution.py:249
  135.3 2.4 %fusion.5 = f32[169,16]{1,0:T(8,128)S(1)} fusion(f32[16,4096]{1,0:T(8,128)} %reshape.198, s32[4096]{0:T(1024)S(1)} %copy-done.35), kind=kOutput, calls=%fused_computation.13 | convolution fusion | flops 133599232 | bytes 289344 | tf_op jit(solution)/shard_map/dot_general | solution.py:250
  137.7 0.1 reshape.199
  137.8 2.3 %convolution_convert_fusion.4.refs_1_ = bf16[512,512]{1,0:T(8,128)(2,1)S(1)} fusion(bf16[784,512]{1,0:T(8,128)(2,1)S(1)} %copy-done.21, f32[784,512]{1,0:T(8,128)} %copy-done.28), kind=kOutput, calls=%fused_computation.47 | convolution fusion | flops 411705344 | bytes 2932736 | tf_op jit(solution)/shard_map/dot_general | solution.py:28
  140.2 3.2 %convolution_convert_fusion.2.refs_0_ = bf16[512,1536]{1,0:T(8,128)(2,1)S(1)} fusion(bf16[784,1536]{1,0:T(8,128)(2,1)S(1)} %copy-done.25, bf16[784,512]{1,0:T(8,128)(2,1)} %param.22, f32[512]{0:T(512)S(1)} %convert_element_type.107, f32[512]{0:T(512)S(1)} %convert_element_type.106, f32[784]{0:T(1024)S(1)} %get-tuple-element.113, f32[784]{0:T(1024)S(1)} %get-tuple-element.112), kind=kOutput, calls=%fused_computation.11 | convolution fusion | flops 1236320256 | bytes 4794496 | tf_op jit(solution)/shard_map/dot_general | solution.py:28
  143.5 28.8 %share_sums.1 = (f32[64,384]{1,0:T(8,128)S(1)}, f32[64,128]{1,0:T(8,128)S(1)}, f32[64,512]{1,0:T(8,128)S(1)}, f32[64,512]{1,0:T(8,128)S(1)}, f32[96,128]{1,0:T(8,128)S(1)}, /*index=5*/bf16[784,512]{1,0:T(8,128)(2,1)S(1)}) custom-call(bf16[512,1536]{1,0:T(8,128)(2,1)S(1)} %convolution_convert_fusion.2.refs_0_, ...), custom_call_target="tpu_custom_call" | custom-call | tf_op jit(solution)/shard_map/share_sums/pallas_call | solution.py:654
  172.4 0.1 constant_dynamic-slice_fusion
  172.5 0.7 copy.45
  173.2 0.6 copy_bitcast_fusion.1
  173.8 0.7 dynamic_slice.11
  174.5 0.6 constant_dynamic-slice_fusion.1
  175.0 0.6 slice_bitcast_fusion.1
  175.6 0.9 copy.75
  176.5 0.6 copy.76
  177.1 0.7 copy.77
  177.8 0.7 copy.78
  (99 shorter events, 0.6 us)
Async XLA Ops:
  0.6 0.8 copy-start
  3.5 0.9 copy-start.5
  4.4 0.8 copy-start.6
  5.3 0.7 copy-start.7
  6.0 0.7 copy-start.8
  37.0 0.6 copy-start.12
  37.6 6.2 %copy-start.9 = (bf16[512,1536]{1,0:T(8,128)(2,1)}, bf16[512,1536]{1,0:T(8,128)(2,1)S(1)}, u32[]{:S(2)}) copy-start(bf16[512,1536]{1,0:T(8,128)(2,1)S(1)} %get-tuple-element.37) | copy-start | bytes 4718596
  41.0 2.8 %copy-start.11 = (bf16[512,64]{0,1:T(8,128)(2,1)S(1)}, bf16[512,64]{0,1:T(8,128)(2,1)}, u32[]{:S(2)}) copy-start(bf16[512,64]{0,1:T(8,128)(2,1)} %param.36) | copy-start | bytes 196612
  41.0 2.8 %copy-start.13 = (bf16[64,512]{1,0:T(8,128)(2,1)S(1)}, bf16[64,512]{1,0:T(8,128)(2,1)}, u32[]{:S(2)}) copy-start(bf16[64,512]{1,0:T(8,128)(2,1)} %copy-done.12) | copy-start | bytes 196612
  41.0 2.8 %copy-start.14 = (bf16[4,256,208]{2,1,0:T(8,128)(2,1)S(1)}, bf16[4,256,208]{2,1,0:T(8,128)(2,1)}, u32[]{:S(2)}) copy-start(bf16[4,256,208]{2,1,0:T(8,128)(2,1)} %constant.93.perm_ref) | copy-start | bytes 1277956
  41.0 2.8 %copy-start.16 = (bf16[4,208,256]{2,1,0:T(8,128)(2,1)S(1)}, bf16[4,208,256]{2,1,0:T(8,128)(2,1)}, u32[]{:S(2)}) copy-start(bf16[4,208,256]{2,1,0:T(8,128)(2,1)} %constant.94.perm_t_ref) | copy-start | bytes 1277956
  41.0 2.8 %copy-start.18 = (bf16[512,256]{1,0:T(8,128)(2,1)S(1)}, bf16[512,256]{1,0:T(8,128)(2,1)}, u32[]{:S(2)}) copy-start(bf16[512,256]{1,0:T(8,128)(2,1)} %constant.95.owner_ref) | copy-start | bytes 786436
  43.9 29.4 %copy-start.31 = (bf16[512]{0:T(512)(128)(2,1)S(1)}, bf16[512]{0:T(512)(128)(2,1)}, u32[]{:S(2)}) copy-start(bf16[512]{0:T(512)(128)(2,1)} %param.31) | copy-start | bytes 3076
  43.9 29.4 %copy-start.29 = (bf16[784,512]{1,0:T(8,128)(2,1)S(1)}, bf16[784,512]{1,0:T(8,128)(2,1)}, u32[]{:S(2)}) copy-start(bf16[784,512]{1,0:T(8,128)(2,1)} %param.22) | copy-start | bytes 2408452
  73.2 1.3 copy-start.3
  73.2 1.6 copy-start.20
  73.2 7.2 %copy-start.22 = (bf16[512,2048]{1,0:T(8,128)(2,1)}, bf16[512,2048]{1,0:T(8,128)(2,1)S(1)}, u32[]{:S(2)}) copy-start(bf16[512,2048]{1,0:T(8,128)(2,1)S(1)} %get-tuple-element.45) | copy-start | bytes 6291460
  73.3 1.5 copy-start.32
  73.3 1.5 copy-start.33
  88.1 2.6 %copy-start.23 = (bf16[512,2048]{1,0:T(8,128)(2,1)S(1)}, bf16[512,2048]{1,0:T(8,128)(2,1)}, u32[]{:S(2)}) copy-start(bf16[512,2048]{1,0:T(8,128)(2,1)} %copy-done.22) | copy-start | bytes 6291460
  90.7 2.3 %copy-start.30 = (bf16[784,512]{1,0:T(8,128)(2,1)S(1)}, bf16[784,512]{1,0:T(8,128)(2,1)}, u32[]{:S(2)}) copy-start(bf16[784,512]{1,0:T(8,128)(2,1)} %param.23) | copy-start | bytes 2408452
  93.0 1.9 %copy-start.1 = (bf16[784,2048]{1,0:T(8,128)(2,1)S(1)}, bf16[784,2048]{1,0:T(8,128)(2,1)}, u32[]{:S(2)}) copy-start(bf16[784,2048]{1,0:T(8,128)(2,1)} %get-tuple-element.118.refs_5_) | copy-start | bytes 9633796
  94.0 34.9 %copy-start.28 = (f32[784,512]{1,0:T(8,128)}, f32[784,512]{1,0:T(8,128)S(1)}, u32[]{:S(2)}) copy-start(f32[784,512]{1,0:T(8,128)S(1)} %get-tuple-element.102) | copy-start | bytes 4816900
  94.0 3.4 %copy-start.27 = (bf16[4,256,1536]{2,1,0:T(8,128)(2,1)S(1)}, bf16[4,256,1536]{2,1,0:T(8,128)(2,1)}, u32[]{:S(2)}) copy-start(bf16[4,256,1536]{2,1,0:T(8,128)(2,1)} %get-tuple-element.46.windows_ref) | copy-start | bytes 9437188
  94.9 2.5 %copy-start.15 = (bf16[4,256,208]{2,1,0:T(8,128)(2,1)S(1)}, bf16[4,256,208]{2,1,0:T(8,128)(2,1)}, u32[]{:S(2)}) copy-start(bf16[4,256,208]{2,1,0:T(8,128)(2,1)} %constant.93.perm_ref) | copy-start | bytes 1277956
  94.9 2.5 %copy-start.17 = (bf16[4,208,256]{2,1,0:T(8,128)(2,1)S(1)}, bf16[4,208,256]{2,1,0:T(8,128)(2,1)}, u32[]{:S(2)}) copy-start(bf16[4,208,256]{2,1,0:T(8,128)(2,1)} %constant.94.perm_t_ref) | copy-start | bytes 1277956
  94.9 2.5 %copy-start.19 = (bf16[512,256]{1,0:T(8,128)(2,1)S(1)}, bf16[512,256]{1,0:T(8,128)(2,1)}, u32[]{:S(2)}) copy-start(bf16[512,256]{1,0:T(8,128)(2,1)} %constant.95.owner_ref) | copy-start | bytes 786436
  94.9 3.1 %copy-start.26 = (f32[4,8,64,512]{3,2,1,0:T(8,128)S(1)}, f32[4,8,64,512]{3,2,1,0:T(8,128)}, u32[]{:S(2)}) copy-start(f32[4,8,64,512]{3,2,1,0:T(8,128)} %get-tuple-element.47.probs_ref) | copy-start | bytes 12582916
  98.1 28.9 %copy-start.10 = (bf16[512,1536]{1,0:T(8,128)(2,1)S(1)}, bf16[512,1536]{1,0:T(8,128)(2,1)}, u32[]{:S(2)}) copy-start(bf16[512,1536]{1,0:T(8,128)(2,1)} %copy-done.9) | copy-start | bytes 4718596
  127.0 1.8 %copy-start.24 = (bf16[784,1536]{1,0:T(8,128)(2,1)}, bf16[784,1536]{1,0:T(8,128)(2,1)S(1)}, u32[]{:S(2)}) copy-start(bf16[784,1536]{1,0:T(8,128)(2,1)S(1)} %get-tuple-element.48) | copy-start | bytes 7225348
  130.3 5.0 %copy-start.35 = (s32[4096]{0:T(1024)S(1)}, s32[4096]{0:T(1024)}, u32[]{:S(2)}) copy-start(s32[4096]{0:T(1024)} %constant.96) | copy-start | bytes 49156
  131.4 6.4 %copy-start.21 = (bf16[784,512]{1,0:T(8,128)(2,1)S(1)}, bf16[784,512]{1,0:T(8,128)(2,1)}, u32[]{:S(2)}) copy-start(bf16[784,512]{1,0:T(8,128)(2,1)} %copy-done.20) | copy-start | bytes 2408452
  137.8 2.4 %copy-start.25 = (bf16[784,1536]{1,0:T(8,128)(2,1)S(1)}, bf16[784,1536]{1,0:T(8,128)(2,1)}, u32[]{:S(2)}) copy-start(bf16[784,1536]{1,0:T(8,128)(2,1)} %copy-done.24) | copy-start | bytes 7225348
  140.1 3.3 %copy-start.34 = (bf16[512]{0:T(512)(128)(2,1)S(1)}, bf16[512]{0:T(512)(128)(2,1)}, u32[]{:S(2)}) copy-start(bf16[512]{0:T(512)(128)(2,1)} %param.37) | copy-start | bytes 3076
  140.2 3.3 %copy-start.2 = (bf16[784,2048]{1,0:T(8,128)(2,1)S(1)}, bf16[784,2048]{1,0:T(8,128)(2,1)}, u32[]{:S(2)}) copy-start(bf16[784,2048]{1,0:T(8,128)(2,1)} %get-tuple-element.118.refs_5_) | copy-start | bytes 9633796
  140.2 3.3 %copy-start.4 = (bf16[512,2048]{1,0:T(8,128)(2,1)S(1)}, bf16[512,2048]{1,0:T(8,128)(2,1)}, u32[]{:S(2)}) copy-start(bf16[512,2048]{1,0:T(8,128)(2,1)} %copy-done.3) | copy-start | bytes 6291460

commit v3 on v2

--- a/solution.py
+++ b/solution.py
@@ -71,14 +71,13 @@
 
 
 def attention_tables(image_count):
-    column, rel, _ = static_tables(image_count)
+    column, _, _ = static_tables(image_count)
     spots = np.arange(SPAN, dtype=np.int32)
     perm = jnp.asarray((column[:, :, None] == spots).astype(np.float32)).astype(jnp.bfloat16)
     perm_t = jnp.asarray((column[:, None, :] == spots[:, None]).astype(np.float32)).astype(jnp.bfloat16)
-    onehot = (jnp.arange(RELS, dtype=jnp.int32)[:, None] == jnp.asarray(rel.reshape(1, -1))).astype(jnp.bfloat16)
     owner = np.arange(PACK * SLOT)[:, None] // SLOT == np.arange(PACK * HD)[None, :] // HD
     owner = jnp.asarray(owner.astype(np.float32)).astype(jnp.bfloat16)
-    return perm, perm_t, owner, onehot
+    return perm, perm_t, owner
 
 
 def spread(rows, owner):
@@ -122,7 +121,7 @@
 
 def backward_kernel(
     d_context_ref, windows_ref, probs_ref, perm_ref, perm_t_ref, owner_ref,
-    d_mixed_ref, d_bias_ref, d_qv_ref, d_ctx_ref, d_win_ref,
+    d_mixed_ref, d_bias_ref, d_qv_ref, d_ctx_ref, d_win_ref, between,
 ):
     image = pl.program_id(0)
     width = d_context_ref.shape[1]
@@ -137,6 +136,7 @@
 
     d_ctx_ref[...] = matmul(perm_ref[0], d_context_ref[pl.ds(start, SPAN), :]).astype(jnp.bfloat16)
     for g in range(groups):
+        between(2 * image + min(g, 1))
         low = g * PACK * HD
         cols = slice(low, low + PACK * HD)
         d_bias = jnp.zeros((SLOT, PACK * SLOT), jnp.float32)
@@ -176,7 +176,7 @@
 
 
 def attend_forward(qkv, tables, bias, later):
-    perm, perm_t, owner, _ = tables
+    perm, perm_t, owner = tables
     tok, wide = qkv.shape
     width = wide // 3
     count, spots = perm.shape[:2]
@@ -213,7 +213,7 @@
 
 
 def attend_backward(d_context, windows, probs, tables, sums):
-    perm, perm_t, owner, onehot = tables
+    perm, perm_t, owner = tables
     tok, width = d_context.shape
     count, spots, wide = windows.shape
     groups = width // (PACK * HD)
@@ -246,11 +246,7 @@
         cost_estimate=pl.CostEstimate(flops=9_000_000_000, bytes_accessed=32_000_000, transcendentals=0),
         name="attend_backward",
     )(d_context, windows, probs, perm, perm_t, owner, *sums)
-    d_bias = d_bias.reshape(groups, SLOT, PACK, SLOT).transpose(0, 2, 1, 3).reshape(groups * PACK, SLOT * SLOT)
-    d_table = lax.dot_general(
-        onehot.astype(jnp.float32), d_bias, (((1,), (1,)), ((), ())), precision=lax.Precision.HIGHEST
-    )
-    return d_mixed, d_qv, d_table, sums
+    return d_mixed, d_qv, d_bias, sums
 
 
 def gelu_parts(pre_act):
@@ -379,16 +375,20 @@
         return sender.plan(own if first else view(at), view(at), "gx", there)
 
     keep = pltpu.make_async_copy(own, view(mine), sem)
-    held, fresh = [mine], [mine]
-    waits, shared, phases = [], [keep], []
-    for place, step in enumerate(steps):
-        copies = [push(at, n == 0, mine + step) for n, at in enumerate(held)]
-        across = [push(at, place == 0, mine + over) for at in fresh]
-        phases.append(phase(waits, None, copies + across + ([keep] if place == 0 else [])))
-        waits = copies
+    early = [push(mine, True, mine + step) for step in steps]
+    over_own = push(mine, True, mine + over)
+    shared = [keep, over_own]
+    phases = [phase((), None, early + [over_own, keep])]
+    held, fresh = [mine], [mine + steps[0]]
+    waits = [early[0]]
+    for place, step in enumerate(steps[1:], 1):
+        held = held + fresh
+        copies = [push(at, False, mine + step) for at in held[1:]]
+        across = [push(at, False, mine + over) for at in fresh]
+        phases.append(phase(waits, None, copies + across))
         shared += across
+        waits = [early[place]] + copies
         fresh = [at + step for at in held]
-        held = held + fresh
     across = [push(at, False, mine + over) for at in fresh]
     phases.append(phase(waits, None, across))
     phases.append(phase(shared + across))
@@ -527,14 +527,17 @@
         join_rows(proj_slots, proj_rows, 1)
         join_rows(fc1_slots, fc1_rows, 1)
 
-    first = gather_column(sender, [small_ref, qkv_ref], [small_all, qkv_slots], own_sem.at[0], sizes, lambda: join_rows(qkv_slots, qkv_rows, 3))
-    second = gather_column(sender, [proj_ref, fc1_ref], [proj_slots, fc1_slots], own_sem.at[1], sizes, join_later)
+    names = gather_column(sender, [small_ref], [small_all], own_sem.at[0], sizes)
+    first = gather_column(sender, [qkv_ref], [qkv_slots], own_sem.at[1], sizes, lambda: join_rows(qkv_slots, qkv_rows, 3))
+    second = gather_column(sender, [proj_ref, fc1_ref], [proj_slots, fc1_slots], own_sem.at[2], sizes, join_later)
     plane = gather_plane(sender, qkv_rows, qkv_full, keep_sem.at[0], sizes)
+    names[0]()
     first[0]()
-    second[0]()
+    names[1]()
+    fill_bias(small_all, rel_ref, mask_ref, bias_ref, spread_ref, heads_local)
     first[1]()
     plane[0]()
-    fill_bias(small_all, rel_ref, mask_ref, bias_ref, spread_ref, heads_local)
+    second[0]()
     for run in plane[1:]:
         run()
     second[1]()
@@ -546,6 +549,10 @@
 
 def hbm_spec():
     return pl.BlockSpec(memory_space=pl.ANY)
+
+
+def in_hbm(value):
+    return pltpu.with_memory_space_constraint(value, pltpu.HBM)
 
 
 def mesh_sizes():
@@ -575,12 +582,31 @@
         + [
             pltpu.VMEM((rows, wide), qkv.dtype),
             pltpu.VMEM((SLOT * gy_size * small.shape[0], SLOT), jnp.float32),
-            pltpu.SemaphoreType.DMA((count,)), pltpu.SemaphoreType.DMA((count,)), pltpu.SemaphoreType.DMA((2, 2)),
+            pltpu.SemaphoreType.DMA((count,)), pltpu.SemaphoreType.DMA((count,)), pltpu.SemaphoreType.DMA((3, 2)),
             pltpu.SemaphoreType.DMA((1,)),
         ],
         compiler_params=pltpu.CompilerParams(collective_id=0, has_side_effects=True, vmem_limit_bytes=14 << 20),
         name="gather_weights",
-    )(qkv, small, proj_t, fc1, jnp.asarray(rel.reshape(1, -1)), jnp.asarray(mask))
+    )(qkv, small, in_hbm(proj_t), in_hbm(fc1), in_hbm(jnp.asarray(rel.reshape(1, -1))), in_hbm(jnp.asarray(mask)))
+
+
+def table_gradient(d_bias_ref, rel_ref, spread_ref, table_ref):
+    groups = d_bias_ref.shape[0]
+    heads, depth = groups * PACK, table_ref.shape[1]
+    for h in range(heads):
+        low = h % PACK * SLOT
+        spread_ref[pl.ds(h, SLOT, stride=heads), :] = d_bias_ref[h // PACK, :, low : low + SLOT]
+    total = jnp.zeros((heads, depth), jnp.float32)
+    step = 8
+    for at in range(0, SLOT, step):
+        pairs = jnp.concatenate([spread_ref[j * heads : (j + 1) * heads, :] for j in range(at, at + step)], 1)
+        spots = lax.broadcasted_iota(jnp.int32, (depth, step * SLOT), 0)
+        onehot = (spots == rel_ref[:, at * SLOT : (at + step) * SLOT]).astype(jnp.bfloat16)
+        for _ in range(3):
+            high = pairs.astype(jnp.bfloat16)
+            total = total + matmul_nt(high, onehot)
+            pairs = pairs - high.astype(jnp.float32)
+    table_ref[...] = total
 
 
 def share_kernel(sizes, groups, whole_count, *refs):
@@ -594,11 +620,11 @@
         return out
 
     inputs, (small,) = take(arrays), take(1)
-    act, fc2_full, resid, shift = take(4)
-    outs, (small_out, output) = take(arrays), take(2)
+    act, fc2_full, resid, shift, d_bias, rel = take(6)
+    outs, (small_out, output, table_out) = take(arrays), take(3)
     planes = [take(gx_bits) for _ in range(whole_count)]
     totals, slots, columns = take(whole_count), take(arrays), take(arrays)
-    small_came, small_totals, small_column, send, recv = take(5)
+    small_came, small_totals, small_column, table_came, table_totals, table_column, table, spread_ref, send, recv = take(10)
     greet(*sizes)
     sender = Sender(send, recv)
     streams = []
@@ -611,6 +637,9 @@
             phases.append(both(last, after))
         streams.append(phases + column)
     streams.append(sum_small(sender, small, small_came, small_totals, small_column, small_out, sizes))
+    late = sum_small(sender, table, table_came, table_totals, table_column, table_out, sizes)
+    late[0] = both(lambda: table_gradient(d_bias, rel, spread_ref, table), late[0])
+    streams.append(late)
     width = output.shape[1]
     chunk = min(2 * 128, width)
     rest = list(range(0, width, chunk))
@@ -637,7 +666,7 @@
     return run
 
 
-def share_sums(fulls, rows_sums, groups, small, product):
+def share_sums(fulls, rows_sums, groups, small, product, d_bias):
     sizes = mesh_sizes()
     gx_size, gy_size = sizes
     gx_bits = bits_of(gx_size)
@@ -650,23 +679,30 @@
         wide = value.shape[1] // gy_size
         slots.append(pltpu.VMEM((gy_size, rows, wide), value.dtype))
         columns.append(pltpu.VMEM((gy_size - 1, rows, wide), value.dtype))
-    count = len(fulls) * (gx_size - 1) + len(arrays) * (gy_size - 1) + gx_bits + gy_size - 1
+    count = len(fulls) * (gx_size - 1) + len(arrays) * (gy_size - 1) + 2 * (gx_bits + gy_size - 1)
+    heads, depth = d_bias.shape[0] * PACK, -(-RELS // 128) * 128
+    _, rel, _ = static_tables(1)
     return pl.pallas_call(
         functools.partial(share_kernel, sizes, groups, len(fulls)),
-        in_specs=[vmem_spec()] * (len(arrays) + 5),
-        out_specs=[vmem_spec()] * (len(arrays) + 2),
+        in_specs=[vmem_spec()] * (len(arrays) + 7),
+        out_specs=[vmem_spec()] * (len(arrays) + 3),
         out_shape=[jax.ShapeDtypeStruct((rows, value.shape[1] // gy_size), jnp.float32) for value in arrays]
-        + [jax.ShapeDtypeStruct(small.shape, small.dtype), jax.ShapeDtypeStruct(product[2].shape, jnp.bfloat16)],
+        + [jax.ShapeDtypeStruct(small.shape, small.dtype), jax.ShapeDtypeStruct(product[2].shape, jnp.bfloat16), jax.ShapeDtypeStruct((heads, depth), jnp.float32)],
         scratch_shapes=planes + [pltpu.VMEM((rows, full.shape[1]), full.dtype) for full in fulls] + slots + columns + [
             pltpu.VMEM((gx_bits,) + small.shape, small.dtype),
             pltpu.VMEM((gx_bits,) + small.shape, small.dtype),
             pltpu.VMEM((gy_size,) + small.shape, small.dtype),
+            pltpu.VMEM((gx_bits, heads, depth), jnp.float32),
+            pltpu.VMEM((gx_bits, heads, depth), jnp.float32),
+            pltpu.VMEM((gy_size, heads, depth), jnp.float32),
+            pltpu.VMEM((heads, depth), jnp.float32),
+            pltpu.VMEM((SLOT * heads, SLOT), jnp.float32),
             pltpu.SemaphoreType.DMA((count,)),
             pltpu.SemaphoreType.DMA((count,)),
         ],
         compiler_params=pltpu.CompilerParams(collective_id=1, has_side_effects=True, vmem_limit_bytes=18 << 20),
         name="share_sums",
-    )(*arrays, small, *product)
+    )(*arrays, small, *product, d_bias, jnp.asarray(rel.reshape(1, -1)))
 
 
 def forward_stage(
@@ -692,15 +728,15 @@
         streams[0][0]()
         streams[1][0]()
 
-    @pl.when(image == jnp.minimum(1, last))
+    @pl.when(image == jnp.minimum(2, last))
     def _():
         streams[0][1]()
-
-    @pl.when(image == jnp.minimum(2, last))
+        column[1]()
+        streams[2][0]()
+
+    @pl.when(image == last)
     def _():
         streams[1][1]()
-        column[1]()
-        streams[2][0]()
 
     forward_kernel(
         qkv_ref, perm_ref, perm_t_ref, bias_ref, owner_ref, context_ref, windows_ref, probs_ref, ctx_ref
@@ -737,23 +773,19 @@
         for phases in streams:
             phases[0]()
 
-    @pl.when(image == jnp.minimum(1, last))
-    def _():
-        for phases in streams:
-            phases[1]()
+    def between(slot):
+        for when, n, place in ((1, 0, 1), (2, 1, 1), (5, 0, 2), (7, 1, 2)):
+            @pl.when(slot == jnp.minimum(when, 2 * last + when % 2))
+            def _(phases=streams[n], place=place):
+                phases[place]()
+
+    backward_kernel(
+        d_context_ref, windows_ref, probs_ref, perm_ref, perm_t_ref, owner_ref,
+        d_mixed_ref, d_bias_ref, d_qv_ref, d_ctx_ref, d_win_ref, between,
+    )
 
     @pl.when(image == last)
     def _():
-        streams[0][2]()
-
-    backward_kernel(
-        d_context_ref, windows_ref, probs_ref, perm_ref, perm_t_ref, owner_ref,
-        d_mixed_ref, d_bias_ref, d_qv_ref, d_ctx_ref, d_win_ref,
-    )
-
-    @pl.when(image == last)
-    def _():
-        streams[1][2]()
         for place in range(3, len(streams[0])):
             for phases in streams:
                 phases[place]()
@@ -836,7 +868,7 @@
     hidden_two = (pre_two.astype(jnp.bfloat16))
     pre_act = matmul(hidden_two, fc1_rows) + fc1_bias.astype(jnp.float32)
     act_full, slope = gelu_parts(pre_act)
-    act_low = act_full.astype(jnp.bfloat16)
+    act_low, slope = lax.optimization_barrier((act_full.astype(jnp.bfloat16), slope.astype(jnp.bfloat16)))
     live_rows = local_live(tok_local, live_images)
     grad_out = jnp.where(live_rows[:, None], cotangent, jnp.zeros_like(cotangent))
     grad_float = grad_out.astype(jnp.float32)
@@ -855,7 +887,7 @@
     d_resid_full = (d_resid_one.astype(jnp.bfloat16))
     d_proj_weight = matmul_tn(d_resid_full, context).astype(jnp.bfloat16)
     d_context = matmul(d_resid_full, proj_cols).astype(jnp.bfloat16)
-    d_mixed, d_qv_bias, d_table, sums = attend_backward(d_context, windows, probs, tables, (d_fc1_weight, d_fc2_weight))
+    d_mixed, d_qv_bias, d_bias, sums = attend_backward(d_context, windows, probs, tables, (d_fc1_weight, d_fc2_weight))
     d_qkv_weight = matmul_tn(hidden_one, d_mixed).astype(jnp.bfloat16)
     d_hidden_one = (matmul_nt(d_mixed, qkv_flat))
     d_ln1_gain = jnp.sum(d_hidden_one * normed_one, 0)
@@ -863,17 +895,17 @@
     d_input = (d_resid_one + norm_back(d_hidden_one, normed_one, scale_one, gain_one)).astype(
         jnp.bfloat16
     )
-    own = (d_ln1_gain, d_ln1_bias, d_proj_bias, d_ln2_gain, d_ln2_bias, d_fc2_bias, d_qv_bias, d_table, d_fc1_bias)
+    own = (d_ln1_gain, d_ln1_bias, d_proj_bias, d_ln2_gain, d_ln2_bias, d_fc2_bias, d_qv_bias, d_fc1_bias)
     product = (act_low, fc2_cols, resid_one, fc2_bias.astype(jnp.float32)[None])
-    d_qkv_weight, d_proj_weight, d_fc1_weight, d_fc2_weight, sums, output = share_sums(
-        (d_qkv_weight, d_proj_weight), sums, (3, 1, 1, 1), pack_rows(own), product
+    d_qkv_weight, d_proj_weight, d_fc1_weight, d_fc2_weight, sums, output, d_table = share_sums(
+        (d_qkv_weight, d_proj_weight), sums, (3, 1, 1, 1), pack_rows(own), product, d_bias
     )
     d_fc2_weight = d_fc2_weight.T
     d_proj_weight = d_proj_weight.T
     d_qkv_weight = d_qkv_weight.reshape(block_rows, 3, part)
     sums = unpack_rows(sums, [value.shape for value in own])
     norm_sums = sums[:6]
-    head_sums = (own_columns(sums[6], 1), own_columns(sums[7], 1), own_columns(sums[8], 0))
+    head_sums = (own_columns(sums[6], 1), own_columns(d_table, 0)[:, :RELS].T, own_columns(sums[7], 0))
     return (
         output,
         d_input,

time: 179 us -> 170 us (0.950)
  Pallas kernels: 117 us -> 110 us
  matrix products: 33.8 us -> 29.5 us
  local copies, waits for them, and re-layouts: 18.9 us -> 21.5 us
    unnamed x88 -> x128, local copies, waits for them, and re-layouts: 11.1 us -> 16.2 us
    reshape x4 -> x0, local copies, waits for them, and re-layouts: 4.98 us -> none  [the longest x3 4.89 us: attend_backward(): d_bias.reshape(groups, SLOT, PACK, SLOT).transpose(0, 2, 1, 3)]
    pallas_call x1, Pallas kernels: 30.3 us -> 25.9 us  [gather_weights(): pl.pallas_call(functools.partial(gather_kernel, sizes, heads_local), in_s...]
    pallas_call x1, Pallas kernels: 29.3 us -> 25.6 us  [attend_forward(): pl.pallas_call(functools.partial(forward_stage, sizes), grid=(count,), in...]
    dot_general x1 -> x0, matrix products: 2.35 us -> none  [attend_backward(): lax.dot_general(onehot.astype(jnp.float32), d_bias, (((1,), (1,)), ((), (...]
    dot_general x4, matrix products: 15.9 us -> 14 us  [matmul(): return jnp.dot(left, right, preferred_element_type=jnp.float32)]
where the time goes in v3:
time: 170 us
  Pallas kernels  110 us (65%)
  matrix products  29.5 us (17%)
  local copies, waits for them, and re-layouts  21.5 us (13%)
  other arithmetic  6.98 us (4%)
  between operations  2.13 us (1%)
    pallas_call x1, Pallas kernels, share_sums(): pl.pallas_call(functools.partial(share_kernel, sizes, groups, len(fulls))...  29.8 us
    pallas_call x1, Pallas kernels, attend_backward(): pl.pallas_call(functools.partial(backward_stage, sizes), grid=(count,), i...  28.2 us
    pallas_call x1, Pallas kernels, gather_weights(): pl.pallas_call(functools.partial(gather_kernel, sizes, heads_local), in_s...  25.9 us
    pallas_call x1, Pallas kernels, attend_forward(): pl.pallas_call(functools.partial(forward_stage, sizes), grid=(count,), in...  25.6 us
    unnamed x128, local copies, waits for them, and re-layouts  16.2 us
    dot_general x4, matrix products, matmul(): return jnp.dot(left, right, preferred_element_type=jnp.float32)  14 us
    dot_general x4, matrix products, matmul_tn(): lax.dot_general(left, right, (((0,), (0,)), ((), ())), preferred_element_...  8.84 us
    dot_general x3, matrix products, matmul_nt(): lax.dot_general(left, right, (((1,), (1,)), ((), ())), preferred_element_...  6.65 us

profile of v3, /device:TPU:0, one launch (start us, length us, event | category | flops | bytes accessed | tf_op | source)
XLA Modules:
  0.0 169.7 jit_solution(11087385755916238994)
XLA Ops:
  0.7 0.8 copy-done
  1.5 0.7 copy.54
  2.1 0.7 broadcast_in_dim.15
  2.8 0.7 fusion.28
  3.5 25.9 %gather_weights.1 = (bf16[512,1536]{1,0:T(8,128)(2,1)S(1)}, bf16[4,16,512]{2,1,0:T(8,128)(2,1)S(1)}, f32[4,2,64,512]{3,2,1,0:T(8,128)S(1)}, bf16[64,512]{1,0:T(8,128)(2,1)S(1)}, bf16[64,2048]{1,0:T(8,128)(2,1)S(1)}) custom-call(bf16[64,384]{1,0:T(8,128)(2,1)S(1)} %copy_bitcast_fusion.1.qkv_ref, bf16[16,512]{1,0:T(8,128)(2,1)S(1)} %pad.33.small_ref, ...), custom_call_target="tpu_custom_call" | custom-call | tf_op jit(solution)/shard_map/gather_weights/pallas_call | solution.py:571
  29.6 0.1 maximum_convert_fusion
  29.7 0.7 convert_element_type.109
  30.4 0.7 convert_element_type.108
  31.1 1.5 convert_reduce_fusion
  32.7 2.7 %add_convert_fusion.qkv_ref = bf16[784,1536]{1,0:T(8,128)(2,1)S(1)} fusion(bf16[512,1536]{1,0:T(8,128)(2,1)S(1)} %get-tuple-element.40, f32[1536]{0:T(1024)S(1)} %reshape.184, bf16[784,512]{1,0:T(8,128)(2,1)} %param.22, f32[512]{0:T(512)S(1)} %convert_element_type.109, f32[512]{0:T(512)S(1)} %convert_element_type.108, f32[784]{0:T(1024)S(1)} %get-tuple-element.121, ...), kind=kOutput, calls=%fused_computation.9 | convolution fusion | flops 1237942272 | bytes 4800640 | tf_op jit(solution)/shard_map/dot_general | solution.py:24
  35.5 0.8 copy-done.26
  36.3 25.6 %attend_forward.1 = (bf16[784,512]{1,0:T(8,128)(2,1)S(1)}, bf16[4,256,1536]{2,1,0:T(8,128)(2,1)}, f32[4,8,64,512]{3,2,1,0:T(8,128)}, bf16[512,512]{1,0:T(8,128)(...) custom-call(bf16[784,1536]{1,0:T(8,128)(2,1)S(1)} %add_convert_fusion.qkv_ref, ...), custom_call_target="tpu_custom_call" | custom-call | flops 6000000000 | bytes 24000000 | tf_op jit(solution)/shard_map/attend_forward/pallas_call | solution.py:188
  62.1 0.9 multiply_reduce_fusion.2
  62.9 0.4 copy-done.1
  63.3 0.2 copy-done.33
  63.5 0.7 copy-done.5
  64.3 6.1 %fusion.4 = (bf16[784,2048]{1,0:T(8,128)(2,1)}, bf16[784,2048]{1,0:T(8,128)(2,1)}) fusion(f32[2048]{0:T(1024)S(1)} %bitcast.86, bf16[512,2048]{1,0:T(8,128)(2,1)S(1)} %get-tuple-element.48, f32[784,512]{1,0:T(8,128)S(1)} %get-tuple-element.124.refs_7_, f32[512]{0:T(512)S(1)} %convert_element_type.120, f32[512]{0:T(512)S(1)} %convert_element_type.119, ...), kind=kOutput, calls=%fused_computation.5 | convolution fusion | flops 1665441792 | bytes 10143872 | tf_op jit(solution)/shard_map/dot_general | solution.py:24
  71.0 4.6 %fusion.5 = (f32[2048]{0:T(1024)S(1)}, f32[784,2048]{1,0:T(8,128)S(1)}) fusion(bf16[784,2048]{1,0:T(8,128)(2,1)} %get-tuple-element.49, bf16[512,2048]{1,0:T(8,128)(2,1)} %copy-done.1, bf16[784,512]{1,0:T(8,128)(2,1)S(1)} %copy-done.40, pred[784]{0:T(1024)(128)(4,1)S(1)} %fusion.30), kind=kOutput, calls=%fused_computation.10 | convolution fusion | flops 1649383424 | bytes 12542736 | tf_op jit(solution)/shard_map/dot_general | solution.py:24
  75.7 2.4 %multiply_reduce_fusion = (f32[512]{0:T(512)S(1)}, f32[784]{0:T(1024)S(1)}, f32[784]{0:T(1024)S(1)}, f32[512]{0:T(512)S(1)}, f32[784,512]{1,0:T(8,128)S(1)}) fusion(f32[784,512]{1,0:T(8,128)S(1)} %get-tuple-element.124.refs_7_, f32[784]{0:T(1024)S(1)} %get-tuple-element.119, f32[784]{0:T(1024)S(1)} %get-tuple-element.118, ...), kind=kOutput, calls=%fused_computation.36 | convolution fusion | flops 1652594176 | bytes 14960896 | tf_op jit(solution)/shard_map/dot_general | solution.py:34
  78.1 1.1 fusion.41
  79.2 0.6 convolution_convert_fusion.3.d_context_ref
  79.8 2.8 %convolution_convert_fusion.1.d_fc1_ref = bf16[512,2048]{1,0:T(8,128)(2,1)S(1)} fusion(f32[784,2048]{1,0:T(8,128)S(1)} %get-tuple-element.128, bf16[784,2048]{1,0:T(8,128)(2,1)S(1)} %copy-done.37, f32[784,512]{1,0:T(8,128)S(1)} %get-tuple-element.124.refs_7_, f32[512]{0:T(512)S(1)} %convert_element_type.120, f32[512]{0:T(512)S(1)} %convert_element_type.119, ...), kind=kOutput, calls=%fused_computation.13 | convolution fusion | flops 1652039680 | bytes 13346944 | tf_op jit(solution)/shard_map/dot_general | solution.py:28
  82.7 2.5 %convolution_convert_fusion.d_fc2_ref = bf16[512,2048]{1,0:T(8,128)(2,1)S(1)} fusion(bf16[784,2048]{1,0:T(8,128)(2,1)S(1)} %copy-done.3, bf16[784,512]{1,0:T(8,128)(2,1)S(1)} %copy-done.41, pred[784]{0:T(1024)(128)(4,1)S(1)} %fusion.30), kind=kOutput, calls=%fused_computation.12 | convolution fusion | flops 1645617152 | bytes 6112016 | tf_op jit(solution)/shard_map/dot_general | solution.py:28
  85.3 28.2 %attend_backward.1 = (bf16[784,1536]{1,0:T(8,128)(2,1)S(1)}, f32[2,64,512]{2,1,0:T(8,128)S(1)}, f32[2,512]{1,0:T(2,128)S(1)}, bf16[64,2048]{1,0:T(8,128)(2,1)S(1)}, bf16[64,2048]{1,0:T(8,128)(2,1)S(1)}) custom-call(bf16[784,512]{1,0:T(8,128)(2,1)S(1)} %convolution_convert_fusion.3.d_context_ref, bf16[4,256,1536]{2,1,0:T(8,128)(2,1)S(1)} %copy-done.36, ...), custom_call_target="tpu_custom_call" | custom-call | flops 8999999488 | bytes 32000000 | tf_op jit(solution)/shard_map/attend_backward/pallas_call | solution.py:227
  113.6 2.0 %convolution_convert_fusion.2.refs_0_ = bf16[512,1536]{1,0:T(8,128)(2,1)S(1)} fusion(bf16[784,1536]{1,0:T(8,128)(2,1)S(1)} %get-tuple-element.53, bf16[784,512]{1,0:T(8,128)(2,1)S(1)} %copy-done.43, f32[512]{0:T(512)S(1)} %convert_element_type.109, f32[512]{0:T(512)S(1)} %convert_element_type.108, f32[784]{0:T(1024)S(1)} %get-tuple-element.121, ...), kind=kOutput, calls=%fused_computation.14 | convolution fusion | flops 1236320256 | bytes 4794496 | tf_op jit(solution)/shard_map/dot_general | solution.py:28
  115.6 1.5 convolution_convert_fusion.4.refs_1_
  117.2 3.4 %fusion.15 = (f32[784]{0:T(1024)}, f32[512]{0:T(512)S(1)}, f32[784]{0:T(1024)}, f32[512]{0:T(512)S(1)}, f32[784,512]{1,0:T(8,128)}) fusion(bf16[784,512]{1,0:T(8,128)(2,1)S(1)} %copy-done.43, f32[512]{0:T(512)S(1)} %convert_element_type.108, f32[784]{0:T(1024)S(1)} %get-tuple-element.121, f32[784]{0:T(1024)S(1)} %get-tuple-element.120, ...), kind=kOutput, calls=%fused_computation.29 | convolution fusion | flops 1237136896 | bytes 6408448 | tf_op jit(solution)/shard_map/dot_general | solution.py:34
  120.6 0.6 reshape.180
  121.2 0.7 constant_dynamic-update-slice_fusion.1
  121.9 0.7 broadcast_in_dim.21
  122.6 1.6 copy-done.2
  124.2 1.9 %copy-done.4 = bf16[784,2048]{1,0:T(8,128)(2,1)S(1)} copy-done((bf16[784,2048]{1,0:T(8,128)(2,1)S(1)}, bf16[784,2048]{1,0:T(8,128)(2,1)}, u32[]{:S(2)}) %copy-start.4) | copy-done | bytes 3211288
  126.1 1.0 copy-done.8
  127.2 0.9 copy-done.10
  128.1 0.9 copy-done.12
  129.1 29.8 %share_sums.1 = (f32[64,384]{1,0:T(8,128)S(1)}, f32[64,128]{1,0:T(8,128)S(1)}, f32[64,512]{1,0:T(8,128)S(1)}, f32[64,512]{1,0:T(8,128)S(1)}, f32[72,128]{1,0:T(8...) custom-call(bf16[512,1536]{1,0:T(8,128)(2,1)S(1)} %convolution_convert_fusion.2.refs_0_, ...), custom_call_target="tpu_custom_call" | custom-call | tf_op jit(solution)/shard_map/share_sums/pallas_call | solution.py:685
  158.9 0.6 copy-done.21
  159.7 1.5 fusion.19
  161.2 0.6 slice_bitcast_fusion.1
  161.8 0.6 copy_bitcast_fusion
  162.4 0.6 constant_dynamic-slice_fusion
  163.0 1.3 dynamic-slice_bitcast_fusion
  164.3 0.7 slice_bitcast_fusion
  165.0 0.7 dynamic_slice.11
  165.7 2.1 %copy.67 = bf16[784,512]{1,0:T(8,128)(2,1)} copy(bf16[784,512]{1,0:T(8,128)(2,1)} %copy-done.7) | data formatting | bytes 1605632
  167.7 0.6 copy.68
  168.3 0.7 copy.69
  169.0 0.7 copy.70
  (131 shorter events, 0.5 us)
Async XLA Ops:
  29.5 6.0 %copy-start.22 = (bf16[512,1536]{1,0:T(8,128)(2,1)}, bf16[512,1536]{1,0:T(8,128)(2,1)S(1)}, u32[]{:S(2)}) copy-start(bf16[512,1536]{1,0:T(8,128)(2,1)S(1)} %get-tuple-element.40) | copy-start | bytes 4718596
  29.5 6.0 %copy-start.25 = (bf16[64,512]{1,0:T(8,128)(2,1)}, bf16[64,512]{1,0:T(8,128)(2,1)S(1)}, u32[]{:S(2)}) copy-start(bf16[64,512]{1,0:T(8,128)(2,1)S(1)} %get-tuple-element.43.proj_rows) | copy-start | bytes 196612
  31.1 86.0 %copy-start.50 = (f32[512]{0:T(512)}, f32[512]{0:T(512)S(1)}, u32[]{:S(2)}) copy-start(f32[512]{0:T(512)S(1)} %convert_element_type.108) | copy-start | bytes 6148
  32.6 84.6 %copy-start.46 = (f32[784]{0:T(1024)}, f32[784]{0:T(1024)S(1)}, u32[]{:S(2)}) copy-start(f32[784]{0:T(1024)S(1)} %get-tuple-element.120) | copy-start | bytes 9412
  32.6 84.5 %copy-start.48 = (f32[784]{0:T(1024)}, f32[784]{0:T(1024)S(1)}, u32[]{:S(2)}) copy-start(f32[784]{0:T(1024)S(1)} %get-tuple-element.121) | copy-start | bytes 9412
  32.6 2.8 %copy-start.24 = (bf16[512,64]{0,1:T(8,128)(2,1)S(1)}, bf16[512,64]{0,1:T(8,128)(2,1)}, u32[]{:S(2)}) copy-start(bf16[512,64]{0,1:T(8,128)(2,1)} %param.36) | copy-start | bytes 196612
  32.6 2.8 %copy-start.27 = (bf16[4,256,208]{2,1,0:T(8,128)(2,1)S(1)}, bf16[4,256,208]{2,1,0:T(8,128)(2,1)}, u32[]{:S(2)}) copy-start(bf16[4,256,208]{2,1,0:T(8,128)(2,1)} %constant.91.perm_ref) | copy-start | bytes 1277956
  32.6 2.8 %copy-start.29 = (bf16[4,208,256]{2,1,0:T(8,128)(2,1)S(1)}, bf16[4,208,256]{2,1,0:T(8,128)(2,1)}, u32[]{:S(2)}) copy-start(bf16[4,208,256]{2,1,0:T(8,128)(2,1)} %constant.92.perm_t_ref) | copy-start | bytes 1277956
  32.7 2.8 %copy-start.31 = (bf16[512,256]{1,0:T(8,128)(2,1)S(1)}, bf16[512,256]{1,0:T(8,128)(2,1)}, u32[]{:S(2)}) copy-start(bf16[512,256]{1,0:T(8,128)(2,1)} %constant.93.owner_ref) | copy-start | bytes 786436
  36.3 25.7 %copy-start.54 = (bf16[512]{0:T(512)(128)(2,1)S(1)}, bf16[512]{0:T(512)(128)(2,1)}, u32[]{:S(2)}) copy-start(bf16[512]{0:T(512)(128)(2,1)} %param.31) | copy-start | bytes 3076
  36.3 25.7 %copy-start.42 = (bf16[784,512]{1,0:T(8,128)(2,1)S(1)}, bf16[784,512]{1,0:T(8,128)(2,1)}, u32[]{:S(2)}) copy-start(bf16[784,512]{1,0:T(8,128)(2,1)} %param.22) | copy-start | bytes 2408452
  62.0 1.6 copy-start.33
  62.0 2.3 %copy-start.5 = (bf16[512,2048]{1,0:T(8,128)(2,1)}, bf16[512,2048]{1,0:T(8,128)(2,1)S(1)}, u32[]{:S(2)}) copy-start(bf16[512,2048]{1,0:T(8,128)(2,1)S(1)} %get-tuple-element.48) | copy-start | bytes 6291460
  64.3 6.8 %copy-start.40 = (bf16[784,512]{1,0:T(8,128)(2,1)S(1)}, bf16[784,512]{1,0:T(8,128)(2,1)}, u32[]{:S(2)}) copy-start(bf16[784,512]{1,0:T(8,128)(2,1)} %param.23) | copy-start | bytes 2408452
  71.0 4.6 %copy-start.6 = (bf16[512,2048]{1,0:T(8,128)(2,1)S(1)}, bf16[512,2048]{1,0:T(8,128)(2,1)}, u32[]{:S(2)}) copy-start(bf16[512,2048]{1,0:T(8,128)(2,1)} %copy-done.5) | copy-start | bytes 6291460
  71.0 4.6 %copy-start.37 = (bf16[784,2048]{1,0:T(8,128)(2,1)S(1)}, bf16[784,2048]{1,0:T(8,128)(2,1)}, u32[]{:S(2)}) copy-start(bf16[784,2048]{1,0:T(8,128)(2,1)} %get-tuple-element.49) | copy-start | bytes 9633796
  79.2 36.4 %copy-start.38 = (f32[784,512]{1,0:T(8,128)}, f32[784,512]{1,0:T(8,128)S(1)}, u32[]{:S(2)}) copy-start(f32[784,512]{1,0:T(8,128)S(1)} %get-tuple-element.108) | copy-start | bytes 4816900
  79.8 2.8 %copy-start.3 = (bf16[784,2048]{1,0:T(8,128)(2,1)S(1)}, bf16[784,2048]{1,0:T(8,128)(2,1)}, u32[]{:S(2)}) copy-start(bf16[784,2048]{1,0:T(8,128)(2,1)} %get-tuple-element.52.refs_5_) | copy-start | bytes 9633796
  79.8 2.8 %copy-start.41 = (bf16[784,512]{1,0:T(8,128)(2,1)S(1)}, bf16[784,512]{1,0:T(8,128)(2,1)}, u32[]{:S(2)}) copy-start(bf16[784,512]{1,0:T(8,128)(2,1)} %param.23) | copy-start | bytes 2408452
  79.8 5.4 %copy-start.36 = (bf16[4,256,1536]{2,1,0:T(8,128)(2,1)S(1)}, bf16[4,256,1536]{2,1,0:T(8,128)(2,1)}, u32[]{:S(2)}) copy-start(bf16[4,256,1536]{2,1,0:T(8,128)(2,1)} %get-tuple-element.50.windows_ref) | copy-start | bytes 9437188
  82.7 2.6 %copy-start.28 = (bf16[4,256,208]{2,1,0:T(8,128)(2,1)S(1)}, bf16[4,256,208]{2,1,0:T(8,128)(2,1)}, u32[]{:S(2)}) copy-start(bf16[4,256,208]{2,1,0:T(8,128)(2,1)} %constant.91.perm_ref) | copy-start | bytes 1277956
  82.7 2.6 %copy-start.30 = (bf16[4,208,256]{2,1,0:T(8,128)(2,1)S(1)}, bf16[4,208,256]{2,1,0:T(8,128)(2,1)}, u32[]{:S(2)}) copy-start(bf16[4,208,256]{2,1,0:T(8,128)(2,1)} %constant.92.perm_t_ref) | copy-start | bytes 1277956
  82.7 2.6 %copy-start.32 = (bf16[512,256]{1,0:T(8,128)(2,1)S(1)}, bf16[512,256]{1,0:T(8,128)(2,1)}, u32[]{:S(2)}) copy-start(bf16[512,256]{1,0:T(8,128)(2,1)} %constant.93.owner_ref) | copy-start | bytes 786436
  82.7 2.6 %copy-start.35 = (f32[4,8,64,512]{3,2,1,0:T(8,128)S(1)}, f32[4,8,64,512]{3,2,1,0:T(8,128)}, u32[]{:S(2)}) copy-start(f32[4,8,64,512]{3,2,1,0:T(8,128)} %get-tuple-element.51.probs_ref) | copy-start | bytes 12582916
  85.3 28.3 %copy-start.43 = (bf16[784,512]{1,0:T(8,128)(2,1)S(1)}, bf16[784,512]{1,0:T(8,128)(2,1)}, u32[]{:S(2)}) copy-start(bf16[784,512]{1,0:T(8,128)(2,1)} %param.22) | copy-start | bytes 2408452
  113.6 2.0 %copy-start.9 = (bf16[64,2048]{1,0:T(8,128)(2,1)}, bf16[64,2048]{1,0:T(8,128)(2,1)S(1)}, u32[]{:S(2)}) copy-start(bf16[64,2048]{1,0:T(8,128)(2,1)S(1)} %get-tuple-element.54.refs_2_) | copy-start | bytes 786436
  113.6 2.0 %copy-start.11 = (bf16[64,2048]{1,0:T(8,128)(2,1)}, bf16[64,2048]{1,0:T(8,128)(2,1)S(1)}, u32[]{:S(2)}) copy-start(bf16[64,2048]{1,0:T(8,128)(2,1)S(1)} %get-tuple-element.55.refs_3_) | copy-start | bytes 786436
  113.6 2.0 %copy-start.34 = (bf16[784,512]{1,0:T(8,128)(2,1)S(1)}, bf16[784,512]{1,0:T(8,128)(2,1)}, u32[]{:S(2)}) copy-start(bf16[784,512]{1,0:T(8,128)(2,1)} %copy-done.33) | copy-start | bytes 2408452
  115.6 1.6 copy-start.23
  117.2 5.5 %copy-start.17 = (s32[1,4096]{1,0:T(1,128)S(1)}, s32[1,4096]{1,0:T(1,128)}, u32[]{:S(2)}) copy-start(s32[1,4096]{1,0:T(1,128)} %constant.65.clone.rel_ref.refs_10_) | copy-start | bytes 49156
  122.6 1.6 copy-start.2
  124.2 1.9 %copy-start.4 = (bf16[784,2048]{1,0:T(8,128)(2,1)S(1)}, bf16[784,2048]{1,0:T(8,128)(2,1)}, u32[]{:S(2)}) copy-start(bf16[784,2048]{1,0:T(8,128)(2,1)} %get-tuple-element.52.refs_5_) | copy-start | bytes 9633796
  129.1 30.5 %copy-start.53 = (f32[784]{0:T(1024)S(1)}, f32[784]{0:T(1024)}, u32[]{:S(2)}) copy-start(f32[784]{0:T(1024)} %get-tuple-element.97) | copy-start | bytes 9412
  129.1 30.5 %copy-start.52 = (f32[784]{0:T(1024)S(1)}, f32[784]{0:T(1024)}, u32[]{:S(2)}) copy-start(f32[784]{0:T(1024)} %get-tuple-element.100) | copy-start | bytes 9412
  129.1 30.5 %copy-start.39 = (f32[784,512]{1,0:T(8,128)S(1)}, f32[784,512]{1,0:T(8,128)}, u32[]{:S(2)}) copy-start(f32[784,512]{1,0:T(8,128)} %copy-done.38) | copy-start | bytes 4816900
  129.1 30.5 %copy-start.44 = (bf16[784,512]{1,0:T(8,128)(2,1)S(1)}, bf16[784,512]{1,0:T(8,128)(2,1)}, u32[]{:S(2)}) copy-start(bf16[784,512]{1,0:T(8,128)(2,1)} %param.22) | copy-start | bytes 2408452
  129.1 30.5 %copy-start.45 = (f32[784,512]{1,0:T(8,128)S(1)}, f32[784,512]{1,0:T(8,128)}, u32[]{:S(2)}) copy-start(f32[784,512]{1,0:T(8,128)} %get-tuple-element.126) | copy-start | bytes 4816900
  129.1 30.5 %copy-start.47 = (f32[784]{0:T(1024)S(1)}, f32[784]{0:T(1024)}, u32[]{:S(2)}) copy-start(f32[784]{0:T(1024)} %copy-done.46) | copy-start | bytes 9412
  129.1 30.5 %copy-start.49 = (f32[784]{0:T(1024)S(1)}, f32[784]{0:T(1024)}, u32[]{:S(2)}) copy-start(f32[784]{0:T(1024)} %copy-done.48) | copy-start | bytes 9412
  129.1 30.5 %copy-start.51 = (f32[512]{0:T(512)S(1)}, f32[512]{0:T(512)}, u32[]{:S(2)}) copy-start(f32[512]{0:T(512)} %copy-done.50) | copy-start | bytes 6148
  159.5 1.6 copy-start.7
  159.5 1.6 copy-start.13
  159.5 1.6 copy-start.15
  159.5 1.6 copy-start.18
  159.5 2.9 %copy-start.20 = (f32[72,128]{1,0:T(8,128)}, f32[72,128]{1,0:T(8,128)S(1)}, u32[]{:S(2)}) copy-start(f32[72,128]{1,0:T(8,128)S(1)} %get-tuple-element.59) | copy-start | bytes 110596
  161.1 6.6 %copy-start.19 = (f32[64,128]{1,0:T(8,128)S(1)}, f32[64,128]{1,0:T(8,128)}, u32[]{:S(2)}) copy-start(f32[64,128]{1,0:T(8,128)} %copy-done.18) | copy-start | bytes 98308
  161.1 7.2 %copy-start.16 = (f32[64,512]{1,0:T(8,128)S(1)}, f32[64,512]{1,0:T(8,128)}, u32[]{:S(2)}) copy-start(f32[64,512]{1,0:T(8,128)} %copy-done.15) | copy-start | bytes 393220
  161.2 7.8 %copy-start.14 = (f32[64,512]{1,0:T(8,128)S(1)}, f32[64,512]{1,0:T(8,128)}, u32[]{:S(2)}) copy-start(f32[64,512]{1,0:T(8,128)} %copy-done.13) | copy-start | bytes 393220
  (9 other events, 9.3 us)
